TPU v7x, 128 devices: a whole 4x4x4 slice. The times are simulated.
128 devices in a mesh: tm: 32 (over z, y, core), ep: 4 (over x).
Axes of the slice: x: 4, y: 4, z: 4, core: 2. Of those that a mesh axis runs over, the one named last changes fastest.
Arguments:
- queries: bfloat16 [16384, 1024], P(('tm', 'ep')), may hold values from -256 to 256
- keys: bfloat16 [16384, 1024], P(('tm', 'ep')), may hold values from -6 to 6
- values: bfloat16 [16384, 1024], P(('tm', 'ep')), may hold values from -6 to 6
- stream: bfloat16 [16384, 1024], P(('tm', 'ep')), may hold values from -16 to 16
- grad_out: bfloat16 [16384, 1024], P(('tm', 'ep')), may hold values from -6 to 6
- norm_gain: float32 [1024], replicated, may hold values from 0.1 to 1.9
- gate_probs: float32 [16384, 2], P(('tm', 'ep')), may hold values from 0.1 to 0.9
- routes: int32 [16384, 2], P(('tm', 'ep')), may hold values from 0 to 31, all different within a row; in each aligned block of 128 rows (0 to 127, 128 to 255, ...) at most 12 rows name the same one
- w_gate: bfloat16 [32, 1024, 4096], P('tm', None, 'ep'), may hold values from -0.1875 to 0.1875
- w_up: bfloat16 [32, 1024, 4096], P('tm', None, 'ep'), may hold values from -0.1875 to 0.1875
- w_down: bfloat16 [32, 4096, 1024], P('tm', 'ep'), may hold values from -0.09375 to 0.09375
Outputs:
- queries_grad: bfloat16 [16384, 1024], P(('tm', 'ep'))
- keys_grad: bfloat16 [16384, 1024], P(('tm', 'ep'))
- values_grad: bfloat16 [16384, 1024], P(('tm', 'ep'))
- stream_grad: bfloat16 [16384, 1024], P(('tm', 'ep'))
- gate_weight_grad: float32 [32, 1024, 4096], P('tm', None, 'ep')
- up_weight_grad: float32 [32, 1024, 4096], P('tm', None, 'ep')
- down_weight_grad: float32 [32, 4096, 1024], P('tm', 'ep')
Inputs may be any that keep to these rules, and one draw needn't show every extreme that they name: `routes`: in the frames of one device no expert is named by more than 12 frames, a bound that some block reaches.
All inputs are finite; a program needn't handle non-finite values.
Results may differ from a plain program's by a relative error of at most 0.015.
Values may be sent and summed in bfloat16 or wider, within the bound.
No kernel may reach another device: no remote copies, remote signals or barrier semaphores. Data moves between devices by JAX's collectives and lax.ppermute only.
A program may use at most 128 MiB of HBM per device.

v0:
```python
import math

import jax
import jax.numpy as jnp
from jax import lax
from jax.experimental import pallas as pl
from jax.experimental.pallas import tpu as pltpu
from jax.sharding import PartitionSpec as P

D = 1024
HEADS = 16
HEAD = 64
SPAN = 64
LEFT = 256
FRAMES = 128
EXPERTS = 32
CAP = 12
EP = 4
ROWS = EXPERTS * EP * CAP
EPSILON = 1e-06
BF16 = jnp.bfloat16
F32 = jnp.float32
NT = (((1,), (1,)), ((), ()))
TN = (((0,), (0,)), ((), ()))


def iota(shape, dim):
    return lax.broadcasted_iota(jnp.int32, shape, dim)


def ones_where(mask):
    return jnp.where(mask, 1.0, 0.0).astype(BF16)


def matmul(a, b, dims=(((1,), (0,)), ((), ()))):
    return lax.dot_general(a, b, dims, preferred_element_type=F32)


def dispatch_x_kernel(stream_ref, gain_ref, routes_ref, gates_ref, packed_ref, meta_ref):
    s = stream_ref[...].astype(F32)
    inverse_rms = lax.rsqrt(jnp.mean(s * s, -1, keepdims=True) + EPSILON)
    normed = ((s * inverse_rms) * gain_ref[...]).astype(BF16)
    routes = routes_ref[...]
    expert = iota((EXPERTS, FRAMES), 0)
    named = [expert == routes[k : k + 1, :] for k in range(2)]
    count = ones_where(jnp.logical_or(named[0], named[1]))
    earlier = ones_where(iota((FRAMES, FRAMES), 0) < iota((FRAMES, FRAMES), 1))
    before = matmul(count, earlier)
    places = []
    for k in range(2):
        slot = jnp.sum(jnp.where(named[k], before, 0.0), 0, keepdims=True)
        places.append(routes[k : k + 1, :].astype(F32) * CAP + slot)
        meta_ref[k : k + 1, :] = places[k]
        meta_ref[2 + k : 3 + k, :] = gates_ref[k : k + 1, :]
    meta_ref[4:8, :] = jnp.zeros((4, FRAMES), F32)
    row = iota((EXPERTS * 16, FRAMES), 0)
    lane = row & 15
    base = (row >> 4) * CAP

    def pick(ids, valid):
        ids = jnp.where(valid, ids, -1).astype(F32)
        return ones_where(jnp.logical_or(ids == places[0], ids == places[1]))

    main = pick(base + lane, lane < CAP)
    for j in range(3):
        last = pick(base + (lane - CAP) + 4 * j, lane >= CAP)
        cols = slice(256 * j, 256 * (j + 1))
        packed_ref[:, cols] = (matmul(main, normed[:, cols]) + matmul(last, normed[:, 768:])).astype(BF16)


def dispatch_x(stream, gain, routes, gates):
    return pl.pallas_call(
        dispatch_x_kernel,
        out_shape=(
            jax.ShapeDtypeStruct((EXPERTS * 16, 768), BF16),
            jax.ShapeDtypeStruct((8, FRAMES), F32),
        ),
        name="dispatch_x",
    )(stream, gain, routes, gates)


def row_keys(start, count, width):
    r = iota((count, width), 0) + start
    group = (r * 1366) >> 16
    rest = r - group * 48
    source = (rest * 43) >> 9
    return (group * CAP + (rest - source * CAP) + source * 512).astype(F32)


G_BLOCK = 384


def dispatch_g_kernel(*refs):
    grads, metas, out_ref, pairs, keys = refs[:4], refs[4:8], refs[8], refs[9], refs[10]

    @pl.when(pl.program_id(0) == 0)
    def _():
        for q in range(EP):
            meta = metas[q][...]
            turned = meta.T
            g = grads[q][...].astype(F32)
            for k in range(2):
                part = slice((2 * q + k) * FRAMES, (2 * q + k + 1) * FRAMES)
                pairs[part, :] = (turned[:, 2 + k : 3 + k] * g).astype(BF16)
                keys[0:1, part] = meta[k : k + 1, :] + 512.0 * q

    key = row_keys(pl.program_id(0) * G_BLOCK, G_BLOCK, FRAMES)
    chosen = jnp.concatenate(
        [ones_where(key == keys[0:1, b * FRAMES : (b + 1) * FRAMES]) for b in range(8)], 1
    )
    out_ref[...] = matmul(chosen, pairs[...]).astype(BF16)


def dispatch_g(grads, metas):
    whole = lambda shape: pl.BlockSpec(shape, lambda i: (0, 0))
    return pl.pallas_call(
        dispatch_g_kernel,
        grid=(ROWS // G_BLOCK,),
        in_specs=[whole((FRAMES, D))] * 4 + [whole((8, FRAMES))] * 4,
        out_specs=pl.BlockSpec((G_BLOCK, D), lambda i: (i, 0)),
        out_shape=jax.ShapeDtypeStruct((ROWS, D), BF16),
        scratch_shapes=[pltpu.VMEM((8 * FRAMES, D), BF16), pltpu.VMEM((8, 8 * FRAMES), F32)],
        name="dispatch_g",
    )(*grads, *metas)


M_BLOCK = 384
STEPS = ROWS // M_BLOCK
PACKED = 16 * M_BLOCK // 48


def expert_forward_kernel(
    own_ref, left_ref, right_ref, top_ref, bottom_ref, gate_ref, up_ref, x_ref, a_ref, s_ref, acted_ref, moves
):
    step = pl.program_id(0)

    @pl.when(step == 0)
    def _():
        r = iota((192, 256), 0)
        c = iota((192, 256), 1)
        group = (r * 1366) >> 16
        rest = r - group * 48
        source = (rest * 43) >> 9
        slot = rest - source * CAP
        same = jnp.logical_and((c >> 6) == source, ((c & 63) >> 4) == group)
        lane = c & 15
        moves[0] = ones_where(jnp.logical_and(same, lane == slot))
        for j in range(3):
            hit = jnp.logical_and(same, lane == CAP + slot - 4 * j)
            hit = jnp.logical_and(hit, (slot >> 2) == j)
            moves[1 + j] = ones_where(hit)

    upper = step < STEPS // 2
    far = jnp.where(upper, top_ref[...].astype(F32), bottom_ref[...].astype(F32)).astype(BF16)
    chunks = (own_ref[...], left_ref[...], right_ref[...], far)
    for half in range(M_BLOCK // 192):
        rows = slice(192 * half, 192 * (half + 1))
        packed = jnp.concatenate([c[64 * half : 64 * (half + 1), :] for c in chunks], 0)
        x_ref[rows, 0:768] = matmul(moves[0], packed).astype(BF16)
        last = matmul(moves[1], packed[:, 0:256])
        last += matmul(moves[2], packed[:, 256:512])
        last += matmul(moves[3], packed[:, 512:768])
        x_ref[rows, 768:1024] = last.astype(BF16)
    x = x_ref[...]
    gate = matmul(x, gate_ref[...])
    up = matmul(x, up_ref[...])
    sig = jax.nn.sigmoid(gate)
    silu = gate * sig
    acted_ref[...] = (silu * up).astype(BF16)
    s_ref[...] = silu
    a_ref[...] = up * sig * (1.0 + gate * (1.0 - sig))


def expert_forward(own, left, right, top, bottom, w_gate, w_up):
    half = STEPS // 2
    rows = lambda f: pl.BlockSpec((PACKED, 768), f)
    weight = pl.BlockSpec((D, D), lambda i: (0, 0), pipeline_mode=pl.Buffered(1))
    out = pl.BlockSpec((M_BLOCK, D), lambda i: (i, 0))
    shape = lambda t: jax.ShapeDtypeStruct((ROWS, D), t)
    return pl.pallas_call(
        expert_forward_kernel,
        grid=(STEPS,),
        in_specs=[
            rows(lambda i: (i, 0)),
            rows(lambda i: (i, 0)),
            rows(lambda i: (i, 0)),
            rows(lambda i: (jnp.minimum(i, half - 1), 0)),
            rows(lambda i: (jnp.maximum(i - half, 0), 0)),
            weight,
            weight,
        ],
        out_specs=[out] * 4,
        out_shape=(shape(BF16), shape(F32), shape(F32), shape(BF16)),
        scratch_shapes=[pltpu.VMEM((4, 192, 256), BF16)],
        name="expert_forward",
    )(own, left, right, top, bottom, w_gate, w_up)


def expert_backward_kernel(g_ref, a_ref, s_ref, gate_ref, up_ref, down_ref, dgate_ref, dup_ref, dx_ref):
    dact = matmul(g_ref[...], down_ref[...], NT)
    dgate = (dact * a_ref[...]).astype(BF16)
    dup = (dact * s_ref[...]).astype(BF16)
    dgate_ref[...] = dgate
    dup_ref[...] = dup
    dx_ref[...] = (matmul(dgate, gate_ref[...], NT) + matmul(dup, up_ref[...], NT)).astype(BF16)


def expert_backward(g, a, s, w_gate, w_up, w_down):
    weight = pl.BlockSpec((D, D), lambda i: (0, 0), pipeline_mode=pl.Buffered(1))
    rows = pl.BlockSpec((M_BLOCK, D), lambda i: (i, 0))
    return pl.pallas_call(
        expert_backward_kernel,
        grid=(STEPS,),
        in_specs=[rows, rows, rows, weight, weight, weight],
        out_specs=[rows] * 3,
        out_shape=(jax.ShapeDtypeStruct((ROWS, D), BF16),) * 3,
        name="expert_backward",
    )(g, a, s, w_gate, w_up, w_down)


def combine_kernel(dx_ref, m0, m1, m2, m3, own_ref, p1_ref, p2_ref, p3_ref):
    r = iota((8, ROWS), 1)
    group = (r * 1366) >> 16
    rest = r - group * 48
    source = (rest * 43) >> 9
    key = (group * CAP + (rest - source * CAP) + source * 512).astype(F32)[0:1, :]
    dx = dx_ref[...]
    for q, (meta, out) in enumerate(zip((m0, m1, m2, m3), (own_ref, p1_ref, p2_ref, p3_ref))):
        turned = meta[...].T + 512.0 * q
        chosen = ones_where(jnp.logical_or(turned[:, 0:1] == key, turned[:, 1:2] == key))
        out[...] = matmul(chosen, dx).astype(out.dtype)


def combine(dx, metas):
    part = lambda t: jax.ShapeDtypeStruct((FRAMES, D), t)
    return pl.pallas_call(
        combine_kernel,
        out_shape=(part(F32), part(BF16), part(BF16), part(BF16)),
        name="combine",
    )(dx, *metas)


WINDOW = LEFT + FRAMES


def one_head(pair, h):
    lane = iota(pair.shape, 1)
    mask = lane >= HEAD if h else lane < HEAD
    return jnp.where(mask, pair.astype(F32), 0.0).astype(BF16)


def attention_probs_kernel(first_ref, q_ref, k2_ref, k1_ref, k0_ref, p_ref):
    keys = jnp.concatenate([k2_ref[...], k1_ref[...], k0_ref[...]], 0)
    q = q_ref[...]
    s = iota((WINDOW, FRAMES), 0)
    skipped = jnp.where(iota((WINDOW, FRAMES), 1) >= SPAN, SPAN, 0)
    allowed = jnp.logical_and(s >= skipped, s < skipped + (WINDOW - SPAN))
    allowed = jnp.logical_and(allowed, s >= first_ref[0])
    for h in range(2):
        mine = one_head(q, h)
        scores = matmul(keys, mine, NT) * (1.0 / math.sqrt(HEAD))
        scores = jnp.where(allowed, scores, -jnp.inf)
        e = jnp.exp(scores - jnp.max(scores, 0, keepdims=True))
        p_ref[h] = e / jnp.sum(e, 0, keepdims=True)


def attention_probs(first, q, k2, k1, k0):
    pair = pl.BlockSpec((FRAMES, 2 * HEAD), lambda i, *_: (0, i))
    return pl.pallas_call(
        attention_probs_kernel,
        grid_spec=pltpu.PrefetchScalarGridSpec(
            num_scalar_prefetch=1,
            grid=(HEADS // 2,),
            in_specs=[pair] * 4,
            out_specs=pl.BlockSpec((2, WINDOW, FRAMES), lambda i, *_: (i, 0, 0)),
        ),
        out_shape=jax.ShapeDtypeStruct((HEADS, WINDOW, FRAMES), F32),
        name="attention_probs",
    )(first, q, k2, k1, k0)


def finish_kernel(
    own_ref, p1_ref, p2_ref, p3_ref, stream_ref, grad_ref, gain_ref,
    p_ref, q_ref, k2_ref, k1_ref, k0_ref, v2_ref, v1_ref, v0_ref,
    o_ref, dq_ref, dk_ref, dv_ref, left1_ref, left2_ref, o_scr,
):
    i = pl.program_id(0)

    @pl.when(i == 0)
    def _():
        dnormed = own_ref[...] + p1_ref[...].astype(F32) + p2_ref[...].astype(F32) + p3_ref[...].astype(F32)
        s = stream_ref[...].astype(F32)
        inverse_rms = lax.rsqrt(jnp.mean(s * s, -1, keepdims=True) + EPSILON)
        scaled = s * inverse_rms
        weighted = dnormed * gain_ref[...]
        mean = jnp.mean(weighted * scaled, -1, keepdims=True)
        o = (grad_ref[...].astype(F32) + inverse_rms * (weighted - scaled * mean)).astype(BF16)
        o_ref[...] = o
        for j in range(HEADS // 2):
            o_scr[j] = o[:, 2 * HEAD * j : 2 * HEAD * (j + 1)]

    o = o_scr[i]
    q = q_ref[...]
    keys = jnp.concatenate([k2_ref[...], k1_ref[...], k0_ref[...]], 0)
    values = jnp.concatenate([v2_ref[...], v1_ref[...], v0_ref[...]], 0)
    dq = dk = dv = None
    for h in range(2):
        o_h, q_h, k_h = one_head(o, h), one_head(q, h), one_head(keys, h)
        probs = p_ref[h]
        rounded = probs.astype(BF16)
        dprob = matmul(values, o_h, NT)
        rowdelta = jnp.sum(rounded.astype(F32) * dprob, 0, keepdims=True)
        dscore = (probs * (dprob - rowdelta)).astype(BF16)
        parts = matmul(dscore, k_h, TN), matmul(dscore, q_h), matmul(rounded, o_h)
        dq, dk, dv = parts if h == 0 else (dq + parts[0], dk + parts[1], dv + parts[2])
    scale = 1.0 / math.sqrt(HEAD)
    dk = dk * scale
    dq_ref[...] = (dq * scale).astype(BF16)
    dk_ref[...] = dk[LEFT:]
    dv_ref[...] = dv[LEFT:]
    left2_ref[0] = dk[:FRAMES].astype(BF16)
    left2_ref[1] = dv[:FRAMES].astype(BF16)
    left1_ref[0] = dk[FRAMES:LEFT].astype(BF16)
    left1_ref[1] = dv[FRAMES:LEFT].astype(BF16)


def finish(parts, stream, grad, gain, probs, q, ks, vs):
    whole = lambda n: pl.BlockSpec((n, D), lambda i: (0, 0))
    pair = pl.BlockSpec((FRAMES, 2 * HEAD), lambda i: (0, i))
    both = pl.BlockSpec((2, FRAMES, 2 * HEAD), lambda i: (0, 0, i))
    out = lambda t: jax.ShapeDtypeStruct((FRAMES, D), t)
    sent = jax.ShapeDtypeStruct((2, FRAMES, D), BF16)
    return pl.pallas_call(
        finish_kernel,
        grid=(HEADS // 2,),
        in_specs=[whole(FRAMES)] * 6
        + [whole(1), pl.BlockSpec((2, WINDOW, FRAMES), lambda i: (i, 0, 0))]
        + [pair] * 7,
        out_specs=[whole(FRAMES), pair, pair, pair, both, both],
        out_shape=(out(BF16), out(BF16), out(F32), out(F32), sent, sent),
        scratch_shapes=[pltpu.VMEM((HEADS // 2, FRAMES, 2 * HEAD), BF16)],
        name="finish",
    )(*parts, stream, grad, gain, probs, q, *ks, *vs)


def turned(x, distance):
    return lax.ppermute(x, "ep", [(i, (i + distance) % EP) for i in range(EP)])


def shifted(x, distance):
    count = lax.axis_size("tm") * lax.axis_size("ep")
    route = [(i, i + distance) for i in range(count) if 0 <= i + distance < count]
    return lax.ppermute(x, ("tm", "ep"), route)


def exchanged(x):
    return lax.all_to_all(x, "tm", split_axis=0, concat_axis=0, tiled=True)


def body(
    queries, keys, values, stream, grad_out, norm_gain, gate_probs, routes, w_gate, w_up, w_down
):
    gain = norm_gain.reshape(1, D)
    weight_gate, weight_up, weight_down = w_gate[0], w_up[0], w_down[0]
    packed, meta = dispatch_x(stream, gain, routes.T, gate_probs.T)
    grads = (grad_out, turned(grad_out, 1), turned(grad_out, -1), turned(grad_out, 2))
    metas = (meta, turned(meta, 1), turned(meta, -1), turned(meta, 2))
    own = exchanged(packed.reshape(EXPERTS, 16, 768)).reshape(EXPERTS * 16, 768)
    left, right = turned(own, 1), turned(own, -1)
    half = EXPERTS * 8
    top, bottom = turned(left[:half], 1), turned(right[half:], -1)
    g_rows = exchanged(dispatch_g(grads, metas).reshape(EXPERTS, EP * CAP, D)).reshape(ROWS, D)
    x_rows, a, s, acted = expert_forward(own, left, right, top, bottom, weight_gate, weight_up)
    dgate, dup, dx = expert_backward(g_rows, a, s, weight_gate, weight_up, weight_down)
    returned = exchanged(dx.reshape(EXPERTS, EP * CAP, D)).reshape(ROWS, D)
    gate_grad = jnp.dot(x_rows.T, dgate, preferred_element_type=F32)
    up_grad = jnp.dot(x_rows.T, dup, preferred_element_type=F32)
    down_grad = jnp.dot(acted.T, g_rows, preferred_element_type=F32)
    mine, part1, part2, part3 = combine(returned, metas)
    parts = (mine, turned(part1, -1), turned(part2, 1), turned(part3, 2))
    ks = (shifted(keys, 2), shifted(keys, 1), keys)
    vs = (shifted(values, 2), shifted(values, 1), values)
    position = lax.axis_index("tm") * lax.axis_size("ep") + lax.axis_index("ep")
    first = jnp.maximum(LEFT - position * FRAMES, 0).astype(jnp.int32).reshape(1)
    probs = attention_probs(first, queries, *ks)
    stream_grad, grad_q, own_k, own_v, left1, left2 = finish(
        parts, stream, grad_out, gain, probs, queries, ks, vs
    )
    back1, back2 = shifted(left1, -1), shifted(left2, -2)
    back = back1.astype(F32) + back2.astype(F32)
    return (
        grad_q,
        (own_k + back[0]).astype(BF16),
        (own_v + back[1]).astype(BF16),
        stream_grad,
        gate_grad[None],
        up_grad[None],
        down_grad[None],
    )


def solution(mesh):
    frames = P(("tm", "ep"), None)
    columns, rows = P("tm", None, "ep"), P("tm", "ep", None)
    return jax.shard_map(
        body,
        mesh=mesh,
        in_specs=(frames,) * 5 + (P(), frames, frames, columns, columns, rows),
        out_specs=(frames,) * 4 + (columns, columns, rows),
        check_vma=False,
    )
```

profile of v0, /device:TPU:31, one launch (start us, length us, event | category | flops | bytes accessed | tf_op | source)
XLA Modules:
  0.0 233.2 jit_solution(13757904344897846334)
XLA Ops:
  0.6 2.6 %dispatch_x.1 = (bf16[512,768]{1,0:T(8,128)(2,1)}, f32[8,128]{1,0:T(8,128)}) custom-call(bf16[128,1024]{1,0:T(8,128)(2,1)} %stream_ref.3, f32[1,1024]{1,0:T(1,128)} %bitcast.51, s32[2,128]{1,0:T(2,128)} %bitcast.53, f32[2,128]{1,0:T(2,128)} %bitcast.54), custom_call_target="tpu_custom_call" | custom-call | tf_op jit(solution)/shard_map/dispatch_x/pallas_call | solution.py:72
  3.2 8.6 %all-to-all-start.1 = ((bf16[32,16,768]{2,1,0:T(8,128)(2,1)}), bf16[32,16,768]{2,1,0:T(8,128)(2,1)S(1)}, u32[]{:S(2)}, u32[]{:S(2)}) async-start(bf16[32,16,768]{2,1,0:T(8,128)(2,1)} %bitcast.50), calls=%async_computation.1 | async-start | bytes 1572864 | tf_op jit(solution)/shard_map/all_to_all | solution.py:357
  14.5 1.8 collective-permute-start.3
  16.3 9.0 %collective-permute-done.3.refs_5_.m1 = f32[8,128]{1,0:T(8,128)S(1)} collective-permute-done((f32[8,128]{1,0:T(8,128)}, f32[8,128]{1,0:T(8,128)S(1)}, u32[]{:S(2)}, u32[]{:S(2)}) %collective-permute-start.3) | collective-permute-done | bytes 4128 | tf_op jit(solution)/shard_map/ppermute | solution.py:347
  26.4 3.0 %collective-permute-done.5.refs_7_.m3 = f32[8,128]{1,0:T(8,128)S(1)} collective-permute-done((f32[8,128]{1,0:T(8,128)}, f32[8,128]{1,0:T(8,128)S(1)}, u32[]{:S(2)}, u32[]{:S(2)}) %collective-permute-start.5) | collective-permute-done | bytes 4128 | tf_op jit(solution)/shard_map/ppermute | solution.py:347
  30.9 6.7 %dispatch_g.1 = bf16[1536,1024]{1,0:T(8,128)(2,1)} custom-call(bf16[128,1024]{1,0:T(8,128)(2,1)} %grad_ref.1, bf16[128,1024]{1,0:T(8,128)(2,1)} %copy-done.12, bf16[128,1024]{1,0:T(8,128)(2,1)} %copy-done.14, bf16[128,1024]{1,0:T(8,128)(2,1)} %copy-done.15, f32[8,128]{1,0:T(8,128)} %get-tuple-element.26.refs_4_.m0, f32[8,128]{1,0:T(8,128)} %copy-done.16, ...), custom_call_target="tpu_custom_call" | custom-call | tf_op jit(solution)/shard_map/dispatch_g/pallas_call | solution.py:116
  38.5 9.4 %all-to-all-start = ((bf16[32,48,1024]{2,1,0:T(8,128)(2,1)}), bf16[32,48,1024]{2,1,0:T(8,128)(2,1)S(1)}, u32[]{:S(2)}, u32[]{:S(2)}) async-start(bf16[32,48,1024]{2,1,0:T(8,128)(2,1)} %bitcast.38), calls=%async_computation | async-start | bytes 6291456 | tf_op jit(solution)/shard_map/all_to_all | solution.py:357
  49.4 17.4 %collective-permute-done.6.left_ref = bf16[512,768]{1,0:T(8,128)(2,1)S(1)} collective-permute-done((bf16[512,768]{1,0:T(8,128)(2,1)}, bf16[512,768]{1,0:T(8,128)(2,1)S(1)}, u32[]{:S(2)}, u32[]{:S(2)}) %collective-permute-start.6) | collective-permute-done | bytes 786464 | tf_op jit(solution)/shard_map/ppermute | solution.py:347
  70.4 7.0 %collective-permute-done.8.top_ref = bf16[256,768]{1,0:T(8,128)(2,1)S(1)} collective-permute-done((bf16[256,768]{1,0:T(8,128)(2,1)S(1)}, bf16[256,768]{1,0:T(8,128)(2,1)S(1)}, u32[]{:S(2)}, u32[]{:S(2)}) %collective-permute-start.8) | collective-permute-done | bytes 393248 | tf_op jit(solution)/shard_map/ppermute | solution.py:347
  77.4 3.7 %collective-permute-done.9.bottom_ref = bf16[256,768]{1,0:T(8,128)(2,1)} collective-permute-done((bf16[256,768]{1,0:T(8,128)(2,1)S(1)}, bf16[256,768]{1,0:T(8,128)(2,1)}, u32[]{:S(2)}, u32[]{:S(2)}) %collective-permute-start.9) | collective-permute-done | bytes 393248 | tf_op jit(solution)/shard_map/ppermute | solution.py:347
  81.1 14.2 %expert_forward.1 = (bf16[1536,1024]{1,0:T(8,128)(2,1)}, f32[1536,1024]{1,0:T(8,128)}, f32[1536,1024]{1,0:T(8,128)}, bf16[1536,1024]{1,0:T(8,128)(2,1)}) custom-call(bf16[512,768]{1,0:T(8,128)(2,1)} %bitcast.47, bf16[512,768]{1,0:T(8,128)(2,1)} %copy-done.4, bf16[512,768]{1,0:T(8,128)(2,1)} %copy-done.5, bf16[256,768]{1,0:T(8,128)(2,1)} %copy-done.9, ...), custom_call_target="tpu_custom_call" | custom-call | tf_op jit(solution)/shard_map/expert_forward/pallas_call | solution.py:180
  97.0 16.5 %expert_backward.1 = (bf16[1536,1024]{1,0:T(8,128)(2,1)}, bf16[1536,1024]{1,0:T(8,128)(2,1)}, bf16[1536,1024]{1,0:T(8,128)(2,1)}) custom-call(bf16[1536,1024]{1,0:T(8,128)(2,1)} %bitcast.39, f32[1536,1024]{1,0:T(8,128)} %get-tuple-element.28.a_ref, f32[1536,1024]{1,0:T(8,128)} %get-tuple-element.29.s_ref, bf16[1024,1024]{1,0:T(8,128)(2,1)} %bitcast.42, ...), custom_call_target="tpu_custom_call" | custom-call | tf_op jit(solution)/shard_map/expert_backward/pallas_call | solution.py:211
  113.5 9.2 %all-to-all-start.2 = ((bf16[32,48,1024]{2,1,0:T(8,128)(2,1)}), bf16[32,48,1024]{2,1,0:T(8,128)(2,1)S(1)}, u32[]{:S(2)}, u32[]{:S(2)}) async-start(bf16[32,48,1024]{2,1,0:T(8,128)(2,1)} %bitcast.48), calls=%async_computation.2 | async-start | bytes 6291456 | tf_op jit(solution)/shard_map/all_to_all | solution.py:357
  122.7 2.7 %collective-permute-start.13 = (bf16[128,1024]{1,0:T(8,128)(2,1)S(1)}, bf16[128,1024]{1,0:T(8,128)(2,1)}, u32[]{:S(2)}, u32[]{:S(2)}) collective-permute-start(bf16[128,1024]{1,0:T(8,128)(2,1)S(1)} %copy-done.6), channel_id=1, source_target_pairs={{0,2},{1,3},{2,4},{3,5},{4,6},{5,7},{6,8},{7,9},{8,10},{9,11},{10,... | collective-permute-start | bytes 786440 | tf_op jit(solution)/shard_map/ppermute | solution.py:353
  125.5 3.8 %collective-permute-start.14 = (bf16[128,1024]{1,0:T(8,128)(2,1)S(1)}, bf16[128,1024]{1,0:T(8,128)(2,1)}, u32[]{:S(2)}, u32[]{:S(2)}) collective-permute-start(bf16[128,1024]{1,0:T(8,128)(2,1)S(1)} %copy-done.6), channel_id=1, source_target_pairs={{0,1},{1,2},{2,3},{3,4},{4,5},{5,6},{6,7},{7,8},{8,9},{9,10},{10,1... | collective-permute-start | bytes 786440 | tf_op jit(solution)/shard_map/ppermute | solution.py:353
  129.2 3.7 %collective-permute-start.15 = (bf16[128,1024]{1,0:T(8,128)(2,1)}, bf16[128,1024]{1,0:T(8,128)(2,1)}, u32[]{:S(2)}, u32[]{:S(2)}) collective-permute-start(bf16[128,1024]{1,0:T(8,128)(2,1)} %v0_ref.1), channel_id=1, source_target_pairs={{0,2},{1,3},{2,4},{3,5},{4,6},{5,7},{6,8},{7,9},{8,10},{9,11},{10,... | collective-permute-start | bytes 786440 | tf_op jit(solution)/shard_map/ppermute | solution.py:353
  132.9 3.3 %collective-permute-start.16 = (bf16[128,1024]{1,0:T(8,128)(2,1)}, bf16[128,1024]{1,0:T(8,128)(2,1)}, u32[]{:S(2)}, u32[]{:S(2)}) collective-permute-start(bf16[128,1024]{1,0:T(8,128)(2,1)} %v0_ref.1), channel_id=1, source_target_pairs={{0,1},{1,2},{2,3},{3,4},{4,5},{5,6},{6,7},{7,8},{8,9},{9,10},{10,1... | collective-permute-start | bytes 786440 | tf_op jit(solution)/shard_map/ppermute | solution.py:353
  136.2 2.4 %collective-permute-done.14.k1_ref = bf16[128,1024]{1,0:T(8,128)(2,1)} collective-permute-done((bf16[128,1024]{1,0:T(8,128)(2,1)S(1)}, bf16[128,1024]{1,0:T(8,128)(2,1)}, u32[]{:S(2)}, u32[]{:S(2)}) %collective-permute-start.14) | collective-permute-done | bytes 262176 | tf_op jit(solution)/shard_map/ppermute | solution.py:353
  138.7 6.4 %attention_probs.1.p_ref = f32[16,384,128]{2,1,0:T(8,128)} custom-call(s32[1]{0:T(128)} %bitcast.12.first_ref, bf16[128,1024]{1,0:T(8,128)(2,1)} %q_ref.3, bf16[128,1024]{1,0:T(8,128)(2,1)} %collective-permute-done.13.k2_ref, bf16[128,1024]{1,0:T(8,128)(2,1)} %collective-permute-done.14.k1_ref, bf16[128,1024]{1,0:T(8,128)(2,1)} %k0_ref.3), custom_call_target="tpu_custom_call" | custom-call | tf_op jit(solution)/shard_map/attention_probs/pallas_call | solution.py:269
  145.1 8.3 %convolution_bitcast_fusion.1 = f32[1,1024,1024]{2,1,0:T(8,128)} fusion(bf16[1536,1024]{1,0:T(8,128)(2,1)} %get-tuple-element.41, bf16[1536,1024]{1,0:T(8,128)(2,1)} %get-tuple-element.43), kind=kOutput, calls=%fused_computation.1 | convolution fusion | flops 3221225472 | bytes 10485760 | tf_op jit(solution)/shard_map/dot_general | solution.py:377
  153.4 8.0 %all-to-all-done.2 = bf16[32,48,1024]{2,1,0:T(8,128)(2,1)S(1)} async-done(((bf16[32,48,1024]{2,1,0:T(8,128)(2,1)}), bf16[32,48,1024]{2,1,0:T(8,128)(2,1)S(1)}, u32[]{:S(2)}, u32[]{:S(2)}) %all-to-all-start.2) | async-done | bytes 3145760 | tf_op jit(solution)/shard_map/all_to_all | solution.py:357
  163.1 4.6 %combine.1 = (f32[128,1024]{1,0:T(8,128)}, bf16[128,1024]{1,0:T(8,128)(2,1)}, bf16[128,1024]{1,0:T(8,128)(2,1)}, bf16[128,1024]{1,0:T(8,128)(2,1)}) custom-call(bf16[1536,1024]{1,0:T(8,128)(2,1)} %bitcast.37, f32[8,128]{1,0:T(8,128)} %get-tuple-element.26.refs_4_.m0, f32[8,128]{1,0:T(8,128)} %copy-done.16, f32[8,128]{1,0:T(8,128)} %copy-done.17, ...), custom_call_target="tpu_custom_call" | custom-call | tf_op jit(solution)/shard_map/combine/pallas_call | solution.py:236
  167.7 7.8 %collective-permute-start.11 = (bf16[128,1024]{1,0:T(8,128)(2,1)}, bf16[128,1024]{1,0:T(8,128)(2,1)S(1)}, u32[]{:S(2)}, u32[]{:S(2)}) collective-permute-start(bf16[128,1024]{1,0:T(8,128)(2,1)} %get-tuple-element.33), channel_id=1, source_target_pairs={{0,1},{1,2},{2,3},{3,0},{4,5},{5,6},{6,7},{7,4},{8,9},{9,10},{10,1... | collective-permute-start | bytes 786440 | tf_op jit(solution)/shard_map/ppermute | solution.py:347
  176.6 8.3 %convolution_bitcast_fusion.2 = f32[1,1024,1024]{2,1,0:T(8,128)} fusion(bf16[1536,1024]{1,0:T(8,128)(2,1)} %get-tuple-element.41, bf16[1536,1024]{1,0:T(8,128)(2,1)} %get-tuple-element.42), kind=kOutput, calls=%fused_computation.2 | convolution fusion | flops 3221225472 | bytes 10485760 | tf_op jit(solution)/shard_map/dot_general | solution.py:376
  185.0 1.8 collective-permute-done.11.p2_ref
  186.7 1.8 collective-permute-done.12.p3_ref
  189.2 9.8 %finish.1 = (bf16[128,1024]{1,0:T(8,128)(2,1)}, bf16[128,1024]{1,0:T(8,128)(2,1)}, f32[128,1024]{1,0:T(8,128)}, f32[128,1024]{1,0:T(8,128)}, bf16[2,128,1024]{2,...) custom-call(f32[128,1024]{1,0:T(8,128)} %get-tuple-element.31.own_ref, bf16[128,1024]{1,0:T(8,128)(2,1)} %copy-done.10, ...), custom_call_target="tpu_custom_call" | custom-call | tf_op jit(solution)/shard_map/finish/pallas_call | solution.py:333
  199.0 2.5 %collective-permute-start.17 = (bf16[2,128,1024]{2,1,0:T(8,128)(2,1)}, bf16[2,128,1024]{2,1,0:T(8,128)(2,1)S(1)}, u32[]{:S(2)}, u32[]{:S(2)}) collective-permute-start(bf16[2,128,1024]{2,1,0:T(8,128)(2,1)} %get-tuple-element.37), channel_id=1, source_target_pairs={{1,0},{2,1},{3,2},{4,3},{5,4},{6,5},{7,6},{8,7},{9,8},{10,9},{11,1... | collective-permute-start | bytes 1572872 | tf_op jit(solution)/shard_map/ppermute | solution.py:353
  201.5 4.7 %collective-permute-start.18 = (bf16[2,128,1024]{2,1,0:T(8,128)(2,1)}, bf16[2,128,1024]{2,1,0:T(8,128)(2,1)S(1)}, u32[]{:S(2)}, u32[]{:S(2)}) collective-permute-start(bf16[2,128,1024]{2,1,0:T(8,128)(2,1)} %get-tuple-element.38), channel_id=1, source_target_pairs={{2,0},{3,1},{4,2},{5,3},{6,4},{7,5},{8,6},{9,7},{10,8},{11,9},{12,... | collective-permute-start | bytes 1572872 | tf_op jit(solution)/shard_map/ppermute | solution.py:353
  206.3 7.0 %convolution_bitcast_fusion = f32[1,1024,1024]{2,1,0:T(8,128)} fusion(bf16[1536,1024]{1,0:T(8,128)(2,1)} %get-tuple-element.44, bf16[1536,1024]{1,0:T(8,128)(2,1)S(1)} %bitcast.40), kind=kOutput, calls=%fused_computation | convolution fusion | flops 3221225472 | bytes 10485760 | tf_op jit(solution)/shard_map/dot_general | solution.py:378
  213.3 7.2 %collective-permute-done.17 = bf16[2,128,1024]{2,1,0:T(8,128)(2,1)S(1)} collective-permute-done((bf16[2,128,1024]{2,1,0:T(8,128)(2,1)}, bf16[2,128,1024]{2,1,0:T(8,128)(2,1)S(1)}, u32[]{:S(2)}, u32[]{:S(2)}) %collective-permute-start.17) | collective-permute-done | bytes 524320 | tf_op jit(solution)/shard_map/ppermute | solution.py:353
  220.5 11.6 %collective-permute-done.18 = bf16[2,128,1024]{2,1,0:T(8,128)(2,1)S(1)} collective-permute-done((bf16[2,128,1024]{2,1,0:T(8,128)(2,1)}, bf16[2,128,1024]{2,1,0:T(8,128)(2,1)S(1)}, u32[]{:S(2)}, u32[]{:S(2)}) %collective-permute-start.18) | collective-permute-done | bytes 524320 | tf_op jit(solution)/shard_map/ppermute | solution.py:353
  (64 shorter events, 17.5 us)
Async XLA Ops:
  3.2 34.4 %all-to-all-start.1 = ((bf16[32,16,768]{2,1,0:T(8,128)(2,1)}), bf16[32,16,768]{2,1,0:T(8,128)(2,1)S(1)}, u32[]{:S(2)}, u32[]{:S(2)}) async-start(bf16[32,16,768]{2,1,0:T(8,128)(2,1)} %bitcast.50), calls=%async_computation.1 | async-start | bytes 1572864 | tf_op jit(solution)/shard_map/all_to_all | solution.py:357
  11.8 17.6 %collective-permute-start = (bf16[128,1024]{1,0:T(8,128)(2,1)}, bf16[128,1024]{1,0:T(8,128)(2,1)S(1)}, u32[]{:S(2)}, u32[]{:S(2)}) collective-permute-start(bf16[128,1024]{1,0:T(8,128)(2,1)} %grad_ref.1), channel_id=1, source_target_pairs={{0,1},{1,2},{2,3},{3,0},{4,5},{5,6},{6,7},{7,4},{8,9},{9,10},{10,1... | collective-permute-start | bytes 786440 | tf_op jit(solution)/shard_map/ppermute | solution.py:347
  12.1 17.4 %collective-permute-start.1 = (bf16[128,1024]{1,0:T(8,128)(2,1)}, bf16[128,1024]{1,0:T(8,128)(2,1)S(1)}, u32[]{:S(2)}, u32[]{:S(2)}) collective-permute-start(bf16[128,1024]{1,0:T(8,128)(2,1)} %grad_ref.1), channel_id=1, source_target_pairs={{0,3},{1,0},{2,1},{3,2},{4,7},{5,4},{6,5},{7,6},{8,11},{9,8},{10,9... | collective-permute-start | bytes 786440 | tf_op jit(solution)/shard_map/ppermute | solution.py:347
  13.3 16.1 %collective-permute-start.2 = (bf16[128,1024]{1,0:T(8,128)(2,1)}, bf16[128,1024]{1,0:T(8,128)(2,1)S(1)}, u32[]{:S(2)}, u32[]{:S(2)}) collective-permute-start(bf16[128,1024]{1,0:T(8,128)(2,1)} %grad_ref.1), channel_id=1, source_target_pairs={{0,2},{1,3},{2,0},{3,1},{4,6},{5,7},{6,4},{7,5},{8,10},{9,11},{10,... | collective-permute-start | bytes 786440 | tf_op jit(solution)/shard_map/ppermute | solution.py:347
  14.5 10.8 %collective-permute-start.3 = (f32[8,128]{1,0:T(8,128)}, f32[8,128]{1,0:T(8,128)S(1)}, u32[]{:S(2)}, u32[]{:S(2)}) collective-permute-start(f32[8,128]{1,0:T(8,128)} %get-tuple-element.26.refs_4_.m0), channel_id=1, source_target_pairs={{0,1},{1,2},{2,3},{3,0},{4,5},{5,6},{6,7},{7,4},{8,9},{9,10},{10,1... | collective-permute-start | bytes 12296 | tf_op jit(solution)/shard_map/ppermute | solution.py:347
  16.3 10.2 %collective-permute-start.4 = (f32[8,128]{1,0:T(8,128)}, f32[8,128]{1,0:T(8,128)S(1)}, u32[]{:S(2)}, u32[]{:S(2)}) collective-permute-start(f32[8,128]{1,0:T(8,128)} %get-tuple-element.26.refs_4_.m0), channel_id=1, source_target_pairs={{0,3},{1,0},{2,1},{3,2},{4,7},{5,4},{6,5},{7,6},{8,11},{9,8},{10,9... | collective-permute-start | bytes 12296 | tf_op jit(solution)/shard_map/ppermute | solution.py:347
  25.3 4.2 %copy-start.16 = (f32[8,128]{1,0:T(8,128)}, f32[8,128]{1,0:T(8,128)S(1)}, u32[]{:S(2)}) copy-start(f32[8,128]{1,0:T(8,128)S(1)} %collective-permute-done.3.refs_5_.m1) | copy-start | bytes 12292
  25.3 4.2 %collective-permute-start.5 = (f32[8,128]{1,0:T(8,128)}, f32[8,128]{1,0:T(8,128)S(1)}, u32[]{:S(2)}, u32[]{:S(2)}) collective-permute-start(f32[8,128]{1,0:T(8,128)} %get-tuple-element.26.refs_4_.m0), channel_id=1, source_target_pairs={{0,2},{1,3},{2,0},{3,1},{4,6},{5,7},{6,4},{7,5},{8,10},{9,11},{10,... | collective-permute-start | bytes 12296 | tf_op jit(solution)/shard_map/ppermute | solution.py:347
  26.4 3.0 %copy-start.17 = (f32[8,128]{1,0:T(8,128)}, f32[8,128]{1,0:T(8,128)S(1)}, u32[]{:S(2)}) copy-start(f32[8,128]{1,0:T(8,128)S(1)} %collective-permute-done.4.refs_6_.m2) | copy-start | bytes 12292
  38.5 56.8 %all-to-all-start = ((bf16[32,48,1024]{2,1,0:T(8,128)(2,1)}), bf16[32,48,1024]{2,1,0:T(8,128)(2,1)S(1)}, u32[]{:S(2)}, u32[]{:S(2)}) async-start(bf16[32,48,1024]{2,1,0:T(8,128)(2,1)} %bitcast.38), calls=%async_computation | async-start | bytes 6291456 | tf_op jit(solution)/shard_map/all_to_all | solution.py:357
  47.9 19.0 %collective-permute-start.6 = (bf16[512,768]{1,0:T(8,128)(2,1)}, bf16[512,768]{1,0:T(8,128)(2,1)S(1)}, u32[]{:S(2)}, u32[]{:S(2)}) collective-permute-start(bf16[512,768]{1,0:T(8,128)(2,1)} %bitcast.45), channel_id=1, source_target_pairs={{0,1},{1,2},{2,3},{3,0},{4,5},{5,6},{6,7},{7,4},{8,9},{9,10},{10,1... | collective-permute-start | bytes 2359304 | tf_op jit(solution)/shard_map/ppermute | solution.py:347
  48.0 21.4 %collective-permute-start.7 = (bf16[512,768]{1,0:T(8,128)(2,1)}, bf16[512,768]{1,0:T(8,128)(2,1)S(1)}, u32[]{:S(2)}, u32[]{:S(2)}) collective-permute-start(bf16[512,768]{1,0:T(8,128)(2,1)} %bitcast.46), channel_id=1, source_target_pairs={{0,3},{1,0},{2,1},{3,2},{4,7},{5,4},{6,5},{7,6},{8,11},{9,8},{10,9... | collective-permute-start | bytes 2359304 | tf_op jit(solution)/shard_map/ppermute | solution.py:347
  67.8 9.6 %collective-permute-start.8 = (bf16[256,768]{1,0:T(8,128)(2,1)S(1)}, bf16[256,768]{1,0:T(8,128)(2,1)S(1)}, u32[]{:S(2)}, u32[]{:S(2)}) collective-permute-start(bf16[256,768]{1,0:T(8,128)(2,1)S(1)} %slice.16), channel_id=1, source_target_pairs={{0,1},{1,2},{2,3},{3,0},{4,5},{5,6},{6,7},{7,4},{8,9},{9,10},{10,1... | collective-permute-start | bytes 1179656 | tf_op jit(solution)/shard_map/ppermute | solution.py:347
  70.3 10.8 %collective-permute-start.9 = (bf16[256,768]{1,0:T(8,128)(2,1)S(1)}, bf16[256,768]{1,0:T(8,128)(2,1)}, u32[]{:S(2)}, u32[]{:S(2)}) collective-permute-start(bf16[256,768]{1,0:T(8,128)(2,1)S(1)} %slice.17), channel_id=1, source_target_pairs={{0,3},{1,0},{2,1},{3,2},{4,7},{5,4},{6,5},{7,6},{8,11},{9,8},{10,9... | collective-permute-start | bytes 1179656 | tf_op jit(solution)/shard_map/ppermute | solution.py:347
  77.4 3.7 %copy-start.9 = (bf16[256,768]{1,0:T(8,128)(2,1)}, bf16[256,768]{1,0:T(8,128)(2,1)S(1)}, u32[]{:S(2)}) copy-start(bf16[256,768]{1,0:T(8,128)(2,1)S(1)} %collective-permute-done.8.top_ref) | copy-start | bytes 1179652
  95.3 1.7 copy-start.1
  113.5 9.2 %copy-start.6 = (bf16[128,1024]{1,0:T(8,128)(2,1)S(1)}, bf16[128,1024]{1,0:T(8,128)(2,1)}, u32[]{:S(2)}) copy-start(bf16[128,1024]{1,0:T(8,128)(2,1)} %k0_ref.3) | copy-start | bytes 786436
  113.5 48.0 %all-to-all-start.2 = ((bf16[32,48,1024]{2,1,0:T(8,128)(2,1)}), bf16[32,48,1024]{2,1,0:T(8,128)(2,1)S(1)}, u32[]{:S(2)}, u32[]{:S(2)}) async-start(bf16[32,48,1024]{2,1,0:T(8,128)(2,1)} %bitcast.48), calls=%async_computation.2 | async-start | bytes 6291456 | tf_op jit(solution)/shard_map/all_to_all | solution.py:357
  122.7 13.5 %collective-permute-start.13 = (bf16[128,1024]{1,0:T(8,128)(2,1)S(1)}, bf16[128,1024]{1,0:T(8,128)(2,1)}, u32[]{:S(2)}, u32[]{:S(2)}) collective-permute-start(bf16[128,1024]{1,0:T(8,128)(2,1)S(1)} %copy-done.6), channel_id=1, source_target_pairs={{0,2},{1,3},{2,4},{3,5},{4,6},{5,7},{6,8},{7,9},{8,10},{9,11},{10,... | collective-permute-start | bytes 786440 | tf_op jit(solution)/shard_map/ppermute | solution.py:353
  125.5 13.2 %collective-permute-start.14 = (bf16[128,1024]{1,0:T(8,128)(2,1)S(1)}, bf16[128,1024]{1,0:T(8,128)(2,1)}, u32[]{:S(2)}, u32[]{:S(2)}) collective-permute-start(bf16[128,1024]{1,0:T(8,128)(2,1)S(1)} %copy-done.6), channel_id=1, source_target_pairs={{0,1},{1,2},{2,3},{3,4},{4,5},{5,6},{6,7},{7,8},{8,9},{9,10},{10,1... | collective-permute-start | bytes 786440 | tf_op jit(solution)/shard_map/ppermute | solution.py:353
  129.2 55.7 %collective-permute-start.15 = (bf16[128,1024]{1,0:T(8,128)(2,1)}, bf16[128,1024]{1,0:T(8,128)(2,1)}, u32[]{:S(2)}, u32[]{:S(2)}) collective-permute-start(bf16[128,1024]{1,0:T(8,128)(2,1)} %v0_ref.1), channel_id=1, source_target_pairs={{0,2},{1,3},{2,4},{3,5},{4,6},{5,7},{6,8},{7,9},{8,10},{9,11},{10,... | collective-permute-start | bytes 786440 | tf_op jit(solution)/shard_map/ppermute | solution.py:353
  132.9 52.0 %collective-permute-start.16 = (bf16[128,1024]{1,0:T(8,128)(2,1)}, bf16[128,1024]{1,0:T(8,128)(2,1)}, u32[]{:S(2)}, u32[]{:S(2)}) collective-permute-start(bf16[128,1024]{1,0:T(8,128)(2,1)} %v0_ref.1), channel_id=1, source_target_pairs={{0,1},{1,2},{2,3},{3,4},{4,5},{5,6},{6,7},{7,8},{8,9},{9,10},{10,1... | collective-permute-start | bytes 786440 | tf_op jit(solution)/shard_map/ppermute | solution.py:353
  167.7 17.3 %collective-permute-start.10 = (bf16[128,1024]{1,0:T(8,128)(2,1)}, bf16[128,1024]{1,0:T(8,128)(2,1)S(1)}, u32[]{:S(2)}, u32[]{:S(2)}) collective-permute-start(bf16[128,1024]{1,0:T(8,128)(2,1)} %get-tuple-element.32), channel_id=1, source_target_pairs={{0,3},{1,0},{2,1},{3,2},{4,7},{5,4},{6,5},{7,6},{8,11},{9,8},{10,9... | collective-permute-start | bytes 786440 | tf_op jit(solution)/shard_map/ppermute | solution.py:347
  167.7 19.1 %collective-permute-start.11 = (bf16[128,1024]{1,0:T(8,128)(2,1)}, bf16[128,1024]{1,0:T(8,128)(2,1)S(1)}, u32[]{:S(2)}, u32[]{:S(2)}) collective-permute-start(bf16[128,1024]{1,0:T(8,128)(2,1)} %get-tuple-element.33), channel_id=1, source_target_pairs={{0,1},{1,2},{2,3},{3,0},{4,5},{5,6},{6,7},{7,4},{8,9},{9,10},{10,1... | collective-permute-start | bytes 786440 | tf_op jit(solution)/shard_map/ppermute | solution.py:347
  175.4 13.1 %collective-permute-start.12 = (bf16[128,1024]{1,0:T(8,128)(2,1)}, bf16[128,1024]{1,0:T(8,128)(2,1)S(1)}, u32[]{:S(2)}, u32[]{:S(2)}) collective-permute-start(bf16[128,1024]{1,0:T(8,128)(2,1)} %get-tuple-element.34), channel_id=1, source_target_pairs={{0,2},{1,3},{2,0},{3,1},{4,6},{5,7},{6,4},{7,5},{8,10},{9,11},{10,... | collective-permute-start | bytes 786440 | tf_op jit(solution)/shard_map/ppermute | solution.py:347
  184.9 4.3 %copy-start.10 = (bf16[128,1024]{1,0:T(8,128)(2,1)}, bf16[128,1024]{1,0:T(8,128)(2,1)S(1)}, u32[]{:S(2)}) copy-start(bf16[128,1024]{1,0:T(8,128)(2,1)S(1)} %collective-permute-done.10.p1_ref) | copy-start | bytes 786436
  186.7 1.8 copy-start.11
  189.2 17.0 %copy-start.2 = (bf16[32,48,1024]{2,1,0:T(8,128)(2,1)S(1)}, bf16[32,48,1024]{2,1,0:T(8,128)(2,1)}, u32[]{:S(2)}) copy-start(bf16[32,48,1024]{2,1,0:T(8,128)(2,1)} %copy-done.1) | copy-start | bytes 9437188
  199.0 21.4 %collective-permute-start.17 = (bf16[2,128,1024]{2,1,0:T(8,128)(2,1)}, bf16[2,128,1024]{2,1,0:T(8,128)(2,1)S(1)}, u32[]{:S(2)}, u32[]{:S(2)}) collective-permute-start(bf16[2,128,1024]{2,1,0:T(8,128)(2,1)} %get-tuple-element.37), channel_id=1, source_target_pairs={{1,0},{2,1},{3,2},{4,3},{5,4},{6,5},{7,6},{8,7},{9,8},{10,9},{11,1... | collective-permute-start | bytes 1572872 | tf_op jit(solution)/shard_map/ppermute | solution.py:353
  201.5 30.6 %collective-permute-start.18 = (bf16[2,128,1024]{2,1,0:T(8,128)(2,1)}, bf16[2,128,1024]{2,1,0:T(8,128)(2,1)S(1)}, u32[]{:S(2)}, u32[]{:S(2)}) collective-permute-start(bf16[2,128,1024]{2,1,0:T(8,128)(2,1)} %get-tuple-element.38), channel_id=1, source_target_pairs={{2,0},{3,1},{4,2},{5,3},{6,4},{7,5},{8,6},{9,7},{10,8},{11,9},{12,... | collective-permute-start | bytes 1572872 | tf_op jit(solution)/shard_map/ppermute | solution.py:353
  206.3 26.0 %copy-start.7 = (f32[128,1024]{1,0:T(8,128)S(1)}, f32[128,1024]{1,0:T(8,128)}, u32[]{:S(2)}) copy-start(f32[128,1024]{1,0:T(8,128)} %get-tuple-element.36) | copy-start | bytes 1572868
  206.3 26.0 %copy-start.8 = (f32[128,1024]{1,0:T(8,128)S(1)}, f32[128,1024]{1,0:T(8,128)}, u32[]{:S(2)}) copy-start(f32[128,1024]{1,0:T(8,128)} %get-tuple-element.39) | copy-start | bytes 1572868
  (9 other events, 7.8 us)
where the time goes:
time: 234 us; the launch traced here: 233 us
  waiting for transfers between devices  73 us (31%)
  starting transfers between devices  65.6 us (28%)
  Pallas kernels  60.8 us (26%)
  matrix products  23.6 us (10%)
  local copies, waits for them, and re-layouts  8.19 us (4%)
    ppermute x13, waiting for transfers between devices, turned(): return lax.ppermute(x, 'ep', [(i, (i + distance) % EP) for i in range(EP)])  43.7 us
    all_to_all x3, starting transfers between devices, exchanged(): return lax.all_to_all(x, 'tm', split_axis=0, concat_axis=0, tiled=True)  27.2 us
    ppermute x6, waiting for transfers between devices, shifted(): return lax.ppermute(x, ('tm', 'ep'), route)  21.3 us
    ppermute x6, starting transfers between devices, shifted(): return lax.ppermute(x, ('tm', 'ep'), route)  20.6 us
    ppermute x13, starting transfers between devices, turned(): return lax.ppermute(x, 'ep', [(i, (i + distance) % EP) for i in range(EP)])  17.8 us
    pallas_call x1, Pallas kernels, expert_backward(): pl.pallas_call(expert_backward_kernel, grid=(STEPS,), in_specs=[rows, row...  16.5 us
    pallas_call x1, Pallas kernels, expert_forward(): pl.pallas_call(expert_forward_kernel, grid=(STEPS,), in_specs=[rows(lambd...  14.2 us
    pallas_call x1, Pallas kernels, finish(): pl.pallas_call(finish_kernel, grid=(HEADS // 2,), in_specs=[whole(FRAMES)...  9.8 us
  transfers between devices with their start and end apart: 22, of which 11 were waited for; matrix products, arithmetic and copies ran while one was open for 10% of the time, Pallas kernels for 14%

commit v1 on v0

v1 whole, which is shorter than its diff:
```python
import math

import jax
import jax.numpy as jnp
from jax import lax
from jax.experimental import pallas as pl
from jax.experimental.pallas import tpu as pltpu
from jax.sharding import PartitionSpec as P

D = 1024
HEADS = 16
HEAD = 64
SPAN = 64
LEFT = 256
FRAMES = 128
EXPERTS = 32
CAP = 12
EP = 4
ROWS = EXPERTS * EP * CAP
EPSILON = 1e-06
BF16 = jnp.bfloat16
F32 = jnp.float32
NT = (((1,), (1,)), ((), ()))
TN = (((0,), (0,)), ((), ()))


def iota(shape, dim):
    return lax.broadcasted_iota(jnp.int32, shape, dim)


def ones_where(mask):
    return jnp.where(mask, 1.0, 0.0).astype(BF16)


def matmul(a, b, dims=(((1,), (0,)), ((), ()))):
    return lax.dot_general(a, b, dims, preferred_element_type=F32)


PACK = EXPERTS * 16
CHUNK = EXPERTS * CAP
GROUP = 16
EXTRA = 16


def column_block(j):
    return slice(256 * j, 256 * (j + 1))


def picked(ids, valid, places):
    ids = jnp.where(valid, ids, -1).astype(F32)
    return ones_where(jnp.logical_or(ids == places[0], ids == places[1]))


def dispatch_x_kernel(stream_ref, grad_ref, gain_ref, routes_ref, gates_ref, packed_ref, block_ref):
    s = stream_ref[...].astype(F32)
    inverse_rms = lax.rsqrt(jnp.mean(s * s, -1, keepdims=True) + EPSILON)
    normed = ((s * inverse_rms) * gain_ref[...]).astype(BF16)
    routes = routes_ref[...]
    expert = iota((EXPERTS, FRAMES), 0)
    named = [expert == routes[k : k + 1, :] for k in range(2)]
    count = ones_where(jnp.logical_or(named[0], named[1]))
    earlier = ones_where(iota((FRAMES, FRAMES), 0) < iota((FRAMES, FRAMES), 1))
    before = matmul(count, earlier)
    route = [routes[k : k + 1, :].astype(F32) for k in range(2)]
    slot = [jnp.sum(jnp.where(named[k], before, 0.0), 0, keepdims=True) for k in range(2)]
    places = [route[k] * CAP + slot[k] for k in range(2)]
    split = []
    for k in range(2):
        gate = gates_ref[k : k + 1, :]
        high = gate.astype(BF16).astype(F32)
        middle = (gate - high).astype(BF16).astype(F32)
        split += [high, middle, gate - high - middle]
    block_ref[0:FRAMES, :] = grad_ref[...]
    block_ref[FRAMES:, :] = jnp.zeros((EXTRA, D), BF16)
    extra = jnp.concatenate(route + slot + split + [jnp.zeros((EXTRA - 10, FRAMES), F32)], 0)
    block_ref[FRAMES:, 0:FRAMES] = extra.astype(BF16)
    row = iota((PACK, FRAMES), 0)
    lane = row & 15
    base = (row >> 4) * CAP
    main = picked(base + lane, lane < CAP, places)
    for j in range(3):
        last = picked(base + (lane - CAP) + 4 * j, lane >= CAP, places)
        c = column_block(j)
        packed_ref[:, c] = (matmul(main, normed[:, c]) + matmul(last, normed[:, 768:])).astype(BF16)


def dispatch_x(stream, grad, gain, routes, gates):
    return pl.pallas_call(
        dispatch_x_kernel,
        out_shape=(
            jax.ShapeDtypeStruct((PACK, 768), BF16),
            jax.ShapeDtypeStruct((FRAMES + EXTRA, D), BF16),
        ),
        name="dispatch_x",
    )(stream, grad, gain, routes, gates)


def dispatch_g_kernel(*refs):
    blocks, out_ref, pairs, keys = refs[:EP], refs[EP], refs[EP + 1], refs[EP + 2]
    step = pl.program_id(0)

    for q in range(EP):

        @pl.when(step == q)
        def _(q=q):
            extra = blocks[q][FRAMES:, 0:FRAMES].astype(F32)
            upright = extra.T
            g = blocks[q][0:FRAMES, :].astype(F32)
            for k in range(2):
                gate = upright[:, 4 + 3 * k : 5 + 3 * k] + upright[:, 5 + 3 * k : 6 + 3 * k]
                gate = gate + upright[:, 6 + 3 * k : 7 + 3 * k]
                pairs[k * FRAMES : (k + 1) * FRAMES, :] = (gate * g).astype(BF16)
                keys[k : k + 1, :] = extra[k : k + 1, :] * CAP + extra[2 + k : 3 + k, :]

    row = iota((PACK, FRAMES), 0)
    lane = row & 15
    base = (row >> 4) * CAP

    def pick(ids, valid):
        ids = jnp.where(valid, ids, -1).astype(F32)
        return jnp.concatenate([ones_where(ids == keys[k : k + 1, :]) for k in range(2)], 1)

    main = pick(base + lane, lane < CAP)
    for j in range(3):
        last = pick(base + (lane - CAP) + 4 * j, lane >= CAP)
        c = column_block(j)
        rows = matmul(main, pairs[:, c]) + matmul(last, pairs[:, 768:])
        out_ref[:, 0, :, c] = rows.astype(BF16).reshape(EXPERTS, 16, 256)


def dispatch_g(blocks):
    return pl.pallas_call(
        dispatch_g_kernel,
        grid=(EP,),
        in_specs=[pl.BlockSpec((FRAMES + EXTRA, D), lambda i: (0, 0))] * EP,
        out_specs=pl.BlockSpec((EXPERTS, 1, 16, 768), lambda i: (0, i, 0, 0)),
        out_shape=jax.ShapeDtypeStruct((EXPERTS, EP, 16, 768), BF16),
        scratch_shapes=[pltpu.VMEM((2 * FRAMES, D), BF16), pltpu.VMEM((8, FRAMES), F32)],
        name="dispatch_g",
    )(*blocks)


def fill_moves(moves, packed_dim):
    shape = (GROUP * 16, GROUP * CAP) if packed_dim == 0 else (GROUP * CAP, GROUP * 16)
    p = iota(shape, packed_dim)
    r = iota(shape, 1 - packed_dim)
    sender = (r * 1366) >> 14
    slot = r - sender * CAP
    same = (p >> 4) == sender
    lane = p & 15
    moves[0] = ones_where(jnp.logical_and(same, lane == slot))
    for j in range(3):
        hit = jnp.logical_and(same, lane == CAP + slot - 4 * j)
        moves[1 + j] = ones_where(jnp.logical_and(hit, (slot >> 2) == j))


def unpack(packed, moves, out_ref):
    for g in range(EXPERTS // GROUP):
        part = packed[GROUP * 16 * g : GROUP * 16 * (g + 1), :]
        rows = slice(GROUP * CAP * g, GROUP * CAP * (g + 1))
        out_ref[rows, 0:768] = matmul(moves[0], part).astype(BF16)
        last = matmul(moves[1], part[:, column_block(0)])
        last += matmul(moves[2], part[:, column_block(1)])
        last += matmul(moves[3], part[:, column_block(2)])
        out_ref[rows, 768:1024] = last.astype(BF16)


N_BLOCK = 256


def forward_kernel(count, *refs):
    parts, gate_ref, up_ref = refs[:count], refs[count], refs[count + 1]
    x_ref, a_ref, s_ref, acted_ref, moves = refs[-5:]

    @pl.when(pl.program_id(0) == 0)
    def _():
        fill_moves(moves, 1)
        unpack(jnp.concatenate([p[...] for p in parts], 0), moves, x_ref)

    x = x_ref[...]
    gate = matmul(x, gate_ref[...])
    up = matmul(x, up_ref[...])
    sig = jax.nn.sigmoid(gate)
    silu = gate * sig
    acted_ref[...] = (silu * up).astype(BF16)
    s_ref[...] = silu
    a_ref[...] = up * sig * (1.0 + gate * (1.0 - sig))


def expert_forward(q, parts, w_gate, w_up, filled):
    whole = [pl.BlockSpec(p.shape, lambda j: (0, 0)) for p in parts]
    weight = pl.BlockSpec((D, N_BLOCK), lambda j: (0, j))
    out = pl.BlockSpec((CHUNK, N_BLOCK), lambda j: (q, j))
    shape = lambda t: jax.ShapeDtypeStruct((ROWS, D), t)
    n = len(parts)
    return pl.pallas_call(
        lambda *refs: forward_kernel(n, *refs),
        grid=(D // N_BLOCK,),
        in_specs=whole + [weight] * 2 + [pl.BlockSpec(memory_space=pl.ANY)] * len(filled),
        out_specs=[pl.BlockSpec((CHUNK, D), lambda j: (q, 0)), out, out, out],
        out_shape=(shape(BF16), shape(F32), shape(F32), shape(BF16)),
        scratch_shapes=[pltpu.VMEM((4, GROUP * CAP, GROUP * 16), BF16)],
        input_output_aliases={n + 2 + i: i for i in range(len(filled))},
        name="expert_forward",
    )(*parts, w_gate, w_up, *filled)


def backward_kernel(
    order_ref, packed_ref, a_ref, s_ref, gate_ref, up_ref, down_ref, g_ref, dgate_ref, dup_ref, out_ref, moves, back
):
    @pl.when(pl.program_id(0) == 0)
    def _():
        fill_moves(moves, 1)
        fill_moves(back, 0)

    unpack(packed_ref[...].reshape(PACK, 768), moves, g_ref)
    dact = matmul(g_ref[...], down_ref[...], NT)
    dgate = (dact * a_ref[...]).astype(BF16)
    dup = (dact * s_ref[...]).astype(BF16)
    dgate_ref[...] = dgate
    dup_ref[...] = dup
    dx = (matmul(dgate, gate_ref[...], NT) + matmul(dup, up_ref[...], NT)).astype(BF16)
    for g in range(EXPERTS // GROUP):
        part = dx[GROUP * CAP * g : GROUP * CAP * (g + 1), :]
        for j in range(3):
            c = column_block(j)
            rows = matmul(back[0], part[:, c]) + matmul(back[1 + j], part[:, 768:])
            out_ref[GROUP * g : GROUP * (g + 1), 0, :, c] = rows.astype(BF16).reshape(GROUP, 16, 256)


def expert_backward(order, packed, a, s, w_gate, w_up, w_down):
    weight = pl.BlockSpec((D, D), lambda i, o: (0, 0), pipeline_mode=pl.Buffered(1))
    rows = pl.BlockSpec((CHUNK, D), lambda i, o: (i, 0))
    shape = jax.ShapeDtypeStruct((ROWS, D), BF16)
    return pl.pallas_call(
        backward_kernel,
        grid_spec=pltpu.PrefetchScalarGridSpec(
            num_scalar_prefetch=1,
            grid=(EP,),
            in_specs=[
                pl.BlockSpec((EXPERTS, 1, 16, 768), lambda i, o: (0, i, 0, 0)),
                rows,
                rows,
                weight,
                weight,
                weight,
            ],
            out_specs=[rows, rows, rows, pl.BlockSpec((EXPERTS, 1, 16, 768), lambda i, o: (0, o[i], 0, 0))],
            scratch_shapes=[
                pltpu.VMEM((4, GROUP * CAP, GROUP * 16), BF16),
                pltpu.VMEM((4, GROUP * 16, GROUP * CAP), BF16),
            ],
        ),
        out_shape=(shape, shape, shape, jax.ShapeDtypeStruct((EXPERTS, EP, 16, 768), BF16)),
        name="expert_backward",
    )(order, packed, a, s, w_gate, w_up, w_down)


WINDOW = LEFT + FRAMES
SCALE = 1.0 / math.sqrt(HEAD)
PAIRS = HEADS // 2


def one_head(pair, h):
    lane = iota(pair.shape, 1)
    mask = lane >= HEAD if h else lane < HEAD
    return jnp.where(mask, pair.astype(F32), 0.0).astype(BF16)


def probs_kernel(first_ref, q_ref, k2_ref, k1_ref, k0_ref, p_ref, stats_ref):
    keys = jnp.concatenate([k2_ref[...], k1_ref[...], k0_ref[...]], 0)
    q = q_ref[...]
    s = iota((WINDOW, FRAMES), 0)
    skipped = jnp.where(iota((WINDOW, FRAMES), 1) >= SPAN, SPAN, 0)
    allowed = jnp.logical_and(s >= skipped, s < skipped + (WINDOW - SPAN))
    allowed = jnp.logical_and(allowed, s >= first_ref[0])
    stats_ref[...] = jnp.zeros((2, 8, FRAMES), F32)
    for h in range(2):
        scores = matmul(keys, one_head(q, h), NT) * SCALE
        scores = jnp.where(allowed, scores, -jnp.inf)
        top = jnp.max(scores, 0, keepdims=True)
        e = jnp.exp(scores - top)
        inverse = 1.0 / jnp.sum(e, 0, keepdims=True)
        p_ref[h] = e * inverse
        stats_ref[h, 0:1, :] = top
        stats_ref[h, 1:2, :] = inverse


def attention_probs(first, q, k2, k1, k0):
    pair = pl.BlockSpec((FRAMES, 2 * HEAD), lambda i, *_: (0, i))
    heads = lambda n: pl.BlockSpec((2, n, FRAMES), lambda i, *_: (i, 0, 0))
    return pl.pallas_call(
        probs_kernel,
        grid_spec=pltpu.PrefetchScalarGridSpec(
            num_scalar_prefetch=1,
            grid=(PAIRS,),
            in_specs=[pair] * 4,
            out_specs=[heads(WINDOW), heads(8)],
        ),
        out_shape=(
            jax.ShapeDtypeStruct((HEADS, WINDOW, FRAMES), F32),
            jax.ShapeDtypeStruct((HEADS, 8, FRAMES), F32),
        ),
        name="attention_probs",
    )(first, q, k2, k1, k0)


def later_probs_kernel(q1_ref, q2_ref, stats1_ref, stats2_ref, k_ref, p_ref):
    k = k_ref[...]
    shape = (FRAMES, FRAMES)
    allowed = iota(shape, 0) >= jnp.where(iota(shape, 1) >= SPAN, SPAN, 0)
    for n, (q_ref, stats_ref) in enumerate(((q1_ref, stats1_ref), (q2_ref, stats2_ref))):
        q = q_ref[...]
        for h in range(2):
            scores = matmul(k, one_head(q, h), NT) * SCALE
            if n == 1:
                scores = jnp.where(allowed, scores, -jnp.inf)
            p_ref[h, n] = jnp.exp(scores - stats_ref[h, 0:1, :]) * stats_ref[h, 1:2, :]


def later_probs(q1, q2, stats1, stats2, k):
    pair = pl.BlockSpec((FRAMES, 2 * HEAD), lambda i: (0, i))
    stats = pl.BlockSpec((2, 8, FRAMES), lambda i: (i, 0, 0))
    return pl.pallas_call(
        later_probs_kernel,
        grid=(PAIRS,),
        in_specs=[pair, pair, stats, stats, pair],
        out_specs=pl.BlockSpec((2, 2, FRAMES, FRAMES), lambda i: (i, 0, 0, 0)),
        out_shape=jax.ShapeDtypeStruct((HEADS, 2, FRAMES, FRAMES), F32),
        name="later_probs",
    )(q1, q2, stats1, stats2, k)


def stream_grad_kernel(rows_ref, block_ref, stream_ref, gain_ref, o_ref, main, total):
    j = pl.program_id(0)
    upright = block_ref[FRAMES:, 0:FRAMES].astype(F32).T
    places = [upright[:, k : k + 1] * CAP + upright[:, 2 + k : 3 + k] for k in range(2)]
    row = iota((FRAMES, PACK * EP), 1)
    lane = row & 15
    base = (row >> 6) * CAP

    @pl.when(j == 0)
    def _():
        main[...] = picked(base + lane, lane < CAP, places)
        total[3] = jnp.zeros((FRAMES, 256), F32)

    rows = rows_ref[...]
    last = picked(base + (lane - CAP) + 4 * j, lane >= CAP, places)
    both = matmul(jnp.concatenate([main[...], last], 0), rows)
    total[j] = both[:FRAMES]
    total[3] += both[FRAMES:]

    @pl.when(j == 2)
    def _():
        dnormed = jnp.concatenate([total[c] for c in range(4)], 1)
        s = stream_ref[...].astype(F32)
        inverse_rms = lax.rsqrt(jnp.mean(s * s, -1, keepdims=True) + EPSILON)
        scaled = s * inverse_rms
        weighted = dnormed * gain_ref[...]
        mean = jnp.mean(weighted * scaled, -1, keepdims=True)
        grad = block_ref[0:FRAMES, :].astype(F32)
        o_ref[...] = (grad + inverse_rms * (weighted - scaled * mean)).astype(BF16)


def stream_gradient(returned, block, stream, gain):
    whole = lambda n: pl.BlockSpec((n, D), lambda j: (0, 0))
    return pl.pallas_call(
        stream_grad_kernel,
        grid=(3,),
        in_specs=[
            pl.BlockSpec((PACK * EP, 256), lambda j: (0, j)),
            whole(FRAMES + EXTRA),
            whole(FRAMES),
            whole(1),
        ],
        out_specs=whole(FRAMES),
        out_shape=jax.ShapeDtypeStruct((FRAMES, D), BF16),
        scratch_shapes=[pltpu.VMEM((FRAMES, PACK * EP), BF16), pltpu.VMEM((4, FRAMES, 256), F32)],
        name="stream_gradient",
    )(returned, block, stream, gain)


def own_grads_kernel(
    p_ref, o_ref, q_ref, k2_ref, k1_ref, k0_ref, v2_ref, v1_ref, v0_ref, dq_ref, dk_ref, dv_ref, delta_ref
):
    o, q = o_ref[...], q_ref[...]
    keys = jnp.concatenate([k2_ref[...], k1_ref[...], k0_ref[...]], 0)
    values = jnp.concatenate([v2_ref[...], v1_ref[...], v0_ref[...]], 0)
    delta_ref[...] = jnp.zeros((2, 8, FRAMES), F32)
    dq = dk = dv = 0.0
    for h in range(2):
        o_h, q_h, k_h = one_head(o, h), one_head(q, h), one_head(keys, h)
        probs = p_ref[h]
        rounded = probs.astype(BF16)
        dprob = matmul(values, o_h, NT)
        delta = jnp.sum(rounded.astype(F32) * dprob, 0, keepdims=True)
        delta_ref[h, 0:1, :] = delta
        dscore = (probs * (dprob - delta)).astype(BF16)
        dq += matmul(dscore, k_h, TN)
        dk += matmul(dscore[LEFT:], q_h)
        dv += matmul(rounded[LEFT:], o_h)
    dq_ref[...] = (dq * SCALE).astype(BF16)
    dk_ref[...] = dk
    dv_ref[...] = dv


def own_grads(probs, o, q, ks, vs):
    pair = pl.BlockSpec((FRAMES, 2 * HEAD), lambda i: (0, i))
    heads = lambda n: pl.BlockSpec((2, n, FRAMES), lambda i: (i, 0, 0))
    out = lambda t: jax.ShapeDtypeStruct((FRAMES, D), t)
    return pl.pallas_call(
        own_grads_kernel,
        grid=(PAIRS,),
        in_specs=[heads(WINDOW)] + [pair] * 8,
        out_specs=[pair, pair, pair, heads(8)],
        out_shape=(out(BF16), out(F32), out(F32), jax.ShapeDtypeStruct((HEADS, 8, FRAMES), F32)),
        name="own_grads",
    )(probs, o, q, *ks, *vs)


def later_grads_kernel(
    p_ref, o1_ref, o2_ref, q1_ref, q2_ref, delta1_ref, delta2_ref, v_ref, dk_ref, dv_ref, keys_ref, values_ref
):
    v = v_ref[...]
    dk, dv = dk_ref[...], dv_ref[...]
    sources = ((o1_ref, q1_ref, delta1_ref), (o2_ref, q2_ref, delta2_ref))
    for n, (o_ref, q_ref, delta_ref) in enumerate(sources):
        o, q = o_ref[...], q_ref[...]
        for h in range(2):
            o_h, q_h = one_head(o, h), one_head(q, h)
            probs = p_ref[h, n]
            dprob = matmul(v, o_h, NT)
            dscore = (probs * (dprob - delta_ref[h, 0:1, :])).astype(BF16)
            dk += matmul(dscore, q_h)
            dv += matmul(probs.astype(BF16), o_h)
    keys_ref[...] = (dk * SCALE).astype(BF16)
    values_ref[...] = dv.astype(BF16)


def later_grads(probs, os, qs, deltas, v, dk, dv):
    pair = pl.BlockSpec((FRAMES, 2 * HEAD), lambda i: (0, i))
    stats = pl.BlockSpec((2, 8, FRAMES), lambda i: (i, 0, 0))
    return pl.pallas_call(
        later_grads_kernel,
        grid=(PAIRS,),
        in_specs=[pl.BlockSpec((2, 2, FRAMES, FRAMES), lambda i: (i, 0, 0, 0))]
        + [pair] * 4
        + [stats] * 2
        + [pair] * 3,
        out_specs=[pair, pair],
        out_shape=(jax.ShapeDtypeStruct((FRAMES, D), BF16),) * 2,
        name="later_grads",
    )(probs, *os, *qs, *deltas, v, dk, dv)


def turned(x, distance):
    return lax.ppermute(x, "ep", [(i, (i + distance) % EP) for i in range(EP)])


def shifted(x, distance):
    count = lax.axis_size("tm") * lax.axis_size("ep")
    route = [(i, i + distance) for i in range(count) if 0 <= i + distance < count]
    return lax.ppermute(x, ("tm", "ep"), route)


def exchanged(x, axes):
    return lax.all_to_all(x, axes, split_axis=0, concat_axis=0, tiled=True)


def body(
    queries, keys, values, stream, grad_out, norm_gain, gate_probs, routes, w_gate, w_up, w_down
):
    gain = norm_gain.reshape(1, D)
    weight_gate, weight_up, weight_down = w_gate[0], w_up[0], w_down[0]
    row, column = lax.axis_index("tm"), lax.axis_index("ep")
    order = jnp.stack([column, (column + 3) % EP, (column + 1) % EP, (column + 2) % EP]).astype(jnp.int32)
    packed, block = dispatch_x(stream, grad_out, gain, routes.T, gate_probs.T)
    own = exchanged(packed.reshape(EXPERTS, 16, 768), "tm").reshape(PACK, 768)
    blocks = (block, turned(block, 1), turned(block, -1), turned(block, 2))
    left, right = turned(own, 1), turned(own, -1)
    half = PACK // 2
    top, bottom = turned(left[:half], 1), turned(right[half:], -1)
    sent_g = dispatch_g(blocks).reshape(EXPERTS, EP * 16, 768)
    packed_g = exchanged(sent_g, "tm").reshape(EXPERTS, EP, 16, 768)
    filled = ()
    for q, parts in enumerate(((own,), (left,), (right,), (top, bottom))):
        filled = expert_forward(q, parts, weight_gate, weight_up, filled)
    x_rows, a, s, acted = filled
    g_rows, dgate, dup, dx = expert_backward(order, packed_g, a, s, weight_gate, weight_up, weight_down)
    returned = exchanged(dx.reshape(EXPERTS * EP, 16, 768), ("tm", "ep")).reshape(PACK * EP, 768)
    gate_grad = jnp.dot(x_rows.T, dgate, preferred_element_type=F32)
    up_grad = jnp.dot(x_rows.T, dup, preferred_element_type=F32)
    down_grad = jnp.dot(acted.T, g_rows, preferred_element_type=F32)
    ks = (shifted(keys, 2), shifted(keys, 1), keys)
    vs = (shifted(values, 2), shifted(values, 1), values)
    qs = (shifted(queries, -1), shifted(queries, -2))
    position = row * lax.axis_size("ep") + column
    first = jnp.maximum(LEFT - position * FRAMES, 0).astype(jnp.int32).reshape(1)
    probs, stats = attention_probs(first, queries, *ks)
    later = later_probs(*qs, shifted(stats, -1), shifted(stats, -2), keys)
    stream_grad = stream_gradient(returned, block, stream, gain)
    later_o = (shifted(stream_grad, -1), shifted(stream_grad, -2))
    grad_q, own_k, own_v, delta = own_grads(probs, stream_grad, queries, ks, vs)
    deltas = (shifted(delta, -1), shifted(delta, -2))
    grad_k, grad_v = later_grads(later, later_o, qs, deltas, values, own_k, own_v)
    return (
        grad_q,
        grad_k,
        grad_v,
        stream_grad,
        gate_grad[None],
        up_grad[None],
        down_grad[None],
    )


def solution(mesh):
    frames = P(("tm", "ep"), None)
    columns, rows = P("tm", None, "ep"), P("tm", "ep", None)
    return jax.shard_map(
        body,
        mesh=mesh,
        in_specs=(frames,) * 5 + (P(), frames, frames, columns, columns, rows),
        out_specs=(frames,) * 4 + (columns, columns, rows),
        check_vma=False,
    )
```

time: 234 us -> 263 us (1.12)
  Pallas kernels: 60.8 us -> 88.1 us
  starting transfers between devices: 65.6 us -> 74.5 us
  matrix products: 23.6 us -> 18.9 us
  waiting for transfers between devices: 73 us -> 69.8 us
    pallas_call x7 -> x12, Pallas kernels: 60.8 us -> 88.1 us  [the longest x4 26.3 us: expert_forward(): pl.pallas_call(lambda *refs: forward_kernel(n, *refs), grid=(D // N_BLOCK...]
    ppermute x6 -> x12, starting transfers between devices: 20.6 us -> 39.6 us  [shifted(): return lax.ppermute(x, ('tm', 'ep'), route)]
    ppermute x6 -> x12, waiting for transfers between devices: 21.3 us -> 39.3 us  [shifted(): return lax.ppermute(x, ('tm', 'ep'), route)]
    ppermute x13 -> x7, waiting for transfers between devices: 43.7 us -> 30.5 us  [turned(): return lax.ppermute(x, 'ep', [(i, (i + distance) % EP) for i in range(EP)])]
    ppermute x13 -> x7, starting transfers between devices: 17.8 us -> 5.75 us  [turned(): return lax.ppermute(x, 'ep', [(i, (i + distance) % EP) for i in range(EP)])]
    all_to_all x3, waiting for transfers between devices: 8 us -> 0.01 us  [exchanged(): return lax.all_to_all(x, axes, split_axis=0, concat_axis=0, tiled=True)]
    dot_general x1, matrix products: 8.33 us -> 4.99 us  [body(): gate_grad = jnp.dot(x_rows.T, dgate, preferred_element_type=F32)]
    unnamed x38 -> x36, local copies, waits for them, and re-layouts: 8.13 us -> 6.83 us
  transfers between devices with their start and end apart: 22 -> 22, of which waited for: 11 -> 7; matrix products, arithmetic and copies ran while one was open for 10% -> 8% of each run, Pallas kernels for 14% -> 19%
where the time goes in v1:
time: 263 us; the launch traced here: 261 us
  Pallas kernels  88.1 us (33%)
  starting transfers between devices  74.5 us (28%)
  waiting for transfers between devices  69.8 us (27%)
  matrix products  18.9 us (7%)
  local copies, waits for them, and re-layouts  7.63 us (3%)
    ppermute x12, starting transfers between devices, shifted(): return lax.ppermute(x, ('tm', 'ep'), route)  39.6 us
    ppermute x12, waiting for transfers between devices, shifted(): return lax.ppermute(x, ('tm', 'ep'), route)  39.3 us
    ppermute x7, waiting for transfers between devices, turned(): return lax.ppermute(x, 'ep', [(i, (i + distance) % EP) for i in range(EP)])  30.5 us
    all_to_all x3, starting transfers between devices, exchanged(): return lax.all_to_all(x, axes, split_axis=0, concat_axis=0, tiled=True)  29.2 us
    pallas_call x4, Pallas kernels, expert_forward(): pl.pallas_call(lambda *refs: forward_kernel(n, *refs), grid=(D // N_BLOCK...  26.3 us
    pallas_call x1, Pallas kernels, expert_backward(): pl.pallas_call(backward_kernel, grid_spec=pltpu.PrefetchScalarGridSpec(nu...  20.4 us
    pallas_call x1, Pallas kernels, own_grads(): pl.pallas_call(own_grads_kernel, grid=(PAIRS,), in_specs=[heads(WINDOW)]...  8.12 us
    pallas_call x1, Pallas kernels, later_grads(): pl.pallas_call(later_grads_kernel, grid=(PAIRS,), in_specs=[pl.BlockSpec(...  7.3 us
  transfers between devices with their start and end apart: 22, of which 7 were waited for; matrix products, arithmetic and copies ran while one was open for 8% of the time, Pallas kernels for 19%

profile of v1, /device:TPU:31, one launch (start us, length us, event | category | flops | bytes accessed | tf_op | source)
XLA Modules:
  0.0 260.7 jit_solution(17272769962968728217)
XLA Ops:
  0.6 2.7 %dispatch_x.1 = (bf16[512,768]{1,0:T(8,128)(2,1)}, bf16[144,1024]{1,0:T(8,128)(2,1)}) custom-call(bf16[128,1024]{1,0:T(8,128)(2,1)} %stream_ref.3, bf16[128,1024]{1,0:T(8,128)(2,1)} %grad_ref.1, f32[1,1024]{1,0:T(1,128)} %bitcast.47, s32[2,128]{1,0:T(2,128)} %bitcast.49, f32[2,128]{1,0:T(2,128)} %bitcast.50), custom_call_target="tpu_custom_call" | custom-call | tf_op jit(solution)/shard_map/dispatch_x/pallas_call | solution.py:88
  3.3 8.6 %all-to-all-start.1 = ((bf16[32,16,768]{2,1,0:T(8,128)(2,1)}), bf16[32,16,768]{2,1,0:T(8,128)(2,1)S(1)}, u32[]{:S(2)}, u32[]{:S(2)}) async-start(bf16[32,16,768]{2,1,0:T(8,128)(2,1)} %bitcast.46), calls=%async_computation.1 | async-start | bytes 1572864 | tf_op jit(solution)/shard_map/all_to_all | solution.py:467
  14.6 5.8 %collective-permute-done.2.refs_1_ = bf16[144,1024]{1,0:T(8,128)(2,1)S(1)} collective-permute-done((bf16[144,1024]{1,0:T(8,128)(2,1)}, bf16[144,1024]{1,0:T(8,128)(2,1)S(1)}, u32[]{:S(2)}, u32[]{:S(2)}) %collective-permute-start.2) | collective-permute-done | bytes 294944 | tf_op jit(solution)/shard_map/ppermute | solution.py:457
  21.8 5.8 %collective-permute-done.4.refs_3_ = bf16[144,1024]{1,0:T(8,128)(2,1)S(1)} collective-permute-done((bf16[144,1024]{1,0:T(8,128)(2,1)}, bf16[144,1024]{1,0:T(8,128)(2,1)S(1)}, u32[]{:S(2)}, u32[]{:S(2)}) %collective-permute-start.4) | collective-permute-done | bytes 294944 | tf_op jit(solution)/shard_map/ppermute | solution.py:457
  28.3 5.8 %dispatch_g.1 = bf16[32,4,16,768]{3,2,1,0:T(8,128)(2,1)} custom-call(bf16[144,1024]{1,0:T(8,128)(2,1)} %get-tuple-element.38.refs_0_.block_ref, bf16[144,1024]{1,0:T(8,128)(2,1)} %copy-done.8, bf16[144,1024]{1,0:T(8,128)(2,1)} %copy-done.9, bf16[144,1024]{1,0:T(8,128)(2,1)} %copy-done.10), custom_call_target="tpu_custom_call" | custom-call | tf_op jit(solution)/shard_map/dispatch_g/pallas_call | solution.py:132
  35.0 9.5 %all-to-all-start = ((bf16[32,64,768]{2,1,0:T(8,128)(2,1)}), bf16[32,64,768]{2,1,0:T(8,128)(2,1)S(1)}, u32[]{:S(2)}, u32[]{:S(2)}) async-start(bf16[32,64,768]{2,1,0:T(8,128)(2,1)} %bitcast.40), calls=%async_computation | async-start | bytes 6291456 | tf_op jit(solution)/shard_map/all_to_all | solution.py:467
  46.0 17.4 %collective-permute-done.5.refs_0_ = bf16[512,768]{1,0:T(8,128)(2,1)S(1)} collective-permute-done((bf16[512,768]{1,0:T(8,128)(2,1)}, bf16[512,768]{1,0:T(8,128)(2,1)S(1)}, u32[]{:S(2)}, u32[]{:S(2)}) %collective-permute-start.5) | collective-permute-done | bytes 786464 | tf_op jit(solution)/shard_map/ppermute | solution.py:457
  67.3 6.6 %expert_forward.4 = (bf16[1536,1024]{1,0:T(8,128)(2,1)}, f32[1536,1024]{1,0:T(8,128)}, f32[1536,1024]{1,0:T(8,128)}, bf16[1536,1024]{1,0:T(8,128)(2,1)}) custom-call(bf16[512,768]{1,0:T(8,128)(2,1)} %bitcast.43, bf16[1024,1024]{1,0:T(8,128)(2,1)} %bitcast.29, bf16[1024,1024]{1,0:T(8,128)(2,1)} %bitcast.34), custom_call_target="tpu_custom_call" | custom-call | tf_op jit(solution)/shard_map/expert_forward/pallas_call | solution.py:196
  73.9 6.6 %expert_forward.5 = (bf16[1536,1024]{1,0:T(8,128)(2,1)}, f32[1536,1024]{1,0:T(8,128)}, f32[1536,1024]{1,0:T(8,128)}, bf16[1536,1024]{1,0:T(8,128)(2,1)}) custom-call(bf16[512,768]{1,0:T(8,128)(2,1)} %copy-done.6, bf16[1024,1024]{1,0:T(8,128)(2,1)} %bitcast.30, ...), custom_call_target="tpu_custom_call", output_to_operand_aliasing={{0}: (3, {}), {1}: (4, {}), {2}: (5, {}), {3}: (6, {})} | custom-call | tf_op jit(solution)/shard_map/expert_forward/pallas_call | solution.py:196
  80.5 6.6 %expert_forward.6 = (bf16[1536,1024]{1,0:T(8,128)(2,1)}, f32[1536,1024]{1,0:T(8,128)}, f32[1536,1024]{1,0:T(8,128)}, bf16[1536,1024]{1,0:T(8,128)(2,1)}) custom-call(bf16[512,768]{1,0:T(8,128)(2,1)} %copy-done.5, bf16[1024,1024]{1,0:T(8,128)(2,1)} %bitcast.31, ...), custom_call_target="tpu_custom_call", output_to_operand_aliasing={{0}: (3, {}), {1}: (4, {}), {2}: (5, {}), {3}: (6, {})} | custom-call | tf_op jit(solution)/shard_map/expert_forward/pallas_call | solution.py:196
  87.1 6.5 %expert_forward.7 = (bf16[1536,1024]{1,0:T(8,128)(2,1)}, f32[1536,1024]{1,0:T(8,128)}, f32[1536,1024]{1,0:T(8,128)}, bf16[1536,1024]{1,0:T(8,128)(2,1)}) custom-call(bf16[256,768]{1,0:T(8,128)(2,1)} %collective-permute-done.6.refs_0_, ...), custom_call_target="tpu_custom_call", output_to_operand_aliasing={{0}: (4, {}), {1}: (5, {}), {2}: (6, {}), {3}: (7, {})} | custom-call | tf_op jit(solution)/shard_map/expert_forward/pallas_call | solution.py:196
  95.4 20.4 %expert_backward.1 = (bf16[1536,1024]{1,0:T(8,128)(2,1)}, bf16[1536,1024]{1,0:T(8,128)(2,1)}, bf16[1536,1024]{1,0:T(8,128)(2,1)}, bf16[32,4,16,768]{3,2,1,0:T(8,128)(2,1)}) custom-call(s32[4]{0:T(128)} %pad_add_fusion.order_ref, bf16[32,4,16,768]{3,2,1,0:T(8,128)(2,1)} %bitcast.39, f32[1536,1024]{1,0:T(8,128)} %get-tuple-element.52.a_ref, ...), custom_call_target="tpu_custom_call" | custom-call | tf_op jit(solution)/shard_map/expert_backward/pallas_call | solution.py:235
  115.8 11.1 %all-to-all-start.2 = ((bf16[128,16,768]{2,1,0:T(8,128)(2,1)}), bf16[128,16,768]{2,1,0:T(8,128)(2,1)}, u32[]{:S(2)}, u32[]{:S(2)}) async-start(bf16[128,16,768]{2,1,0:T(8,128)(2,1)} %bitcast.44), calls=%async_computation.2 | async-start | bytes 6291456 | tf_op jit(solution)/shard_map/all_to_all | solution.py:467
  126.9 4.6 %collective-permute-start = (bf16[128,1024]{1,0:T(8,128)(2,1)S(1)}, bf16[128,1024]{1,0:T(8,128)(2,1)}, u32[]{:S(2)}, u32[]{:S(2)}) collective-permute-start(bf16[128,1024]{1,0:T(8,128)(2,1)S(1)} %copy-done.4), channel_id=1, source_target_pairs={{0,2},{1,3},{2,4},{3,5},{4,6},{5,7},{6,8},{7,9},{8,10},{9,11},{10,... | collective-permute-start | bytes 786440 | tf_op jit(solution)/shard_map/ppermute | solution.py:463
  131.5 4.0 %collective-permute-start.1 = (bf16[128,1024]{1,0:T(8,128)(2,1)S(1)}, bf16[128,1024]{1,0:T(8,128)(2,1)}, u32[]{:S(2)}, u32[]{:S(2)}) collective-permute-start(bf16[128,1024]{1,0:T(8,128)(2,1)S(1)} %copy-done.4), channel_id=1, source_target_pairs={{0,1},{1,2},{2,3},{3,4},{4,5},{5,6},{6,7},{7,8},{8,9},{9,10},{10,1... | collective-permute-start | bytes 786440 | tf_op jit(solution)/shard_map/ppermute | solution.py:463
  139.4 27.7 %collective-permute-done.k2_ref = bf16[128,1024]{1,0:T(8,128)(2,1)} collective-permute-done((bf16[128,1024]{1,0:T(8,128)(2,1)S(1)}, bf16[128,1024]{1,0:T(8,128)(2,1)}, u32[]{:S(2)}, u32[]{:S(2)}) %collective-permute-start) | collective-permute-done | bytes 262176 | tf_op jit(solution)/shard_map/ppermute | solution.py:463
  167.1 5.0 %collective-permute-done.1.k1_ref = bf16[128,1024]{1,0:T(8,128)(2,1)} collective-permute-done((bf16[128,1024]{1,0:T(8,128)(2,1)S(1)}, bf16[128,1024]{1,0:T(8,128)(2,1)}, u32[]{:S(2)}, u32[]{:S(2)}) %collective-permute-start.1) | collective-permute-done | bytes 262176 | tf_op jit(solution)/shard_map/ppermute | solution.py:463
  172.1 6.5 %attention_probs.1 = (f32[16,384,128]{2,1,0:T(8,128)}, f32[16,8,128]{2,1,0:T(8,128)}) custom-call(s32[1]{0:T(128)} %bitcast.first_ref, bf16[128,1024]{1,0:T(8,128)(2,1)} %q_ref.3, bf16[128,1024]{1,0:T(8,128)(2,1)} %collective-permute-done.k2_ref, bf16[128,1024]{1,0:T(8,128)(2,1)} %collective-permute-done.1.k1_ref, bf16[128,1024]{1,0:T(8,128)(2,1)} %k_ref.1), custom_call_target="tpu_custom_call" | custom-call | tf_op jit(solution)/shard_map/attention_probs/pallas_call | solution.py:292
  180.8 5.5 %collective-permute-start.14 = (f32[16,8,128]{2,1,0:T(8,128)}, f32[16,8,128]{2,1,0:T(8,128)S(1)}, u32[]{:S(2)}, u32[]{:S(2)}) collective-permute-start(f32[16,8,128]{2,1,0:T(8,128)} %get-tuple-element.56), channel_id=1, source_target_pairs={{2,0},{3,1},{4,2},{5,3},{6,4},{7,5},{8,6},{9,7},{10,8},{11,9},{12,... | collective-permute-start | bytes 196616 | tf_op jit(solution)/shard_map/ppermute | solution.py:463
  186.3 4.3 %collective-permute-start.10 = (bf16[128,1024]{1,0:T(8,128)(2,1)}, bf16[128,1024]{1,0:T(8,128)(2,1)}, u32[]{:S(2)}, u32[]{:S(2)}) collective-permute-start(bf16[128,1024]{1,0:T(8,128)(2,1)} %v_ref.1), channel_id=1, source_target_pairs={{0,1},{1,2},{2,3},{3,4},{4,5},{5,6},{6,7},{7,8},{8,9},{9,10},{10,1... | collective-permute-start | bytes 786440 | tf_op jit(solution)/shard_map/ppermute | solution.py:463
  190.6 4.8 %collective-permute-start.9 = (bf16[128,1024]{1,0:T(8,128)(2,1)}, bf16[128,1024]{1,0:T(8,128)(2,1)}, u32[]{:S(2)}, u32[]{:S(2)}) collective-permute-start(bf16[128,1024]{1,0:T(8,128)(2,1)} %v_ref.1), channel_id=1, source_target_pairs={{0,2},{1,3},{2,4},{3,5},{4,6},{5,7},{6,8},{7,9},{8,10},{9,11},{10,... | collective-permute-start | bytes 786440 | tf_op jit(solution)/shard_map/ppermute | solution.py:463
  196.7 5.9 %later_probs.1.p_ref = f32[16,2,128,128]{3,2,1,0:T(8,128)} custom-call(bf16[128,1024]{1,0:T(8,128)(2,1)} %collective-permute-done.11.q1_ref, bf16[128,1024]{1,0:T(8,128)(2,1)} %collective-permute-done.12.q2_ref, f32[16,8,128]{2,1,0:T(8,128)} %copy-done.15, f32[16,8,128]{2,1,0:T(8,128)} %copy-done.16, bf16[128,1024]{1,0:T(8,128)(2,1)} %k_ref.1), custom_call_target="tpu_custom_call" | custom-call | tf_op jit(solution)/shard_map/later_probs/pallas_call | solution.py:324
  202.5 7.0 %convolution_bitcast_fusion.1 = f32[1,1024,1024]{2,1,0:T(8,128)} fusion(bf16[1536,1024]{1,0:T(8,128)(2,1)S(1)} %copy-done, bf16[1536,1024]{1,0:T(8,128)(2,1)} %get-tuple-element.64), kind=kOutput, calls=%fused_computation.1 | convolution fusion | flops 3221225472 | bytes 10485760 | tf_op jit(solution)/shard_map/dot_general | solution.py:492
  209.6 5.0 %convolution_bitcast_fusion.2 = f32[1,1024,1024]{2,1,0:T(8,128)} fusion(bf16[1536,1024]{1,0:T(8,128)(2,1)S(1)} %copy-done, bf16[1536,1024]{1,0:T(8,128)(2,1)S(1)} %copy-done.17), kind=kOutput, calls=%fused_computation.2 | convolution fusion | flops 3221225472 | bytes 10485760 | tf_op jit(solution)/shard_map/dot_general | solution.py:491
  214.6 5.1 %stream_gradient.1.o_ref = bf16[128,1024]{1,0:T(8,128)(2,1)} custom-call(bf16[2048,768]{1,0:T(8,128)(2,1)} %bitcast.16.rows_ref, bf16[144,1024]{1,0:T(8,128)(2,1)} %get-tuple-element.38.refs_0_.block_ref, bf16[128,1024]{1,0:T(8,128)(2,1)} %stream_ref.3, f32[1,1024]{1,0:T(1,128)} %bitcast.48), custom_call_target="tpu_custom_call" | custom-call | tf_op jit(solution)/shard_map/stream_gradient/pallas_call | solution.py:367
  219.7 8.1 %own_grads.1 = (bf16[128,1024]{1,0:T(8,128)(2,1)}, f32[128,1024]{1,0:T(8,128)}, f32[128,1024]{1,0:T(8,128)}, f32[16,8,128]{2,1,0:T(8,128)}) custom-call(f32[16,384,128]{2,1,0:T(8,128)} %get-tuple-element.37.p_ref, bf16[128,1024]{1,0:T(8,128)(2,1)} %stream_gradient.1.o_ref, bf16[128,1024]{1,0:T(8,128)(2,1)} %q_ref.3, ...), custom_call_target="tpu_custom_call" | custom-call | tf_op jit(solution)/shard_map/own_grads/pallas_call | solution.py:411
  229.8 2.2 collective-permute-start.18
  232.0 2.7 %collective-permute-start.15 = (bf16[128,1024]{1,0:T(8,128)(2,1)S(1)}, bf16[128,1024]{1,0:T(8,128)(2,1)S(1)}, u32[]{:S(2)}, u32[]{:S(2)}) collective-permute-start(bf16[128,1024]{1,0:T(8,128)(2,1)S(1)} %copy-done.7), channel_id=1, source_target_pairs={{1,0},{2,1},{3,2},{4,3},{5,4},{6,5},{7,6},{8,7},{9,8},{10,9},{11,1... | collective-permute-start | bytes 786440 | tf_op jit(solution)/shard_map/ppermute | solution.py:463
  234.7 3.6 %collective-permute-start.16 = (bf16[128,1024]{1,0:T(8,128)(2,1)S(1)}, bf16[128,1024]{1,0:T(8,128)(2,1)S(1)}, u32[]{:S(2)}, u32[]{:S(2)}) collective-permute-start(bf16[128,1024]{1,0:T(8,128)(2,1)S(1)} %copy-done.7), channel_id=1, source_target_pairs={{2,0},{3,1},{4,2},{5,3},{6,4},{7,5},{8,6},{9,7},{10,8},{11,9},{12,... | collective-permute-start | bytes 786440 | tf_op jit(solution)/shard_map/ppermute | solution.py:463
  238.4 6.9 %convolution_bitcast_fusion = f32[1,1024,1024]{2,1,0:T(8,128)} fusion(bf16[1536,1024]{1,0:T(8,128)(2,1)S(1)} %copy-done.1, bf16[1536,1024]{1,0:T(8,128)(2,1)} %get-tuple-element.66), kind=kOutput, calls=%fused_computation | convolution fusion | flops 3221225472 | bytes 10485760 | tf_op jit(solution)/shard_map/dot_general | solution.py:493
  245.3 6.6 %collective-permute-done.15.o1_ref = bf16[128,1024]{1,0:T(8,128)(2,1)S(1)} collective-permute-done((bf16[128,1024]{1,0:T(8,128)(2,1)S(1)}, bf16[128,1024]{1,0:T(8,128)(2,1)S(1)}, u32[]{:S(2)}, u32[]{:S(2)}) %collective-permute-start.15) | collective-permute-done | bytes 262176 | tf_op jit(solution)/shard_map/ppermute | solution.py:463
  253.3 7.3 %later_grads.1 = (bf16[128,1024]{1,0:T(8,128)(2,1)}, bf16[128,1024]{1,0:T(8,128)(2,1)}) custom-call(f32[16,2,128,128]{3,2,1,0:T(8,128)} %later_probs.1.p_ref, bf16[128,1024]{1,0:T(8,128)(2,1)} %copy-done.11, bf16[128,1024]{1,0:T(8,128)(2,1)} %copy-done.12, bf16[128,1024]{1,0:T(8,128)(2,1)} %collective-permute-done.11.q1_ref, ...), custom_call_target="tpu_custom_call" | custom-call | tf_op jit(solution)/shard_map/later_grads/pallas_call | solution.py:443
  (66 shorter events, 23.4 us)
Async XLA Ops:
  3.3 30.8 %all-to-all-start.1 = ((bf16[32,16,768]{2,1,0:T(8,128)(2,1)}), bf16[32,16,768]{2,1,0:T(8,128)(2,1)S(1)}, u32[]{:S(2)}, u32[]{:S(2)}) async-start(bf16[32,16,768]{2,1,0:T(8,128)(2,1)} %bitcast.46), calls=%async_computation.1 | async-start | bytes 1572864 | tf_op jit(solution)/shard_map/all_to_all | solution.py:467
  11.9 8.5 %collective-permute-start.2 = (bf16[144,1024]{1,0:T(8,128)(2,1)}, bf16[144,1024]{1,0:T(8,128)(2,1)S(1)}, u32[]{:S(2)}, u32[]{:S(2)}) collective-permute-start(bf16[144,1024]{1,0:T(8,128)(2,1)} %get-tuple-element.38.refs_0_.block_ref), channel_id=1, source_target_pairs={{0,1},{1,2},{2,3},{3,0},{4,5},{5,6},{6,7},{7,4},{8,9},{9,10},{10,1... | collective-permute-start | bytes 884744 | tf_op jit(solution)/shard_map/ppermute | solution.py:457
  12.2 9.6 %collective-permute-start.3 = (bf16[144,1024]{1,0:T(8,128)(2,1)}, bf16[144,1024]{1,0:T(8,128)(2,1)S(1)}, u32[]{:S(2)}, u32[]{:S(2)}) collective-permute-start(bf16[144,1024]{1,0:T(8,128)(2,1)} %get-tuple-element.38.refs_0_.block_ref), channel_id=1, source_target_pairs={{0,3},{1,0},{2,1},{3,2},{4,7},{5,4},{6,5},{7,6},{8,11},{9,8},{10,9... | collective-permute-start | bytes 884744 | tf_op jit(solution)/shard_map/ppermute | solution.py:457
  13.5 14.1 %collective-permute-start.4 = (bf16[144,1024]{1,0:T(8,128)(2,1)}, bf16[144,1024]{1,0:T(8,128)(2,1)S(1)}, u32[]{:S(2)}, u32[]{:S(2)}) collective-permute-start(bf16[144,1024]{1,0:T(8,128)(2,1)} %get-tuple-element.38.refs_0_.block_ref), channel_id=1, source_target_pairs={{0,2},{1,3},{2,0},{3,1},{4,6},{5,7},{6,4},{7,5},{8,10},{9,11},{10,... | collective-permute-start | bytes 884744 | tf_op jit(solution)/shard_map/ppermute | solution.py:457
  20.4 7.2 %copy-start.8 = (bf16[144,1024]{1,0:T(8,128)(2,1)}, bf16[144,1024]{1,0:T(8,128)(2,1)S(1)}, u32[]{:S(2)}) copy-start(bf16[144,1024]{1,0:T(8,128)(2,1)S(1)} %collective-permute-done.2.refs_1_) | copy-start | bytes 884740
  21.8 5.8 %copy-start.9 = (bf16[144,1024]{1,0:T(8,128)(2,1)}, bf16[144,1024]{1,0:T(8,128)(2,1)S(1)}, u32[]{:S(2)}) copy-start(bf16[144,1024]{1,0:T(8,128)(2,1)S(1)} %collective-permute-done.3.refs_2_) | copy-start | bytes 884740
  35.0 58.7 %all-to-all-start = ((bf16[32,64,768]{2,1,0:T(8,128)(2,1)}), bf16[32,64,768]{2,1,0:T(8,128)(2,1)S(1)}, u32[]{:S(2)}, u32[]{:S(2)}) async-start(bf16[32,64,768]{2,1,0:T(8,128)(2,1)} %bitcast.40), calls=%async_computation | async-start | bytes 6291456 | tf_op jit(solution)/shard_map/all_to_all | solution.py:467
  44.4 19.0 %collective-permute-start.5 = (bf16[512,768]{1,0:T(8,128)(2,1)}, bf16[512,768]{1,0:T(8,128)(2,1)S(1)}, u32[]{:S(2)}, u32[]{:S(2)}) collective-permute-start(bf16[512,768]{1,0:T(8,128)(2,1)} %bitcast.41), channel_id=1, source_target_pairs={{0,1},{1,2},{2,3},{3,0},{4,5},{5,6},{6,7},{7,4},{8,9},{9,10},{10,1... | collective-permute-start | bytes 2359304 | tf_op jit(solution)/shard_map/ppermute | solution.py:457
  44.8 20.2 %collective-permute-start.7 = (bf16[512,768]{1,0:T(8,128)(2,1)}, bf16[512,768]{1,0:T(8,128)(2,1)S(1)}, u32[]{:S(2)}, u32[]{:S(2)}) collective-permute-start(bf16[512,768]{1,0:T(8,128)(2,1)} %bitcast.42), channel_id=1, source_target_pairs={{0,3},{1,0},{2,1},{3,2},{4,7},{5,4},{6,5},{7,6},{8,11},{9,8},{10,9... | collective-permute-start | bytes 2359304 | tf_op jit(solution)/shard_map/ppermute | solution.py:457
  63.4 3.2 %copy-start.6 = (bf16[512,768]{1,0:T(8,128)(2,1)}, bf16[512,768]{1,0:T(8,128)(2,1)S(1)}, u32[]{:S(2)}) copy-start(bf16[512,768]{1,0:T(8,128)(2,1)S(1)} %collective-permute-done.5.refs_0_) | copy-start | bytes 2359300
  63.5 23.7 %collective-permute-start.6 = (bf16[256,768]{1,0:T(8,128)(2,1)S(1)}, bf16[256,768]{1,0:T(8,128)(2,1)}, u32[]{:S(2)}, u32[]{:S(2)}) collective-permute-start(bf16[256,768]{1,0:T(8,128)(2,1)S(1)} %slice.8), channel_id=1, source_target_pairs={{0,1},{1,2},{2,3},{3,0},{4,5},{5,6},{6,7},{7,4},{8,9},{9,10},{10,1... | collective-permute-start | bytes 1179656 | tf_op jit(solution)/shard_map/ppermute | solution.py:457
  66.7 20.5 %collective-permute-start.8 = (bf16[256,768]{1,0:T(8,128)(2,1)}, bf16[256,768]{1,0:T(8,128)(2,1)}, u32[]{:S(2)}, u32[]{:S(2)}) collective-permute-start(bf16[256,768]{1,0:T(8,128)(2,1)} %slice.9), channel_id=1, source_target_pairs={{0,3},{1,0},{2,1},{3,2},{4,7},{5,4},{6,5},{7,6},{8,11},{9,8},{10,9... | collective-permute-start | bytes 1179656 | tf_op jit(solution)/shard_map/ppermute | solution.py:457
  115.8 11.1 %copy-start.4 = (bf16[128,1024]{1,0:T(8,128)(2,1)S(1)}, bf16[128,1024]{1,0:T(8,128)(2,1)}, u32[]{:S(2)}) copy-start(bf16[128,1024]{1,0:T(8,128)(2,1)} %k_ref.1) | copy-start | bytes 786436
  115.8 98.8 %all-to-all-start.2 = ((bf16[128,16,768]{2,1,0:T(8,128)(2,1)}), bf16[128,16,768]{2,1,0:T(8,128)(2,1)}, u32[]{:S(2)}, u32[]{:S(2)}) async-start(bf16[128,16,768]{2,1,0:T(8,128)(2,1)} %bitcast.44), calls=%async_computation.2 | async-start | bytes 6291456 | tf_op jit(solution)/shard_map/all_to_all | solution.py:467
  126.9 75.6 %copy-start = (bf16[1536,1024]{1,0:T(8,128)(2,1)S(1)}, bf16[1536,1024]{1,0:T(8,128)(2,1)}, u32[]{:S(2)}) copy-start(bf16[1536,1024]{1,0:T(8,128)(2,1)} %get-tuple-element.62) | copy-start | bytes 9437188
  126.9 40.2 %collective-permute-start = (bf16[128,1024]{1,0:T(8,128)(2,1)S(1)}, bf16[128,1024]{1,0:T(8,128)(2,1)}, u32[]{:S(2)}, u32[]{:S(2)}) collective-permute-start(bf16[128,1024]{1,0:T(8,128)(2,1)S(1)} %copy-done.4), channel_id=1, source_target_pairs={{0,2},{1,3},{2,4},{3,5},{4,6},{5,7},{6,8},{7,9},{8,10},{9,11},{10,... | collective-permute-start | bytes 786440 | tf_op jit(solution)/shard_map/ppermute | solution.py:463
  131.5 40.6 %collective-permute-start.1 = (bf16[128,1024]{1,0:T(8,128)(2,1)S(1)}, bf16[128,1024]{1,0:T(8,128)(2,1)}, u32[]{:S(2)}, u32[]{:S(2)}) collective-permute-start(bf16[128,1024]{1,0:T(8,128)(2,1)S(1)} %copy-done.4), channel_id=1, source_target_pairs={{0,1},{1,2},{2,3},{3,4},{4,5},{5,6},{6,7},{7,8},{8,9},{9,10},{10,1... | collective-permute-start | bytes 786440 | tf_op jit(solution)/shard_map/ppermute | solution.py:463
  135.5 55.1 %collective-permute-start.11 = (bf16[128,1024]{1,0:T(8,128)(2,1)}, bf16[128,1024]{1,0:T(8,128)(2,1)}, u32[]{:S(2)}, u32[]{:S(2)}) collective-permute-start(bf16[128,1024]{1,0:T(8,128)(2,1)} %q_ref.3), channel_id=1, source_target_pairs={{1,0},{2,1},{3,2},{4,3},{5,4},{6,5},{7,6},{8,7},{9,8},{10,9},{11,1... | collective-permute-start | bytes 786440 | tf_op jit(solution)/shard_map/ppermute | solution.py:463
  137.5 57.9 %collective-permute-start.12 = (bf16[128,1024]{1,0:T(8,128)(2,1)}, bf16[128,1024]{1,0:T(8,128)(2,1)}, u32[]{:S(2)}, u32[]{:S(2)}) collective-permute-start(bf16[128,1024]{1,0:T(8,128)(2,1)} %q_ref.3), channel_id=1, source_target_pairs={{2,0},{3,1},{4,2},{5,3},{6,4},{7,5},{8,6},{9,7},{10,8},{11,9},{12,... | collective-permute-start | bytes 786440 | tf_op jit(solution)/shard_map/ppermute | solution.py:463
  178.6 16.8 %collective-permute-start.13 = (f32[16,8,128]{2,1,0:T(8,128)}, f32[16,8,128]{2,1,0:T(8,128)S(1)}, u32[]{:S(2)}, u32[]{:S(2)}) collective-permute-start(f32[16,8,128]{2,1,0:T(8,128)} %get-tuple-element.56), channel_id=1, source_target_pairs={{1,0},{2,1},{3,2},{4,3},{5,4},{6,5},{7,6},{8,7},{9,8},{10,9},{11,1... | collective-permute-start | bytes 196616 | tf_op jit(solution)/shard_map/ppermute | solution.py:463
  180.8 14.6 %collective-permute-start.14 = (f32[16,8,128]{2,1,0:T(8,128)}, f32[16,8,128]{2,1,0:T(8,128)S(1)}, u32[]{:S(2)}, u32[]{:S(2)}) collective-permute-start(f32[16,8,128]{2,1,0:T(8,128)} %get-tuple-element.56), channel_id=1, source_target_pairs={{2,0},{3,1},{4,2},{5,3},{6,4},{7,5},{8,6},{9,7},{10,8},{11,9},{12,... | collective-permute-start | bytes 196616 | tf_op jit(solution)/shard_map/ppermute | solution.py:463
  186.3 33.4 %collective-permute-start.10 = (bf16[128,1024]{1,0:T(8,128)(2,1)}, bf16[128,1024]{1,0:T(8,128)(2,1)}, u32[]{:S(2)}, u32[]{:S(2)}) collective-permute-start(bf16[128,1024]{1,0:T(8,128)(2,1)} %v_ref.1), channel_id=1, source_target_pairs={{0,1},{1,2},{2,3},{3,4},{4,5},{5,6},{6,7},{7,8},{8,9},{9,10},{10,1... | collective-permute-start | bytes 786440 | tf_op jit(solution)/shard_map/ppermute | solution.py:463
  190.6 29.1 %collective-permute-start.9 = (bf16[128,1024]{1,0:T(8,128)(2,1)}, bf16[128,1024]{1,0:T(8,128)(2,1)}, u32[]{:S(2)}, u32[]{:S(2)}) collective-permute-start(bf16[128,1024]{1,0:T(8,128)(2,1)} %v_ref.1), channel_id=1, source_target_pairs={{0,2},{1,3},{2,4},{3,5},{4,6},{5,7},{6,8},{7,9},{8,10},{9,11},{10,... | collective-permute-start | bytes 786440 | tf_op jit(solution)/shard_map/ppermute | solution.py:463
  202.5 7.1 %copy-start.17 = (bf16[1536,1024]{1,0:T(8,128)(2,1)S(1)}, bf16[1536,1024]{1,0:T(8,128)(2,1)}, u32[]{:S(2)}) copy-start(bf16[1536,1024]{1,0:T(8,128)(2,1)} %get-tuple-element.63) | copy-start | bytes 9437188
  219.7 12.3 %copy-start.7 = (bf16[128,1024]{1,0:T(8,128)(2,1)S(1)}, bf16[128,1024]{1,0:T(8,128)(2,1)}, u32[]{:S(2)}) copy-start(bf16[128,1024]{1,0:T(8,128)(2,1)} %stream_gradient.1.o_ref) | copy-start | bytes 786436
  219.7 18.6 %copy-start.1 = (bf16[1536,1024]{1,0:T(8,128)(2,1)S(1)}, bf16[1536,1024]{1,0:T(8,128)(2,1)}, u32[]{:S(2)}) copy-start(bf16[1536,1024]{1,0:T(8,128)(2,1)} %get-tuple-element.65) | copy-start | bytes 9437188
  227.9 17.4 %collective-permute-start.17 = (f32[16,8,128]{2,1,0:T(8,128)}, f32[16,8,128]{2,1,0:T(8,128)S(1)}, u32[]{:S(2)}, u32[]{:S(2)}) collective-permute-start(f32[16,8,128]{2,1,0:T(8,128)} %get-tuple-element.57), channel_id=1, source_target_pairs={{1,0},{2,1},{3,2},{4,3},{5,4},{6,5},{7,6},{8,7},{9,8},{10,9},{11,1... | collective-permute-start | bytes 196616 | tf_op jit(solution)/shard_map/ppermute | solution.py:463
  229.8 15.5 %collective-permute-start.18 = (f32[16,8,128]{2,1,0:T(8,128)}, f32[16,8,128]{2,1,0:T(8,128)S(1)}, u32[]{:S(2)}, u32[]{:S(2)}) collective-permute-start(f32[16,8,128]{2,1,0:T(8,128)} %get-tuple-element.57), channel_id=1, source_target_pairs={{2,0},{3,1},{4,2},{5,3},{6,4},{7,5},{8,6},{9,7},{10,8},{11,9},{12,... | collective-permute-start | bytes 196616 | tf_op jit(solution)/shard_map/ppermute | solution.py:463
  232.0 19.8 %collective-permute-start.15 = (bf16[128,1024]{1,0:T(8,128)(2,1)S(1)}, bf16[128,1024]{1,0:T(8,128)(2,1)S(1)}, u32[]{:S(2)}, u32[]{:S(2)}) collective-permute-start(bf16[128,1024]{1,0:T(8,128)(2,1)S(1)} %copy-done.7), channel_id=1, source_target_pairs={{1,0},{2,1},{3,2},{4,3},{5,4},{6,5},{7,6},{8,7},{9,8},{10,9},{11,1... | collective-permute-start | bytes 786440 | tf_op jit(solution)/shard_map/ppermute | solution.py:463
  234.7 17.1 %collective-permute-start.16 = (bf16[128,1024]{1,0:T(8,128)(2,1)S(1)}, bf16[128,1024]{1,0:T(8,128)(2,1)S(1)}, u32[]{:S(2)}, u32[]{:S(2)}) collective-permute-start(bf16[128,1024]{1,0:T(8,128)(2,1)S(1)} %copy-done.7), channel_id=1, source_target_pairs={{2,0},{3,1},{4,2},{5,3},{6,4},{7,5},{8,6},{9,7},{10,8},{11,9},{12,... | collective-permute-start | bytes 786440 | tf_op jit(solution)/shard_map/ppermute | solution.py:463
  245.2 8.0 %copy-start.13 = (f32[16,8,128]{2,1,0:T(8,128)}, f32[16,8,128]{2,1,0:T(8,128)S(1)}, u32[]{:S(2)}) copy-start(f32[16,8,128]{2,1,0:T(8,128)S(1)} %collective-permute-done.17.delta1_ref) | copy-start | bytes 196612
  245.3 8.0 %copy-start.14 = (f32[16,8,128]{2,1,0:T(8,128)}, f32[16,8,128]{2,1,0:T(8,128)S(1)}, u32[]{:S(2)}) copy-start(f32[16,8,128]{2,1,0:T(8,128)S(1)} %collective-permute-done.18.delta2_ref) | copy-start | bytes 196612
  (8 other events, 6.8 us)

commit v2 on v1

v2 whole, which is shorter than its diff:
```python
import math

import jax
import jax.numpy as jnp
from jax import lax
from jax.experimental import pallas as pl
from jax.experimental.pallas import tpu as pltpu
from jax.sharding import PartitionSpec as P


D = 1024
HEADS = 16
HEAD = 64
SPAN = 64
LEFT = 256
FRAMES = 128
EXPERTS = 32
CAP = 12
EP = 4
ROWS = EXPERTS * EP * CAP
EPSILON = 1e-06
BF16 = jnp.bfloat16
F32 = jnp.float32
NT = (((1,), (1,)), ((), ()))
TN = (((0,), (0,)), ((), ()))


def iota(shape, dim):
    return lax.broadcasted_iota(jnp.int32, shape, dim)


def ones_where(mask):
    return jnp.where(mask, 1.0, 0.0).astype(BF16)


def matmul(a, b, dims=(((1,), (0,)), ((), ()))):
    return lax.dot_general(a, b, dims, preferred_element_type=F32)


PACK = EXPERTS * 8
WIDE = 1536
CHUNK = EXPERTS * CAP
HALF = D // 2
EXTRA = 16


def picked(ids, valid, places):
    ids = jnp.where(valid, ids, -1).astype(F32)
    return ones_where(jnp.logical_or(ids == places[0], ids == places[1]))


def dispatch_x_kernel(
    stream_ref, grad_ref, gain_ref, routes_ref, gates_ref, k_ref, v_ref, packed_ref, block_ref, both_ref
):
    s = stream_ref[...].astype(F32)
    inverse_rms = lax.rsqrt(jnp.mean(s * s, -1, keepdims=True) + EPSILON)
    normed = ((s * inverse_rms) * gain_ref[...]).astype(BF16)
    routes = routes_ref[...]
    expert = iota((EXPERTS, FRAMES), 0)
    named = [expert == routes[k : k + 1, :] for k in range(2)]
    count = ones_where(jnp.logical_or(named[0], named[1]))
    earlier = ones_where(iota((FRAMES, FRAMES), 0) < iota((FRAMES, FRAMES), 1))
    before = matmul(count, earlier)
    route = [routes[k : k + 1, :].astype(F32) for k in range(2)]
    slot = [jnp.sum(jnp.where(named[k], before, 0.0), 0, keepdims=True) for k in range(2)]
    places = [route[k] * CAP + slot[k] for k in range(2)]
    split = []
    for k in range(2):
        gate = gates_ref[k : k + 1, :]
        high = gate.astype(BF16).astype(F32)
        middle = (gate - high).astype(BF16).astype(F32)
        split += [high, middle, gate - high - middle]
    block_ref[0:FRAMES, :] = grad_ref[...]
    block_ref[FRAMES:, :] = jnp.zeros((EXTRA, D), BF16)
    extra = jnp.concatenate(route + slot + split + [jnp.zeros((EXTRA - 10, FRAMES), F32)], 0)
    block_ref[FRAMES:, 0:FRAMES] = extra.astype(BF16)
    both_ref[0] = k_ref[...]
    both_ref[1] = v_ref[...]
    row = iota((PACK, FRAMES), 0)
    r = row & 7
    base = (row >> 3) * CAP
    main = picked(base + r, r < 8, places)
    low = picked(base + 8 + r, r < 4, places)
    high = picked(base + 4 + r, r >= 4, places)
    packed_ref[:, 0:D] = matmul(main, normed).astype(BF16)
    packed_ref[:, D:] = (matmul(low, normed[:, :HALF]) + matmul(high, normed[:, HALF:])).astype(BF16)


def dispatch_x(stream, grad, gain, routes, gates, keys, values):
    return pl.pallas_call(
        dispatch_x_kernel,
        out_shape=(
            jax.ShapeDtypeStruct((PACK, WIDE), BF16),
            jax.ShapeDtypeStruct((FRAMES + EXTRA, D), BF16),
            jax.ShapeDtypeStruct((2, FRAMES, D), BF16),
        ),
        name="dispatch_x",
    )(stream, grad, gain, routes, gates, keys, values)


def dispatch_g_kernel(*refs):
    blocks, out_ref, pairs, keys = refs[:EP], refs[EP], refs[EP + 1], refs[EP + 2]
    step = pl.program_id(0)

    for q in range(EP):

        @pl.when(step == q)
        def _(q=q):
            extra = blocks[q][FRAMES:, 0:FRAMES].astype(F32)
            upright = extra.T
            g = blocks[q][0:FRAMES, :].astype(F32)
            for k in range(2):
                gate = upright[:, 4 + 3 * k : 5 + 3 * k] + upright[:, 5 + 3 * k : 6 + 3 * k]
                gate = gate + upright[:, 6 + 3 * k : 7 + 3 * k]
                pairs[k * FRAMES : (k + 1) * FRAMES, :] = (gate * g).astype(BF16)
                keys[k : k + 1, :] = extra[k : k + 1, :] * CAP + extra[2 + k : 3 + k, :]

    row = iota((PACK, FRAMES), 0)
    r = row & 7
    base = (row >> 3) * CAP

    def pick(ids, valid):
        ids = jnp.where(valid, ids, -1).astype(F32)
        return jnp.concatenate([ones_where(ids == keys[k : k + 1, :]) for k in range(2)], 1)

    main = pick(base + r, r < 8)
    low = pick(base + 8 + r, r < 4)
    high = pick(base + 4 + r, r >= 4)
    out_ref[:, 0, :, 0:D] = matmul(main, pairs[...]).reshape(EXPERTS, 8, D).astype(BF16)
    rest = matmul(low, pairs[:, :HALF]) + matmul(high, pairs[:, HALF:])
    out_ref[:, 0, :, D:] = rest.reshape(EXPERTS, 8, HALF).astype(BF16)


def dispatch_g(blocks):
    return pl.pallas_call(
        dispatch_g_kernel,
        grid=(EP,),
        in_specs=[pl.BlockSpec((FRAMES + EXTRA, D), lambda i: (0, 0))] * EP,
        out_specs=pl.BlockSpec((EXPERTS, 1, 8, WIDE), lambda i: (0, i, 0, 0)),
        out_shape=jax.ShapeDtypeStruct((EXPERTS, EP, 8, WIDE), BF16),
        scratch_shapes=[pltpu.VMEM((2 * FRAMES, D), BF16), pltpu.VMEM((8, FRAMES), F32)],
        name="dispatch_g",
    )(*blocks)


def fill_moves(moves, packed_dim):
    shape = (PACK, PACK // 2) if packed_dim == 0 else (PACK // 2, PACK)
    p = iota(shape, packed_dim)
    r = iota(shape, 1 - packed_dim)
    same = (p >> 3) == (r >> 2)
    for n in range(2):
        moves[n] = ones_where(jnp.logical_and(same, (p & 7) == (r & 3) + 4 * n))


def unpack(packed, moves, out_ref, start):
    out_ref[start : start + PACK, :] = packed[:, 0:D]
    for n in range(2):
        rest = matmul(moves[n], packed[:, D:]).astype(BF16)
        out_ref[start + PACK : start + CHUNK, n * HALF : (n + 1) * HALF] = rest


N_BLOCK = 256


def forward_kernel(count, *refs):
    parts, gate_ref, up_ref = refs[:count], refs[count], refs[count + 1]
    x_ref, a_ref, s_ref, acted_ref, moves = refs[-5:]

    @pl.when(pl.program_id(0) == 0)
    def _():
        fill_moves(moves, 1)
        for n, part in enumerate(parts):
            unpack(part[...], moves, x_ref, n * CHUNK)

    x = x_ref[...]
    gate = matmul(x, gate_ref[...])
    up = matmul(x, up_ref[...])
    sig = jax.nn.sigmoid(gate)
    silu = gate * sig
    acted_ref[...] = (silu * up).astype(BF16)
    s_ref[...] = silu
    a_ref[...] = up * sig * (1.0 + gate * (1.0 - sig))


def expert_forward(q, parts, w_gate, w_up, filled):
    rows = len(parts) * CHUNK
    whole = [pl.BlockSpec(p.shape, lambda j: (0, 0)) for p in parts]
    weight = pl.BlockSpec((D, N_BLOCK), lambda j: (0, j))
    out = pl.BlockSpec((rows, N_BLOCK), lambda j: (q, j))
    shape = lambda t: jax.ShapeDtypeStruct((ROWS, D), t)
    n = len(parts)
    return pl.pallas_call(
        lambda *refs: forward_kernel(n, *refs),
        grid=(D // N_BLOCK,),
        in_specs=whole + [weight] * 2 + [pl.BlockSpec(memory_space=pl.ANY)] * len(filled),
        out_specs=[pl.BlockSpec((rows, D), lambda j: (q, 0)), out, out, out],
        out_shape=(shape(BF16), shape(F32), shape(F32), shape(BF16)),
        scratch_shapes=[pltpu.VMEM((2, PACK // 2, PACK), BF16)],
        input_output_aliases={n + 2 + i: i for i in range(len(filled))},
        name="expert_forward",
    )(*parts, w_gate, w_up, *filled)


def backward_kernel(
    column_ref, packed_ref, a_ref, s_ref, gate_ref, up_ref, down_ref, g_ref, dgate_ref, dup_ref, out_ref, moves, back
):
    @pl.when(pl.program_id(0) == 0)
    def _():
        fill_moves(moves, 1)
        fill_moves(back, 0)

    unpack(packed_ref[...].astype(F32).reshape(PACK, WIDE).astype(BF16), moves, g_ref, 0)
    dact = matmul(g_ref[...], down_ref[...], NT)
    dgate = (dact * a_ref[...]).astype(BF16)
    dup = (dact * s_ref[...]).astype(BF16)
    dgate_ref[...] = dgate
    dup_ref[...] = dup
    dx = matmul(dgate, gate_ref[...], NT) + matmul(dup, up_ref[...], NT)
    out_ref[:, 0, :, 0:D] = dx[:PACK].reshape(EXPERTS, 8, D).astype(BF16)
    last = dx[PACK:].astype(BF16)
    rest = matmul(back[0], last[:, :HALF]) + matmul(back[1], last[:, HALF:])
    out_ref[:, 0, :, D:] = rest.reshape(EXPERTS, 8, HALF).astype(BF16)


def expert_backward(column, packed, a, s, w_gate, w_up, w_down):
    def home(q, c):
        return (c[0] + jnp.where(q < 2, 3 - 2 * q, 2 * q - 4)) & 3

    weight = pl.BlockSpec((D, D), lambda i, c: (0, 0), pipeline_mode=pl.Buffered(1))
    rows = pl.BlockSpec((CHUNK, D), lambda i, c: (i, 0))
    shape = jax.ShapeDtypeStruct((ROWS, D), BF16)
    return pl.pallas_call(
        backward_kernel,
        grid_spec=pltpu.PrefetchScalarGridSpec(
            num_scalar_prefetch=1,
            grid=(EP,),
            in_specs=[
                pl.BlockSpec((EXPERTS, 1, 8, WIDE), lambda i, c: (0, i, 0, 0)),
                rows,
                rows,
                weight,
                weight,
                weight,
            ],
            out_specs=[rows, rows, rows, pl.BlockSpec((EXPERTS, 1, 8, WIDE), lambda i, c: (0, home(i, c), 0, 0))],
            scratch_shapes=[
                pltpu.VMEM((2, PACK // 2, PACK), BF16),
                pltpu.VMEM((2, PACK, PACK // 2), BF16),
            ],
        ),
        out_shape=(shape, shape, shape, jax.ShapeDtypeStruct((EXPERTS, EP, 8, WIDE), BF16)),
        name="expert_backward",
    )(column, packed, a, s, w_gate, w_up, w_down)


WINDOW = LEFT + FRAMES
SCALE = 1.0 / math.sqrt(HEAD)
PAIR = 2 * HEAD
STEP_PAIRS = 2
WIDTH = STEP_PAIRS * PAIR
STEP_HEADS = 2 * STEP_PAIRS
STEPS = HEADS // STEP_HEADS


def one_head(pair, h):
    lane = iota(pair.shape, 1)
    mask = lane >= HEAD if h else lane < HEAD
    return jnp.where(mask, pair.astype(F32), 0.0).astype(BF16)


def lanes(n):
    return slice(n * PAIR, (n + 1) * PAIR)


def columns_spec(*lead):
    return pl.BlockSpec((*lead, WIDTH), lambda i, *_: (0,) * len(lead) + (i,))


def heads_spec(*rest):
    return pl.BlockSpec((STEP_HEADS, *rest), lambda i, *_: (i,) + (0,) * len(rest))


def probs_kernel(first_ref, q_ref, both2_ref, both1_ref, k_ref, v_ref, p_ref, stats_ref, attn_ref):
    s = iota((WINDOW, FRAMES), 0)
    skipped = jnp.where(iota((WINDOW, FRAMES), 1) >= SPAN, SPAN, 0)
    allowed = jnp.logical_and(s >= skipped, s < skipped + (WINDOW - SPAN))
    allowed = jnp.logical_and(allowed, s >= first_ref[0])
    stats_ref[...] = jnp.zeros((STEP_HEADS, 8, FRAMES), F32)
    for n in range(STEP_PAIRS):
        c = lanes(n)
        keys = jnp.concatenate([both2_ref[0, :, c], both1_ref[0, :, c], k_ref[:, c]], 0)
        values = jnp.concatenate([both2_ref[1, :, c], both1_ref[1, :, c], v_ref[:, c]], 0)
        q = q_ref[:, c]
        attn = 0.0
        for h in range(2):
            at = 2 * n + h
            scores = matmul(keys, one_head(q, h), NT) * SCALE
            scores = jnp.where(allowed, scores, -jnp.inf)
            top = jnp.max(scores, 0, keepdims=True)
            e = jnp.exp(scores - top)
            inverse = 1.0 / jnp.sum(e, 0, keepdims=True)
            probs = e * inverse
            p_ref[at] = probs
            attn += matmul(probs.astype(BF16), one_head(values, h), TN)
            stats_ref[at, 0:1, :] = top
            stats_ref[at, 1:2, :] = inverse
        attn_ref[:, c] = attn


def attention_probs(first, q, both2, both1, k, v):
    both, one = columns_spec(2, FRAMES), columns_spec(FRAMES)
    return pl.pallas_call(
        probs_kernel,
        grid_spec=pltpu.PrefetchScalarGridSpec(
            num_scalar_prefetch=1,
            grid=(STEPS,),
            in_specs=[one, both, both, one, one],
            out_specs=[heads_spec(WINDOW, FRAMES), heads_spec(8, FRAMES), one],
        ),
        out_shape=(
            jax.ShapeDtypeStruct((HEADS, WINDOW, FRAMES), F32),
            jax.ShapeDtypeStruct((HEADS, 8, FRAMES), F32),
            jax.ShapeDtypeStruct((FRAMES, D), F32),
        ),
        name="attention_probs",
    )(first, q, both2, both1, k, v)


def later_probs_kernel(q1_ref, q2_ref, stats1_ref, stats2_ref, k_ref, p_ref):
    shape = (FRAMES, FRAMES)
    allowed = iota(shape, 0) >= jnp.where(iota(shape, 1) >= SPAN, SPAN, 0)
    for n in range(STEP_PAIRS):
        k = k_ref[:, lanes(n)]
        for m, (q_ref, stats_ref) in enumerate(((q1_ref, stats1_ref), (q2_ref, stats2_ref))):
            q = q_ref[:, lanes(n)]
            for h in range(2):
                at = 2 * n + h
                scores = matmul(k, one_head(q, h), NT) * SCALE
                if m == 1:
                    scores = jnp.where(allowed, scores, -jnp.inf)
                p_ref[at, m] = jnp.exp(scores - stats_ref[at, 0:1, :]) * stats_ref[at, 1:2, :]


def later_probs(q1, q2, stats1, stats2, k):
    one, stats = columns_spec(FRAMES), heads_spec(8, FRAMES)
    return pl.pallas_call(
        later_probs_kernel,
        grid=(STEPS,),
        in_specs=[one, one, stats, stats, one],
        out_specs=heads_spec(2, FRAMES, FRAMES),
        out_shape=jax.ShapeDtypeStruct((HEADS, 2, FRAMES, FRAMES), F32),
        name="later_probs",
    )(q1, q2, stats1, stats2, k)


def thirds(x):
    high = x.astype(BF16)
    rest = x - high.astype(F32)
    middle = rest.astype(BF16)
    return high, middle, (rest - middle.astype(F32)).astype(BF16)


def stream_grad_kernel(rows_ref, block_ref, stream_ref, gain_ref, attn_ref, o_ref, sent_ref, main, total):
    j = pl.program_id(0)
    upright = block_ref[FRAMES:, 0:FRAMES].astype(F32).T
    places = [upright[:, k : k + 1] * CAP + upright[:, 2 + k : 3 + k] for k in range(2)]
    row = iota((FRAMES, PACK * EP), 1)
    r = row & 7
    base = (row >> 5) * CAP

    @pl.when(j == 0)
    def _():
        main[...] = picked(base + r, r < 8, places)

    @pl.when(j < 2)
    def _():
        total[j] = matmul(main[...], rows_ref[...])

    @pl.when(j == 2)
    def _():
        low = picked(base + 8 + r, r < 4, places)
        high = picked(base + 4 + r, r >= 4, places)
        rest = matmul(jnp.concatenate([low, high], 0), rows_ref[...])
        dnormed = jnp.concatenate([total[0] + rest[:FRAMES], total[1] + rest[FRAMES:]], 1)
        s = stream_ref[...].astype(F32)
        inverse_rms = lax.rsqrt(jnp.mean(s * s, -1, keepdims=True) + EPSILON)
        scaled = s * inverse_rms
        weighted = dnormed * gain_ref[...]
        mean = jnp.mean(weighted * scaled, -1, keepdims=True)
        grad = block_ref[0:FRAMES, :].astype(F32)
        o = (grad + inverse_rms * (weighted - scaled * mean)).astype(BF16)
        o_ref[...] = o
        sent_ref[0:FRAMES, :] = o
        head = ones_where((iota((HEADS, D), 1) >> 6) == iota((HEADS, D), 0))
        delta = 0.0
        for part in thirds(o.astype(F32) * attn_ref[...]):
            delta += matmul(head, part, NT)
        sent_ref[FRAMES:, :] = jnp.concatenate(
            [*thirds(delta), jnp.zeros((HEADS, D - 3 * FRAMES), BF16)], 1
        )


def stream_gradient(returned, block, stream, gain, attn):
    whole = lambda n: pl.BlockSpec((n, D), lambda j: (0, 0))
    return pl.pallas_call(
        stream_grad_kernel,
        grid=(3,),
        in_specs=[
            pl.BlockSpec((PACK * EP, HALF), lambda j: (0, j)),
            whole(FRAMES + EXTRA),
            whole(FRAMES),
            whole(1),
            whole(FRAMES),
        ],
        out_specs=[whole(FRAMES), whole(FRAMES + HEADS)],
        out_shape=(
            jax.ShapeDtypeStruct((FRAMES, D), BF16),
            jax.ShapeDtypeStruct((FRAMES + HEADS, D), BF16),
        ),
        scratch_shapes=[pltpu.VMEM((FRAMES, PACK * EP), BF16), pltpu.VMEM((2, FRAMES, HALF), F32)],
        name="stream_gradient",
    )(returned, block, stream, gain, attn)


DELTA_SPEC = pl.BlockSpec((HEADS, 3 * FRAMES), lambda i: (FRAMES // HEADS, 0))


def delta_of(ref):
    part = lambda n: ref[:, n * FRAMES : (n + 1) * FRAMES].astype(F32)
    return part(0) + part(1) + part(2)


def own_grads_kernel(
    p_ref, o_ref, extra_ref, q_ref, both2_ref, both1_ref, k_ref, v_ref, dq_ref, dk_ref, dv_ref, deltas
):
    deltas[...] = delta_of(extra_ref)
    for n in range(STEP_PAIRS):
        c = lanes(n)
        o, q = o_ref[:, c], q_ref[:, c]
        keys = jnp.concatenate([both2_ref[0, :, c], both1_ref[0, :, c], k_ref[:, c]], 0)
        values = jnp.concatenate([both2_ref[1, :, c], both1_ref[1, :, c], v_ref[:, c]], 0)
        dq = dk = dv = 0.0
        for h in range(2):
            at = 2 * n + h
            o_h, q_h, k_h = one_head(o, h), one_head(q, h), one_head(keys, h)
            probs = p_ref[at]
            delta = deltas[pl.ds(STEP_HEADS * pl.program_id(0) + at, 1), :]
            dscore = (probs * (matmul(values, o_h, NT) - delta)).astype(BF16)
            dq += matmul(dscore, k_h, TN)
            dk += matmul(dscore[LEFT:], q_h)
            dv += matmul(probs[LEFT:].astype(BF16), o_h)
        dq_ref[:, c] = (dq * SCALE).astype(BF16)
        dk_ref[:, c] = dk
        dv_ref[:, c] = dv


def own_grads(probs, sent, q, both2, both1, keys, values):
    one, both = columns_spec(FRAMES), columns_spec(2, FRAMES)
    out = lambda t: jax.ShapeDtypeStruct((FRAMES, D), t)
    return pl.pallas_call(
        own_grads_kernel,
        grid=(STEPS,),
        in_specs=[heads_spec(WINDOW, FRAMES), one, DELTA_SPEC, one, both, both, one, one],
        out_specs=[one, one, one],
        out_shape=(out(BF16), out(F32), out(F32)),
        scratch_shapes=[pltpu.VMEM((HEADS, FRAMES), F32)],
        name="own_grads",
    )(probs, sent, sent, q, both2, both1, keys, values)


def later_grads_kernel(
    p_ref, o1_ref, o2_ref, extra1_ref, extra2_ref, q1_ref, q2_ref, v_ref, dk_ref, dv_ref, keys_ref, values_ref, deltas
):
    deltas[0] = delta_of(extra1_ref)
    deltas[1] = delta_of(extra2_ref)
    for n in range(STEP_PAIRS):
        c = lanes(n)
        v = v_ref[:, c]
        dk, dv = dk_ref[:, c], dv_ref[:, c]
        for m, (o_ref, q_ref) in enumerate(((o1_ref, q1_ref), (o2_ref, q2_ref))):
            o, q = o_ref[:, c], q_ref[:, c]
            for h in range(2):
                at = 2 * n + h
                o_h, q_h = one_head(o, h), one_head(q, h)
                probs = p_ref[at, m]
                delta = deltas[m, pl.ds(STEP_HEADS * pl.program_id(0) + at, 1), :]
                dscore = (probs * (matmul(v, o_h, NT) - delta)).astype(BF16)
                dk += matmul(dscore, q_h)
                dv += matmul(probs.astype(BF16), o_h)
        keys_ref[:, c] = (dk * SCALE).astype(BF16)
        values_ref[:, c] = dv.astype(BF16)


def later_grads(probs, os, qs, v, dk, dv):
    one = columns_spec(FRAMES)
    return pl.pallas_call(
        later_grads_kernel,
        grid=(STEPS,),
        in_specs=[heads_spec(2, FRAMES, FRAMES), one, one, DELTA_SPEC, DELTA_SPEC] + [one] * 5,
        out_specs=[one, one],
        out_shape=(jax.ShapeDtypeStruct((FRAMES, D), BF16),) * 2,
        scratch_shapes=[pltpu.VMEM((2, HEADS, FRAMES), F32)],
        name="later_grads",
    )(probs, *os, *os, *qs, v, dk, dv)


def turned(x, distance):
    return lax.ppermute(x, "ep", [(i, (i + distance) % EP) for i in range(EP)])


def shifted(x, distance):
    count = lax.axis_size("tm") * lax.axis_size("ep")
    route = [(i, i + distance) for i in range(count) if 0 <= i + distance < count]
    return lax.ppermute(x, ("tm", "ep"), route)


def exchanged(x, axes):
    return lax.all_to_all(x, axes, split_axis=0, concat_axis=0, tiled=True)


def step(
    queries, keys, values, stream, grad_out, norm_gain, gate_probs, routes, w_gate, w_up, w_down
):
    gain = norm_gain.reshape(1, D)
    weight_gate, weight_up, weight_down = w_gate[0], w_up[0], w_down[0]
    row, column = lax.axis_index("tm"), lax.axis_index("ep")
    packed, block, both = dispatch_x(
        stream, grad_out, gain, routes.T, gate_probs.T, keys, values
    )
    block_left = turned(block, 1)
    block_right = turned(block, -1)
    block_far = turned(block, 2)
    own = exchanged(packed.reshape(EXPERTS, 8, WIDE), "tm").reshape(PACK, WIDE)
    left = turned(own, 1)
    right = turned(own, -1)
    far = turned(left, 1)
    sent_g = dispatch_g((block_left, block_right, block, block_far)).reshape(EXPERTS, EP * 8, WIDE)
    packed_g = exchanged(sent_g, "tm").reshape(EXPERTS, EP, 8, WIDE)
    filled = expert_forward(2, (own,), weight_gate, weight_up, ())
    filled = expert_forward(0, (left, right), weight_gate, weight_up, filled)
    x_rows, a, s, acted = expert_forward(3, (far,), weight_gate, weight_up, filled)
    both1 = shifted(both, 1)
    both2 = shifted(both, 2)
    q1 = shifted(queries, -1)
    q2 = shifted(queries, -2)
    g_rows, dgate, dup, dx = expert_backward(
        column.astype(jnp.int32).reshape(1), packed_g, a, s, weight_gate, weight_up, weight_down
    )
    returned = exchanged(dx.reshape(EXPERTS * EP, 8, WIDE), ("tm", "ep")).reshape(PACK * EP, WIDE)
    gate_grad = jnp.dot(x_rows.T, dgate, preferred_element_type=F32)
    up_grad = jnp.dot(x_rows.T, dup, preferred_element_type=F32)
    down_grad = jnp.dot(acted.T, g_rows, preferred_element_type=F32)
    position = row * lax.axis_size("ep") + column
    first = jnp.maximum(LEFT - position * FRAMES, 0).astype(jnp.int32).reshape(1)
    probs, stats, attn = attention_probs(first, queries, both2, both1, keys, values)
    stats1 = shifted(stats, -1)
    stats2 = shifted(stats, -2)
    later = later_probs(q1, q2, stats1, stats2, keys)
    returned, later, probs, gate_grad, up_grad, down_grad = lax.optimization_barrier(
        (returned, later, probs, gate_grad, up_grad, down_grad)
    )
    stream_grad, sent_o = stream_gradient(returned, block, stream, gain, attn)
    o1 = shifted(sent_o, -1)
    o2 = shifted(sent_o, -2)
    grad_q, own_k, own_v = own_grads(probs, sent_o, queries, both2, both1, keys, values)
    grad_k, grad_v = later_grads(later, (o1, o2), (q1, q2), values, own_k, own_v)
    return (
        grad_q,
        grad_k,
        grad_v,
        stream_grad,
        gate_grad[None],
        up_grad[None],
        down_grad[None],
    )


def solution(mesh):
    frames = P(("tm", "ep"), None)
    columns, rows = P("tm", None, "ep"), P("tm", "ep", None)
    return jax.shard_map(
        step,
        mesh=mesh,
        in_specs=(frames,) * 5 + (P(), frames, frames, columns, columns, rows),
        out_specs=(frames,) * 4 + (columns, columns, rows),
        check_vma=False,
    )
```

time: 263 us -> 251 us (0.954)
  waiting for transfers between devices: 69.8 us -> 89.4 us
  starting transfers between devices: 74.5 us -> 60 us
  Pallas kernels: 88.1 us -> 74.4 us
    ppermute x12 -> x8, waiting for transfers between devices: 39.3 us -> 57.1 us  [shifted(): return lax.ppermute(x, ('tm', 'ep'), route)]
    ppermute x12 -> x8, starting transfers between devices: 39.6 us -> 25.2 us  [shifted(): return lax.ppermute(x, ('tm', 'ep'), route)]
    pallas_call x3, Pallas kernels: 21.3 us -> 15.1 us  [the longest x1 5.95 us: own_grads(): pl.pallas_call(own_grads_kernel, grid=(STEPS,), in_specs=[heads_spec(WIND...]
    pallas_call x4 -> x3, Pallas kernels: 26.3 us -> 21.3 us  [expert_forward(): pl.pallas_call(lambda *refs: forward_kernel(n, *refs), grid=(D // N_BLOCK...]
    ppermute x7 -> x6, waiting for transfers between devices: 30.5 us -> 32.3 us  [turned(): return lax.ppermute(x, 'ep', [(i, (i + distance) % EP) for i in range(EP)])]
    unnamed x36 -> x30, local copies, waits for them, and re-layouts: 6.83 us -> 6.51 us
    ppermute x7 -> x6, starting transfers between devices: 5.75 us -> 5.68 us  [turned(): return lax.ppermute(x, 'ep', [(i, (i + distance) % EP) for i in range(EP)])]
  transfers between devices with their start and end apart: 22 -> 17, of which waited for: 7 -> 10; matrix products, arithmetic and copies ran while one was open for 8% -> 7% of each run, Pallas kernels for 19% -> 17%
where the time goes in v2:
time: 251 us; the launch traced here: 250 us
  waiting for transfers between devices  89.4 us (36%)
  Pallas kernels  74.4 us (30%)
  starting transfers between devices  60 us (24%)
  matrix products  18.5 us (7%)
  local copies, waits for them, and re-layouts  6.51 us (3%)
    ppermute x8, waiting for transfers between devices, shifted(): return lax.ppermute(x, ('tm', 'ep'), route)  57.1 us
    ppermute x6, waiting for transfers between devices, turned(): return lax.ppermute(x, 'ep', [(i, (i + distance) % EP) for i in range(EP)])  32.3 us
    all_to_all x3, starting transfers between devices, exchanged(): return lax.all_to_all(x, axes, split_axis=0, concat_axis=0, tiled=True)  29.1 us
    ppermute x8, starting transfers between devices, shifted(): return lax.ppermute(x, ('tm', 'ep'), route)  25.2 us
    pallas_call x3, Pallas kernels, expert_forward(): pl.pallas_call(lambda *refs: forward_kernel(n, *refs), grid=(D // N_BLOCK...  21.3 us
    pallas_call x1, Pallas kernels, expert_backward(): pl.pallas_call(backward_kernel, grid_spec=pltpu.PrefetchScalarGridSpec(nu...  18.1 us
    dot_general x1, matrix products, step(): up_grad = jnp.dot(x_rows.T, dup, preferred_element_type=F32)  8.47 us
    unnamed x30, local copies, waits for them, and re-layouts  6.51 us
  transfers between devices with their start and end apart: 17, of which 10 were waited for; matrix products, arithmetic and copies ran while one was open for 7% of the time, Pallas kernels for 17%

profile of v2, /device:TPU:31, one launch (start us, length us, event | category | flops | bytes accessed | tf_op | source)
XLA Modules:
  0.0 249.7 jit_solution(8484789420837223095)
XLA Ops:
  0.6 2.9 %dispatch_x.1 = (bf16[256,1536]{1,0:T(8,128)(2,1)}, bf16[144,1024]{1,0:T(8,128)(2,1)}, bf16[2,128,1024]{2,1,0:T(8,128)(2,1)}) custom-call(bf16[128,1024]{1,0:T(8,128)(2,1)} %stream_ref.3, bf16[128,1024]{1,0:T(8,128)(2,1)} %grad_ref.1, f32[1,1024]{1,0:T(1,128)} %bitcast.40, s32[2,128]{1,0:T(2,128)} %bitcast.42, f32[2,128]{1,0:T(2,128)} %bitcast.43, ...), custom_call_target="tpu_custom_call" | custom-call | tf_op jit(solution)/shard_map/dispatch_x/pallas_call | solution.py:90
  3.5 8.6 %all-to-all-start.1 = ((bf16[32,8,1536]{2,1,0:T(8,128)(2,1)}), bf16[32,8,1536]{2,1,0:T(8,128)(2,1)S(1)}, u32[]{:S(2)}, u32[]{:S(2)}) async-start(bf16[32,8,1536]{2,1,0:T(8,128)(2,1)} %bitcast.39), calls=%async_computation.1 | async-start | bytes 1572864 | tf_op jit(solution)/shard_map/all_to_all | solution.py:518
  14.8 5.8 %collective-permute-done.refs_0_ = bf16[144,1024]{1,0:T(8,128)(2,1)S(1)} collective-permute-done((bf16[144,1024]{1,0:T(8,128)(2,1)}, bf16[144,1024]{1,0:T(8,128)(2,1)S(1)}, u32[]{:S(2)}, u32[]{:S(2)}) %collective-permute-start) | collective-permute-done | bytes 294944 | tf_op jit(solution)/shard_map/ppermute | solution.py:508
  22.0 5.8 %collective-permute-done.2.refs_3_ = bf16[144,1024]{1,0:T(8,128)(2,1)S(1)} collective-permute-done((bf16[144,1024]{1,0:T(8,128)(2,1)}, bf16[144,1024]{1,0:T(8,128)(2,1)S(1)}, u32[]{:S(2)}, u32[]{:S(2)}) %collective-permute-start.2) | collective-permute-done | bytes 294944 | tf_op jit(solution)/shard_map/ppermute | solution.py:508
  28.5 5.3 %dispatch_g.1 = bf16[32,4,8,1536]{3,2,1,0:T(8,128)(2,1)} custom-call(bf16[144,1024]{1,0:T(8,128)(2,1)} %copy-done.8, bf16[144,1024]{1,0:T(8,128)(2,1)} %copy-done.9, bf16[144,1024]{1,0:T(8,128)(2,1)} %get-tuple-element.42.refs_2_.block_ref, bf16[144,1024]{1,0:T(8,128)(2,1)} %copy-done.10), custom_call_target="tpu_custom_call" | custom-call | tf_op jit(solution)/shard_map/dispatch_g/pallas_call | solution.py:135
  34.7 9.5 %all-to-all-start = ((bf16[32,32,1536]{2,1,0:T(8,128)(2,1)}), bf16[32,32,1536]{2,1,0:T(8,128)(2,1)S(1)}, u32[]{:S(2)}, u32[]{:S(2)}) async-start(bf16[32,32,1536]{2,1,0:T(8,128)(2,1)} %bitcast.33), calls=%async_computation | async-start | bytes 6291456 | tf_op jit(solution)/shard_map/all_to_all | solution.py:518
  45.7 17.6 %collective-permute-done.3.refs_0_ = bf16[256,1536]{1,0:T(8,128)(2,1)} collective-permute-done((bf16[256,1536]{1,0:T(8,128)(2,1)}, bf16[256,1536]{1,0:T(8,128)(2,1)}, u32[]{:S(2)}, u32[]{:S(2)}) %collective-permute-start.3) | collective-permute-done | bytes 786464 | tf_op jit(solution)/shard_map/ppermute | solution.py:508
  64.8 6.3 %expert_forward.3 = (bf16[1536,1024]{1,0:T(8,128)(2,1)}, f32[1536,1024]{1,0:T(8,128)}, f32[1536,1024]{1,0:T(8,128)}, bf16[1536,1024]{1,0:T(8,128)(2,1)}) custom-call(bf16[256,1536]{1,0:T(8,128)(2,1)} %bitcast.36, bf16[1024,1024]{1,0:T(8,128)(2,1)} %bitcast.23, bf16[1024,1024]{1,0:T(8,128)(2,1)} %bitcast.27), custom_call_target="tpu_custom_call" | custom-call | tf_op jit(solution)/shard_map/expert_forward/pallas_call | solution.py:192
  71.0 8.7 %expert_forward.4 = (bf16[1536,1024]{1,0:T(8,128)(2,1)}, f32[1536,1024]{1,0:T(8,128)}, f32[1536,1024]{1,0:T(8,128)}, bf16[1536,1024]{1,0:T(8,128)(2,1)}) custom-call(bf16[256,1536]{1,0:T(8,128)(2,1)} %collective-permute-done.3.refs_0_, ...), custom_call_target="tpu_custom_call", output_to_operand_aliasing={{0}: (4, {}), {1}: (5, {}), {2}: (6, {}), {3}: (7, {})} | custom-call | tf_op jit(solution)/shard_map/expert_forward/pallas_call | solution.py:192
  81.4 6.3 %expert_forward.5 = (bf16[1536,1024]{1,0:T(8,128)(2,1)}, f32[1536,1024]{1,0:T(8,128)}, f32[1536,1024]{1,0:T(8,128)}, bf16[1536,1024]{1,0:T(8,128)(2,1)}) custom-call(bf16[256,1536]{1,0:T(8,128)(2,1)} %collective-permute-done.4.refs_0_, bf16[1024,1024]{1,0:T(8,128)(2,1)} %bitcast.25, ...), custom_call_target="tpu_custom_call", output_to_operand_aliasing={{0}: (3, {}), {1}: (4, {}), {2}: (5, {}), {3}: (6, {})} | custom-call | tf_op jit(solution)/shard_map/expert_forward/pallas_call | solution.py:192
  89.4 18.1 %expert_backward.1 = (bf16[1536,1024]{1,0:T(8,128)(2,1)}, bf16[1536,1024]{1,0:T(8,128)(2,1)}, bf16[1536,1024]{1,0:T(8,128)(2,1)}, bf16[32,4,8,1536]{3,2,1,0:T(8,128)(2,1)}) custom-call(s32[1]{0:T(128)} %bitcast.column_ref, bf16[32,4,8,1536]{3,2,1,0:T(8,128)(2,1)} %bitcast.31, f32[1536,1024]{1,0:T(8,128)} %get-tuple-element.52.a_ref, ...), custom_call_target="tpu_custom_call" | custom-call | tf_op jit(solution)/shard_map/expert_backward/pallas_call | solution.py:232
  107.5 11.0 %all-to-all-start.2 = ((bf16[128,8,1536]{2,1,0:T(8,128)(2,1)}), bf16[128,8,1536]{2,1,0:T(8,128)(2,1)S(1)}, u32[]{:S(2)}, u32[]{:S(2)}) async-start(bf16[128,8,1536]{2,1,0:T(8,128)(2,1)} %bitcast.37), calls=%async_computation.2 | async-start | bytes 6291456 | tf_op jit(solution)/shard_map/all_to_all | solution.py:518
  118.5 4.3 %collective-permute-start.8 = (bf16[2,128,1024]{2,1,0:T(8,128)(2,1)}, bf16[2,128,1024]{2,1,0:T(8,128)(2,1)}, u32[]{:S(2)}, u32[]{:S(2)}) collective-permute-start(bf16[2,128,1024]{2,1,0:T(8,128)(2,1)} %get-tuple-element.55), channel_id=1, source_target_pairs={{0,2},{1,3},{2,4},{3,5},{4,6},{5,7},{6,8},{7,9},{8,10},{9,11},{10,... | collective-permute-start | bytes 1572872 | tf_op jit(solution)/shard_map/ppermute | solution.py:514
  122.8 4.0 %collective-permute-start.9 = (bf16[2,128,1024]{2,1,0:T(8,128)(2,1)}, bf16[2,128,1024]{2,1,0:T(8,128)(2,1)}, u32[]{:S(2)}, u32[]{:S(2)}) collective-permute-start(bf16[2,128,1024]{2,1,0:T(8,128)(2,1)} %get-tuple-element.55), channel_id=1, source_target_pairs={{0,1},{1,2},{2,3},{3,4},{4,5},{5,6},{6,7},{7,8},{8,9},{9,10},{10,1... | collective-permute-start | bytes 1572872 | tf_op jit(solution)/shard_map/ppermute | solution.py:514
  126.8 1.9 collective-permute-start.6
  128.8 1.9 collective-permute-start.7
  130.7 34.0 %collective-permute-done.8.both2_ref = bf16[2,128,1024]{2,1,0:T(8,128)(2,1)} collective-permute-done((bf16[2,128,1024]{2,1,0:T(8,128)(2,1)}, bf16[2,128,1024]{2,1,0:T(8,128)(2,1)}, u32[]{:S(2)}, u32[]{:S(2)}) %collective-permute-start.8) | collective-permute-done | bytes 524320 | tf_op jit(solution)/shard_map/ppermute | solution.py:514
  164.7 10.6 %collective-permute-done.9.both1_ref = bf16[2,128,1024]{2,1,0:T(8,128)(2,1)} collective-permute-done((bf16[2,128,1024]{2,1,0:T(8,128)(2,1)}, bf16[2,128,1024]{2,1,0:T(8,128)(2,1)}, u32[]{:S(2)}, u32[]{:S(2)}) %collective-permute-start.9) | collective-permute-done | bytes 524320 | tf_op jit(solution)/shard_map/ppermute | solution.py:514
  175.4 5.9 %attention_probs.1 = (f32[16,384,128]{2,1,0:T(8,128)}, f32[16,8,128]{2,1,0:T(8,128)}, f32[128,1024]{1,0:T(8,128)}) custom-call(s32[1]{0:T(128)} %bitcast.13.first_ref, bf16[128,1024]{1,0:T(8,128)(2,1)} %q_ref.3, bf16[2,128,1024]{2,1,0:T(8,128)(2,1)} %collective-permute-done.8.both2_ref, bf16[2,128,1024]{2,1,0:T(8,128)(2,1)} %collective-permute-done.9.both1_ref, ...), custom_call_target="tpu_custom_call" | custom-call | tf_op jit(solution)/shard_map/attention_probs/pallas_call | solution.py:312
  181.3 2.2 collective-permute-start.10
  183.5 5.6 %collective-permute-start.11 = (f32[16,8,128]{2,1,0:T(8,128)}, f32[16,8,128]{2,1,0:T(8,128)S(1)}, u32[]{:S(2)}, u32[]{:S(2)}) collective-permute-start(f32[16,8,128]{2,1,0:T(8,128)} %get-tuple-element.56), channel_id=1, source_target_pairs={{2,0},{3,1},{4,2},{5,3},{6,4},{7,5},{8,6},{9,7},{10,8},{11,9},{12,... | collective-permute-start | bytes 196616 | tf_op jit(solution)/shard_map/ppermute | solution.py:514
  189.2 2.1 collective-permute-done.10.stats1_ref
  191.3 2.8 %collective-permute-done.11.stats2_ref = f32[16,8,128]{2,1,0:T(8,128)S(1)} collective-permute-done((f32[16,8,128]{2,1,0:T(8,128)}, f32[16,8,128]{2,1,0:T(8,128)S(1)}, u32[]{:S(2)}, u32[]{:S(2)}) %collective-permute-start.11) | collective-permute-done | bytes 65568 | tf_op jit(solution)/shard_map/ppermute | solution.py:514
  194.8 4.2 %later_probs.1.p_ref = f32[16,2,128,128]{3,2,1,0:T(8,128)} custom-call(bf16[128,1024]{1,0:T(8,128)(2,1)} %copy-done.7, bf16[128,1024]{1,0:T(8,128)(2,1)} %collective-permute-done.7.q2_ref, f32[16,8,128]{2,1,0:T(8,128)} %copy-done.11, f32[16,8,128]{2,1,0:T(8,128)} %copy-done.12, bf16[128,1024]{1,0:T(8,128)(2,1)} %k_ref.7), custom_call_target="tpu_custom_call" | custom-call | tf_op jit(solution)/shard_map/later_probs/pallas_call | solution.py:346
  199.0 8.5 %fusion.1 = f32[1024,1024]{1,0:T(8,128)} fusion(bf16[1536,1024]{1,0:T(8,128)(2,1)} %get-tuple-element.58, bf16[1536,1024]{1,0:T(8,128)(2,1)} %get-tuple-element.60), kind=kOutput, calls=%fused_computation.1 | convolution fusion | flops 3221225472 | bytes 10485760 | tf_op jit(solution)/shard_map/dot_general | solution.py:551
  207.5 5.0 %fusion = f32[1024,1024]{1,0:T(8,128)} fusion(bf16[1536,1024]{1,0:T(8,128)(2,1)S(1)} %copy-done.2, bf16[1536,1024]{1,0:T(8,128)(2,1)S(1)} %copy-done.14), kind=kOutput, calls=%fused_computation | convolution fusion | flops 3221225472 | bytes 10485760 | tf_op jit(solution)/shard_map/dot_general | solution.py:550
  212.5 5.0 %fusion.2 = f32[1024,1024]{1,0:T(8,128)} fusion(bf16[1536,1024]{1,0:T(8,128)(2,1)S(1)} %copy-done.3, bf16[1536,1024]{1,0:T(8,128)(2,1)S(1)} %copy-done.13), kind=kOutput, calls=%fused_computation.2 | convolution fusion | flops 3221225472 | bytes 10485760 | tf_op jit(solution)/shard_map/dot_general | solution.py:552
  219.2 5.8 %stream_gradient.1 = (bf16[128,1024]{1,0:T(8,128)(2,1)}, bf16[144,1024]{1,0:T(8,128)(2,1)}) custom-call(bf16[1024,1536]{1,0:T(8,128)(2,1)} %bitcast.32, bf16[144,1024]{1,0:T(8,128)(2,1)} %get-tuple-element.42.refs_2_.block_ref, bf16[128,1024]{1,0:T(8,128)(2,1)} %stream_ref.3, f32[1,1024]{1,0:T(1,128)} %bitcast.41, f32[128,1024]{1,0:T(8,128)} %get-tuple-element.65.attn_ref), custom_call_target="tpu_custom_call" | custom-call | tf_op jit(solution)/shard_map/stream_gradient/pallas_call | solution.py:405
  226.9 3.3 %collective-permute-start.13 = (bf16[144,1024]{1,0:T(8,128)(2,1)}, bf16[144,1024]{1,0:T(8,128)(2,1)S(1)}, u32[]{:S(2)}, u32[]{:S(2)}) collective-permute-start(bf16[144,1024]{1,0:T(8,128)(2,1)} %get-tuple-element.66.o_ref.extra_ref), channel_id=1, source_target_pairs={{2,0},{3,1},{4,2},{5,3},{6,4},{7,5},{8,6},{9,7},{10,8},{11,9},{12,... | collective-permute-start | bytes 884744 | tf_op jit(solution)/shard_map/ppermute | solution.py:514
  230.2 5.9 %own_grads.1 = (bf16[128,1024]{1,0:T(8,128)(2,1)}, f32[128,1024]{1,0:T(8,128)}, f32[128,1024]{1,0:T(8,128)}) custom-call(f32[16,384,128]{2,1,0:T(8,128)} %get-tuple-element.63.p_ref, bf16[144,1024]{1,0:T(8,128)(2,1)} %get-tuple-element.66.o_ref.extra_ref, bf16[144,1024]{1,0:T(8,128)(2,1)} %get-tuple-element.66.o_ref.extra_ref, bf16[128,1024]{1,0:T(8,128)(2,1)} %q_ref.3, ...), custom_call_target="tpu_custom_call" | custom-call | tf_op jit(solution)/shard_map/own_grads/pallas_call | solution.py:460
  236.2 7.5 %collective-permute-done.12.o1_ref.extra1_ref = bf16[144,1024]{1,0:T(8,128)(2,1)S(1)} collective-permute-done((bf16[144,1024]{1,0:T(8,128)(2,1)}, bf16[144,1024]{1,0:T(8,128)(2,1)S(1)}, u32[]{:S(2)}, u32[]{:S(2)}) %collective-permute-start.12) | collective-permute-done | bytes 294944 | tf_op jit(solution)/shard_map/ppermute | solution.py:514
  244.6 5.0 %later_grads.1 = (bf16[128,1024]{1,0:T(8,128)(2,1)}, bf16[128,1024]{1,0:T(8,128)(2,1)}) custom-call(f32[16,2,128,128]{3,2,1,0:T(8,128)} %later_probs.1.p_ref, bf16[144,1024]{1,0:T(8,128)(2,1)} %copy-done.5, bf16[144,1024]{1,0:T(8,128)(2,1)} %copy-done.6, bf16[144,1024]{1,0:T(8,128)(2,1)} %copy-done.5, bf16[144,1024]{1,0:T(8,128)(2,1)} %copy-done.6, ...), custom_call_target="tpu_custom_call" | custom-call | tf_op jit(solution)/shard_map/later_grads/pallas_call | solution.py:496
  (46 shorter events, 17.2 us)
Async XLA Ops:
  3.5 30.3 %all-to-all-start.1 = ((bf16[32,8,1536]{2,1,0:T(8,128)(2,1)}), bf16[32,8,1536]{2,1,0:T(8,128)(2,1)S(1)}, u32[]{:S(2)}, u32[]{:S(2)}) async-start(bf16[32,8,1536]{2,1,0:T(8,128)(2,1)} %bitcast.39), calls=%async_computation.1 | async-start | bytes 1572864 | tf_op jit(solution)/shard_map/all_to_all | solution.py:518
  12.1 8.5 %collective-permute-start = (bf16[144,1024]{1,0:T(8,128)(2,1)}, bf16[144,1024]{1,0:T(8,128)(2,1)S(1)}, u32[]{:S(2)}, u32[]{:S(2)}) collective-permute-start(bf16[144,1024]{1,0:T(8,128)(2,1)} %get-tuple-element.42.refs_2_.block_ref), channel_id=1, source_target_pairs={{0,1},{1,2},{2,3},{3,0},{4,5},{5,6},{6,7},{7,4},{8,9},{9,10},{10,1... | collective-permute-start | bytes 884744 | tf_op jit(solution)/shard_map/ppermute | solution.py:508
  12.4 9.6 %collective-permute-start.1 = (bf16[144,1024]{1,0:T(8,128)(2,1)}, bf16[144,1024]{1,0:T(8,128)(2,1)S(1)}, u32[]{:S(2)}, u32[]{:S(2)}) collective-permute-start(bf16[144,1024]{1,0:T(8,128)(2,1)} %get-tuple-element.42.refs_2_.block_ref), channel_id=1, source_target_pairs={{0,3},{1,0},{2,1},{3,2},{4,7},{5,4},{6,5},{7,6},{8,11},{9,8},{10,9... | collective-permute-start | bytes 884744 | tf_op jit(solution)/shard_map/ppermute | solution.py:508
  13.7 14.1 %collective-permute-start.2 = (bf16[144,1024]{1,0:T(8,128)(2,1)}, bf16[144,1024]{1,0:T(8,128)(2,1)S(1)}, u32[]{:S(2)}, u32[]{:S(2)}) collective-permute-start(bf16[144,1024]{1,0:T(8,128)(2,1)} %get-tuple-element.42.refs_2_.block_ref), channel_id=1, source_target_pairs={{0,2},{1,3},{2,0},{3,1},{4,6},{5,7},{6,4},{7,5},{8,10},{9,11},{10,... | collective-permute-start | bytes 884744 | tf_op jit(solution)/shard_map/ppermute | solution.py:508
  20.6 7.2 %copy-start.8 = (bf16[144,1024]{1,0:T(8,128)(2,1)}, bf16[144,1024]{1,0:T(8,128)(2,1)S(1)}, u32[]{:S(2)}) copy-start(bf16[144,1024]{1,0:T(8,128)(2,1)S(1)} %collective-permute-done.refs_0_) | copy-start | bytes 884740
  22.0 5.8 %copy-start.9 = (bf16[144,1024]{1,0:T(8,128)(2,1)}, bf16[144,1024]{1,0:T(8,128)(2,1)S(1)}, u32[]{:S(2)}) copy-start(bf16[144,1024]{1,0:T(8,128)(2,1)S(1)} %collective-permute-done.1.refs_1_) | copy-start | bytes 884740
  27.8 0.7 copy-start.10
  33.8 0.9 copy-start.4
  34.7 53.1 %all-to-all-start = ((bf16[32,32,1536]{2,1,0:T(8,128)(2,1)}), bf16[32,32,1536]{2,1,0:T(8,128)(2,1)S(1)}, u32[]{:S(2)}, u32[]{:S(2)}) async-start(bf16[32,32,1536]{2,1,0:T(8,128)(2,1)} %bitcast.33), calls=%async_computation | async-start | bytes 6291456 | tf_op jit(solution)/shard_map/all_to_all | solution.py:518
  44.2 19.1 %collective-permute-start.3 = (bf16[256,1536]{1,0:T(8,128)(2,1)}, bf16[256,1536]{1,0:T(8,128)(2,1)}, u32[]{:S(2)}, u32[]{:S(2)}) collective-permute-start(bf16[256,1536]{1,0:T(8,128)(2,1)} %bitcast.34), channel_id=1, source_target_pairs={{0,1},{1,2},{2,3},{3,0},{4,5},{5,6},{6,7},{7,4},{8,9},{9,10},{10,1... | collective-permute-start | bytes 2359304 | tf_op jit(solution)/shard_map/ppermute | solution.py:508
  44.5 26.5 %collective-permute-start.5 = (bf16[256,1536]{1,0:T(8,128)(2,1)}, bf16[256,1536]{1,0:T(8,128)(2,1)}, u32[]{:S(2)}, u32[]{:S(2)}) collective-permute-start(bf16[256,1536]{1,0:T(8,128)(2,1)} %bitcast.35), channel_id=1, source_target_pairs={{0,3},{1,0},{2,1},{3,2},{4,7},{5,4},{6,5},{7,6},{8,11},{9,8},{10,9... | collective-permute-start | bytes 2359304 | tf_op jit(solution)/shard_map/ppermute | solution.py:508
  63.3 18.2 %collective-permute-start.4 = (bf16[256,1536]{1,0:T(8,128)(2,1)}, bf16[256,1536]{1,0:T(8,128)(2,1)}, u32[]{:S(2)}, u32[]{:S(2)}) collective-permute-start(bf16[256,1536]{1,0:T(8,128)(2,1)} %collective-permute-done.3.refs_0_), channel_id=1, source_target_pairs={{0,1},{1,2},{2,3},{3,0},{4,5},{5,6},{6,7},{7,4},{8,9},{9,10},{10,1... | collective-permute-start | bytes 2359304 | tf_op jit(solution)/shard_map/ppermute | solution.py:508
  87.8 1.7 copy-start
  107.5 110.0 %all-to-all-start.2 = ((bf16[128,8,1536]{2,1,0:T(8,128)(2,1)}), bf16[128,8,1536]{2,1,0:T(8,128)(2,1)S(1)}, u32[]{:S(2)}, u32[]{:S(2)}) async-start(bf16[128,8,1536]{2,1,0:T(8,128)(2,1)} %bitcast.37), calls=%async_computation.2 | async-start | bytes 6291456 | tf_op jit(solution)/shard_map/all_to_all | solution.py:518
  118.5 46.2 %collective-permute-start.8 = (bf16[2,128,1024]{2,1,0:T(8,128)(2,1)}, bf16[2,128,1024]{2,1,0:T(8,128)(2,1)}, u32[]{:S(2)}, u32[]{:S(2)}) collective-permute-start(bf16[2,128,1024]{2,1,0:T(8,128)(2,1)} %get-tuple-element.55), channel_id=1, source_target_pairs={{0,2},{1,3},{2,4},{3,5},{4,6},{5,7},{6,8},{7,9},{8,10},{9,11},{10,... | collective-permute-start | bytes 1572872 | tf_op jit(solution)/shard_map/ppermute | solution.py:514
  122.8 52.5 %collective-permute-start.9 = (bf16[2,128,1024]{2,1,0:T(8,128)(2,1)}, bf16[2,128,1024]{2,1,0:T(8,128)(2,1)}, u32[]{:S(2)}, u32[]{:S(2)}) collective-permute-start(bf16[2,128,1024]{2,1,0:T(8,128)(2,1)} %get-tuple-element.55), channel_id=1, source_target_pairs={{0,1},{1,2},{2,3},{3,4},{4,5},{5,6},{6,7},{7,8},{8,9},{9,10},{10,1... | collective-permute-start | bytes 1572872 | tf_op jit(solution)/shard_map/ppermute | solution.py:514
  126.8 62.4 %collective-permute-start.6 = (bf16[128,1024]{1,0:T(8,128)(2,1)}, bf16[128,1024]{1,0:T(8,128)(2,1)S(1)}, u32[]{:S(2)}, u32[]{:S(2)}) collective-permute-start(bf16[128,1024]{1,0:T(8,128)(2,1)} %q_ref.3), channel_id=1, source_target_pairs={{1,0},{2,1},{3,2},{4,3},{5,4},{6,5},{7,6},{8,7},{9,8},{10,9},{11,1... | collective-permute-start | bytes 786440 | tf_op jit(solution)/shard_map/ppermute | solution.py:514
  128.8 60.4 %collective-permute-start.7 = (bf16[128,1024]{1,0:T(8,128)(2,1)}, bf16[128,1024]{1,0:T(8,128)(2,1)}, u32[]{:S(2)}, u32[]{:S(2)}) collective-permute-start(bf16[128,1024]{1,0:T(8,128)(2,1)} %q_ref.3), channel_id=1, source_target_pairs={{2,0},{3,1},{4,2},{5,3},{6,4},{7,5},{8,6},{9,7},{10,8},{11,9},{12,... | collective-permute-start | bytes 786440 | tf_op jit(solution)/shard_map/ppermute | solution.py:514
  181.3 10.0 %collective-permute-start.10 = (f32[16,8,128]{2,1,0:T(8,128)}, f32[16,8,128]{2,1,0:T(8,128)S(1)}, u32[]{:S(2)}, u32[]{:S(2)}) collective-permute-start(f32[16,8,128]{2,1,0:T(8,128)} %get-tuple-element.56), channel_id=1, source_target_pairs={{1,0},{2,1},{3,2},{4,3},{5,4},{6,5},{7,6},{8,7},{9,8},{10,9},{11,1... | collective-permute-start | bytes 196616 | tf_op jit(solution)/shard_map/ppermute | solution.py:514
  183.5 10.6 %collective-permute-start.11 = (f32[16,8,128]{2,1,0:T(8,128)}, f32[16,8,128]{2,1,0:T(8,128)S(1)}, u32[]{:S(2)}, u32[]{:S(2)}) collective-permute-start(f32[16,8,128]{2,1,0:T(8,128)} %get-tuple-element.56), channel_id=1, source_target_pairs={{2,0},{3,1},{4,2},{5,3},{6,4},{7,5},{8,6},{9,7},{10,8},{11,9},{12,... | collective-permute-start | bytes 196616 | tf_op jit(solution)/shard_map/ppermute | solution.py:514
  189.2 5.0 %copy-start.7 = (bf16[128,1024]{1,0:T(8,128)(2,1)}, bf16[128,1024]{1,0:T(8,128)(2,1)S(1)}, u32[]{:S(2)}) copy-start(bf16[128,1024]{1,0:T(8,128)(2,1)S(1)} %collective-permute-done.6.q1_ref) | copy-start | bytes 786436
  191.3 2.8 %copy-start.11 = (f32[16,8,128]{2,1,0:T(8,128)}, f32[16,8,128]{2,1,0:T(8,128)S(1)}, u32[]{:S(2)}) copy-start(f32[16,8,128]{2,1,0:T(8,128)S(1)} %collective-permute-done.10.stats1_ref) | copy-start | bytes 196612
  194.2 0.6 copy-start.12
  199.0 8.5 %copy-start.2 = (bf16[1536,1024]{1,0:T(8,128)(2,1)S(1)}, bf16[1536,1024]{1,0:T(8,128)(2,1)}, u32[]{:S(2)}) copy-start(bf16[1536,1024]{1,0:T(8,128)(2,1)} %get-tuple-element.58) | copy-start | bytes 9437188
  199.0 8.5 %copy-start.14 = (bf16[1536,1024]{1,0:T(8,128)(2,1)S(1)}, bf16[1536,1024]{1,0:T(8,128)(2,1)}, u32[]{:S(2)}) copy-start(bf16[1536,1024]{1,0:T(8,128)(2,1)} %get-tuple-element.59) | copy-start | bytes 9437188
  207.4 5.0 %copy-start.3 = (bf16[1536,1024]{1,0:T(8,128)(2,1)S(1)}, bf16[1536,1024]{1,0:T(8,128)(2,1)}, u32[]{:S(2)}) copy-start(bf16[1536,1024]{1,0:T(8,128)(2,1)} %get-tuple-element.61) | copy-start | bytes 9437188
  207.4 5.0 %copy-start.13 = (bf16[1536,1024]{1,0:T(8,128)(2,1)S(1)}, bf16[1536,1024]{1,0:T(8,128)(2,1)}, u32[]{:S(2)}) copy-start(bf16[1536,1024]{1,0:T(8,128)(2,1)} %get-tuple-element.62) | copy-start | bytes 9437188
  217.5 1.7 copy-start.1
  225.0 18.7 %collective-permute-start.12 = (bf16[144,1024]{1,0:T(8,128)(2,1)}, bf16[144,1024]{1,0:T(8,128)(2,1)S(1)}, u32[]{:S(2)}, u32[]{:S(2)}) collective-permute-start(bf16[144,1024]{1,0:T(8,128)(2,1)} %get-tuple-element.66.o_ref.extra_ref), channel_id=1, source_target_pairs={{1,0},{2,1},{3,2},{4,3},{5,4},{6,5},{7,6},{8,7},{9,8},{10,9},{11,1... | collective-permute-start | bytes 884744 | tf_op jit(solution)/shard_map/ppermute | solution.py:514
  226.9 16.8 %collective-permute-start.13 = (bf16[144,1024]{1,0:T(8,128)(2,1)}, bf16[144,1024]{1,0:T(8,128)(2,1)S(1)}, u32[]{:S(2)}, u32[]{:S(2)}) collective-permute-start(bf16[144,1024]{1,0:T(8,128)(2,1)} %get-tuple-element.66.o_ref.extra_ref), channel_id=1, source_target_pairs={{2,0},{3,1},{4,2},{5,3},{6,4},{7,5},{8,6},{9,7},{10,8},{11,9},{12,... | collective-permute-start | bytes 884744 | tf_op jit(solution)/shard_map/ppermute | solution.py:514
  243.7 0.7 copy-start.5
  243.7 0.9 copy-start.6

commit v3 on v2

--- a/solution.py
+++ b/solution.py
@@ -23,6 +23,9 @@
 F32 = jnp.float32
 NT = (((1,), (1,)), ((), ()))
 TN = (((0,), (0,)), ((), ()))
+
+
+VMEM_SPEC = pl.BlockSpec(memory_space=pltpu.VMEM)
 
 
 def iota(shape, dim):
@@ -135,7 +138,7 @@
     return pl.pallas_call(
         dispatch_g_kernel,
         grid=(EP,),
-        in_specs=[pl.BlockSpec((FRAMES + EXTRA, D), lambda i: (0, 0))] * EP,
+        in_specs=[VMEM_SPEC, VMEM_SPEC, pl.BlockSpec((FRAMES + EXTRA, D), lambda i: (0, 0)), VMEM_SPEC],
         out_specs=pl.BlockSpec((EXPERTS, 1, 8, WIDE), lambda i: (0, i, 0, 0)),
         out_shape=jax.ShapeDtypeStruct((EXPERTS, EP, 8, WIDE), BF16),
         scratch_shapes=[pltpu.VMEM((2 * FRAMES, D), BF16), pltpu.VMEM((8, FRAMES), F32)],
@@ -159,7 +162,7 @@
         out_ref[start + PACK : start + CHUNK, n * HALF : (n + 1) * HALF] = rest
 
 
-N_BLOCK = 256
+N_BLOCK = 512
 
 
 def forward_kernel(count, *refs):
@@ -184,7 +187,7 @@
 
 def expert_forward(q, parts, w_gate, w_up, filled):
     rows = len(parts) * CHUNK
-    whole = [pl.BlockSpec(p.shape, lambda j: (0, 0)) for p in parts]
+    whole = [VMEM_SPEC] * len(parts)
     weight = pl.BlockSpec((D, N_BLOCK), lambda j: (0, j))
     out = pl.BlockSpec((rows, N_BLOCK), lambda j: (q, j))
     shape = lambda t: jax.ShapeDtypeStruct((ROWS, D), t)
@@ -198,7 +201,7 @@
         scratch_shapes=[pltpu.VMEM((2, PACK // 2, PACK), BF16)],
         input_output_aliases={n + 2 + i: i for i in range(len(filled))},
         name="expert_forward",
-    )(*parts, w_gate, w_up, *filled)
+    )(*[near(p) for p in parts], w_gate, w_up, *filled)
 
 
 def backward_kernel(
@@ -374,13 +377,13 @@
 
     @pl.when(j < 2)
     def _():
-        total[j] = matmul(main[...], rows_ref[...])
+        total[j] = matmul(main[...], rows_ref[:, pl.ds(pl.multiple_of(j * HALF, HALF), HALF)])
 
     @pl.when(j == 2)
     def _():
         low = picked(base + 8 + r, r < 4, places)
         high = picked(base + 4 + r, r >= 4, places)
-        rest = matmul(jnp.concatenate([low, high], 0), rows_ref[...])
+        rest = matmul(jnp.concatenate([low, high], 0), rows_ref[:, D:])
         dnormed = jnp.concatenate([total[0] + rest[:FRAMES], total[1] + rest[FRAMES:]], 1)
         s = stream_ref[...].astype(F32)
         inverse_rms = lax.rsqrt(jnp.mean(s * s, -1, keepdims=True) + EPSILON)
@@ -406,7 +409,7 @@
         stream_grad_kernel,
         grid=(3,),
         in_specs=[
-            pl.BlockSpec((PACK * EP, HALF), lambda j: (0, j)),
+            pl.BlockSpec(memory_space=pltpu.VMEM),
             whole(FRAMES + EXTRA),
             whole(FRAMES),
             whole(1),
@@ -469,16 +472,17 @@
 
 
 def later_grads_kernel(
-    p_ref, o1_ref, o2_ref, extra1_ref, extra2_ref, q1_ref, q2_ref, v_ref, dk_ref, dv_ref, keys_ref, values_ref, deltas
+    p_ref, o1_ref, o2_ref, q1_ref, q2_ref, v_ref, dk_ref, dv_ref, keys_ref, values_ref, deltas
 ):
-    deltas[0] = delta_of(extra1_ref)
-    deltas[1] = delta_of(extra2_ref)
+    deltas[0] = delta_of(o1_ref.at[FRAMES:, :])
+    deltas[1] = delta_of(o2_ref.at[FRAMES:, :])
     for n in range(STEP_PAIRS):
         c = lanes(n)
         v = v_ref[:, c]
         dk, dv = dk_ref[:, c], dv_ref[:, c]
         for m, (o_ref, q_ref) in enumerate(((o1_ref, q1_ref), (o2_ref, q2_ref))):
-            o, q = o_ref[:, c], q_ref[:, c]
+            place = pl.multiple_of(WIDTH * pl.program_id(0) + PAIR * n, PAIR)
+            o, q = o_ref[0:FRAMES, pl.ds(place, PAIR)], q_ref[:, c]
             for h in range(2):
                 at = 2 * n + h
                 o_h, q_h = one_head(o, h), one_head(q, h)
@@ -496,12 +500,16 @@
     return pl.pallas_call(
         later_grads_kernel,
         grid=(STEPS,),
-        in_specs=[heads_spec(2, FRAMES, FRAMES), one, one, DELTA_SPEC, DELTA_SPEC] + [one] * 5,
+        in_specs=[heads_spec(2, FRAMES, FRAMES), VMEM_SPEC, VMEM_SPEC] + [one] * 5,
         out_specs=[one, one],
         out_shape=(jax.ShapeDtypeStruct((FRAMES, D), BF16),) * 2,
         scratch_shapes=[pltpu.VMEM((2, HEADS, FRAMES), F32)],
         name="later_grads",
-    )(probs, *os, *os, *qs, v, dk, dv)
+    )(probs, *os, *qs, v, dk, dv)
+
+
+def near(x):
+    return pltpu.with_memory_space_constraint(x, pltpu.VMEM)
 
 
 def turned(x, distance):
@@ -534,7 +542,7 @@
     left = turned(own, 1)
     right = turned(own, -1)
     far = turned(left, 1)
-    sent_g = dispatch_g((block_left, block_right, block, block_far)).reshape(EXPERTS, EP * 8, WIDE)
+    sent_g = dispatch_g((near(block_left), near(block_right), block, near(block_far))).reshape(EXPERTS, EP * 8, WIDE)
     packed_g = exchanged(sent_g, "tm").reshape(EXPERTS, EP, 8, WIDE)
     filled = expert_forward(2, (own,), weight_gate, weight_up, ())
     filled = expert_forward(0, (left, right), weight_gate, weight_up, filled)
@@ -556,14 +564,14 @@
     stats1 = shifted(stats, -1)
     stats2 = shifted(stats, -2)
     later = later_probs(q1, q2, stats1, stats2, keys)
-    returned, later, probs, gate_grad, up_grad, down_grad = lax.optimization_barrier(
-        (returned, later, probs, gate_grad, up_grad, down_grad)
+    returned, probs, gate_grad, up_grad, down_grad = lax.optimization_barrier(
+        (returned, probs, gate_grad, up_grad, down_grad)
     )
-    stream_grad, sent_o = stream_gradient(returned, block, stream, gain, attn)
+    stream_grad, sent_o = stream_gradient(near(returned), block, stream, gain, attn)
     o1 = shifted(sent_o, -1)
     o2 = shifted(sent_o, -2)
     grad_q, own_k, own_v = own_grads(probs, sent_o, queries, both2, both1, keys, values)
-    grad_k, grad_v = later_grads(later, (o1, o2), (q1, q2), values, own_k, own_v)
+    grad_k, grad_v = later_grads(later, (near(o1), near(o2)), (q1, q2), values, own_k, own_v)
     return (
         grad_q,
         grad_k,

time: 251 us -> 245 us (0.976)
  local copies, waits for them, and re-layouts: 6.51 us -> 0.66 us
  Pallas kernels: 74.4 us -> 70.3 us
  starting transfers between devices: 60 us -> 62.8 us
    unnamed x30 -> x18, local copies, waits for them, and re-layouts: 6.51 us -> 0.66 us
    pallas_call x3, Pallas kernels: 21.3 us -> 18.6 us  [expert_forward(): pl.pallas_call(lambda *refs: forward_kernel(n, *refs), grid=(D // N_BLOCK...]
  transfers between devices with their start and end apart: 17 -> 17, of which waited for: 10 -> 10; matrix products, arithmetic and copies ran while one was open for 7% -> 8% of each run, Pallas kernels for 17% -> 18%
where the time goes in v3:
time: 245 us; the launch traced here: 244 us
  waiting for transfers between devices  91.3 us (37%)
  Pallas kernels  70.3 us (29%)
  starting transfers between devices  62.8 us (26%)
  matrix products  18.5 us (8%)
    ppermute x8, waiting for transfers between devices, shifted(): return lax.ppermute(x, ('tm', 'ep'), route)  58.2 us
    ppermute x6, waiting for transfers between devices, turned(): return lax.ppermute(x, 'ep', [(i, (i + distance) % EP) for i in range(EP)])  33.1 us
    all_to_all x3, starting transfers between devices, exchanged(): return lax.all_to_all(x, axes, split_axis=0, concat_axis=0, tiled=True)  28.9 us
    ppermute x8, starting transfers between devices, shifted(): return lax.ppermute(x, ('tm', 'ep'), route)  27.5 us
    pallas_call x3, Pallas kernels, expert_forward(): pl.pallas_call(lambda *refs: forward_kernel(n, *refs), grid=(D // N_BLOCK...  18.6 us
    pallas_call x1, Pallas kernels, expert_backward(): pl.pallas_call(backward_kernel, grid_spec=pltpu.PrefetchScalarGridSpec(nu...  18.1 us
    dot_general x1, matrix products, step(): up_grad = jnp.dot(x_rows.T, dup, preferred_element_type=F32)  8.48 us
    ppermute x6, starting transfers between devices, turned(): return lax.ppermute(x, 'ep', [(i, (i + distance) % EP) for i in range(EP)])  6.39 us
  transfers between devices with their start and end apart: 17, of which 10 were waited for; matrix products, arithmetic and copies ran while one was open for 8% of the time, Pallas kernels for 18%

profile of v3, /device:TPU:31, one launch (start us, length us, event | category | flops | bytes accessed | tf_op | source)
XLA Modules:
  0.0 244.4 jit_solution(17172333000671527337)
XLA Ops:
  0.6 2.9 %dispatch_x.1 = (bf16[256,1536]{1,0:T(8,128)(2,1)}, bf16[144,1024]{1,0:T(8,128)(2,1)}, bf16[2,128,1024]{2,1,0:T(8,128)(2,1)}) custom-call(bf16[128,1024]{1,0:T(8,128)(2,1)} %stream_ref.3, bf16[128,1024]{1,0:T(8,128)(2,1)} %grad_ref.1, f32[1,1024]{1,0:T(1,128)} %bitcast.39, s32[2,128]{1,0:T(2,128)} %bitcast.41, f32[2,128]{1,0:T(2,128)} %bitcast.42, ...), custom_call_target="tpu_custom_call" | custom-call | tf_op jit(solution)/shard_map/dispatch_x/pallas_call | solution.py:93
  3.5 8.6 %all-to-all-start.1 = ((bf16[32,8,1536]{2,1,0:T(8,128)(2,1)}), bf16[32,8,1536]{2,1,0:T(8,128)(2,1)S(1)}, u32[]{:S(2)}, u32[]{:S(2)}) async-start(bf16[32,8,1536]{2,1,0:T(8,128)(2,1)} %bitcast.38), calls=%async_computation.1 | async-start | bytes 1572864 | tf_op jit(solution)/shard_map/all_to_all | solution.py:526
  14.8 5.8 %collective-permute-done.refs_0_ = bf16[144,1024]{1,0:T(8,128)(2,1)S(1)} collective-permute-done((bf16[144,1024]{1,0:T(8,128)(2,1)}, bf16[144,1024]{1,0:T(8,128)(2,1)S(1)}, u32[]{:S(2)}, u32[]{:S(2)}) %collective-permute-start) | collective-permute-done | bytes 294944 | tf_op jit(solution)/shard_map/ppermute | solution.py:516
  22.0 5.8 %collective-permute-done.2.refs_3_ = bf16[144,1024]{1,0:T(8,128)(2,1)S(1)} collective-permute-done((bf16[144,1024]{1,0:T(8,128)(2,1)}, bf16[144,1024]{1,0:T(8,128)(2,1)S(1)}, u32[]{:S(2)}, u32[]{:S(2)}) %collective-permute-start.2) | collective-permute-done | bytes 294944 | tf_op jit(solution)/shard_map/ppermute | solution.py:516
  27.8 5.0 %dispatch_g.1 = bf16[32,4,8,1536]{3,2,1,0:T(8,128)(2,1)} custom-call(bf16[144,1024]{1,0:T(8,128)(2,1)S(1)} %collective-permute-done.refs_0_, bf16[144,1024]{1,0:T(8,128)(2,1)S(1)} %collective-permute-done.1.refs_1_, bf16[144,1024]{1,0:T(8,128)(2,1)} %get-tuple-element.41.refs_2_.block_ref, bf16[144,1024]{1,0:T(8,128)(2,1)S(1)} %collective-permute-done.2.refs_3_), custom_call_target="tpu_custom_call" | custom-call | tf_op jit(solution)/shard_map/dispatch_g/pallas_call | solution.py:138
  32.8 8.8 %all-to-all-start = ((bf16[32,32,1536]{2,1,0:T(8,128)(2,1)}), bf16[32,32,1536]{2,1,0:T(8,128)(2,1)}, u32[]{:S(2)}, u32[]{:S(2)}) async-start(bf16[32,32,1536]{2,1,0:T(8,128)(2,1)} %bitcast.35), calls=%async_computation | async-start | bytes 6291456 | tf_op jit(solution)/shard_map/all_to_all | solution.py:526
  43.2 17.3 %collective-permute-done.3.refs_0_ = bf16[256,1536]{1,0:T(8,128)(2,1)S(1)} collective-permute-done((bf16[256,1536]{1,0:T(8,128)(2,1)S(1)}, bf16[256,1536]{1,0:T(8,128)(2,1)S(1)}, u32[]{:S(2)}, u32[]{:S(2)}) %collective-permute-start.3) | collective-permute-done | bytes 786464 | tf_op jit(solution)/shard_map/ppermute | solution.py:516
  60.5 2.2 collective-permute-start.4
  62.7 5.4 %expert_forward.3 = (bf16[1536,1024]{1,0:T(8,128)(2,1)}, f32[1536,1024]{1,0:T(8,128)}, f32[1536,1024]{1,0:T(8,128)}, bf16[1536,1024]{1,0:T(8,128)(2,1)}) custom-call(bf16[256,1536]{1,0:T(8,128)(2,1)S(1)} %bitcast.26, bf16[1024,1024]{1,0:T(8,128)(2,1)} %bitcast.27, bf16[1024,1024]{1,0:T(8,128)(2,1)} %bitcast.31), custom_call_target="tpu_custom_call" | custom-call | tf_op jit(solution)/shard_map/expert_forward/pallas_call | solution.py:195
  68.2 7.7 %expert_forward.4 = (bf16[1536,1024]{1,0:T(8,128)(2,1)}, f32[1536,1024]{1,0:T(8,128)}, f32[1536,1024]{1,0:T(8,128)}, bf16[1536,1024]{1,0:T(8,128)(2,1)}) custom-call(bf16[256,1536]{1,0:T(8,128)(2,1)S(1)} %collective-permute-done.3.refs_0_, ...), custom_call_target="tpu_custom_call", output_to_operand_aliasing={{0}: (4, {}), {1}: (5, {}), {2}: (6, {}), {3}: (7, {})} | custom-call | tf_op jit(solution)/shard_map/expert_forward/pallas_call | solution.py:195
  75.8 2.7 %collective-permute-done.4.refs_0_ = bf16[256,1536]{1,0:T(8,128)(2,1)S(1)} collective-permute-done((bf16[256,1536]{1,0:T(8,128)(2,1)S(1)}, bf16[256,1536]{1,0:T(8,128)(2,1)S(1)}, u32[]{:S(2)}, u32[]{:S(2)}) %collective-permute-start.4) | collective-permute-done | bytes 786464 | tf_op jit(solution)/shard_map/ppermute | solution.py:516
  78.6 5.5 %expert_forward.5 = (bf16[1536,1024]{1,0:T(8,128)(2,1)}, f32[1536,1024]{1,0:T(8,128)}, f32[1536,1024]{1,0:T(8,128)}, bf16[1536,1024]{1,0:T(8,128)(2,1)}) custom-call(bf16[256,1536]{1,0:T(8,128)(2,1)S(1)} %collective-permute-done.4.refs_0_, bf16[1024,1024]{1,0:T(8,128)(2,1)} %bitcast.29, ...), custom_call_target="tpu_custom_call", output_to_operand_aliasing={{0}: (3, {}), {1}: (4, {}), {2}: (5, {}), {3}: (6, {})} | custom-call | tf_op jit(solution)/shard_map/expert_forward/pallas_call | solution.py:195
  84.0 18.1 %expert_backward.1 = (bf16[1536,1024]{1,0:T(8,128)(2,1)}, bf16[1536,1024]{1,0:T(8,128)(2,1)}, bf16[1536,1024]{1,0:T(8,128)(2,1)}, bf16[32,4,8,1536]{3,2,1,0:T(8,128)(2,1)}) custom-call(s32[1]{0:T(128)} %bitcast.column_ref, bf16[32,4,8,1536]{3,2,1,0:T(8,128)(2,1)} %bitcast.5.packed_ref, f32[1536,1024]{1,0:T(8,128)} %get-tuple-element.51.a_ref, ...), custom_call_target="tpu_custom_call" | custom-call | tf_op jit(solution)/shard_map/expert_backward/pallas_call | solution.py:235
  102.2 11.5 %all-to-all-start.2 = ((bf16[128,8,1536]{2,1,0:T(8,128)(2,1)}), bf16[128,8,1536]{2,1,0:T(8,128)(2,1)S(1)}, u32[]{:S(2)}, u32[]{:S(2)}) async-start(bf16[128,8,1536]{2,1,0:T(8,128)(2,1)} %bitcast.36), calls=%async_computation.2 | async-start | bytes 6291456 | tf_op jit(solution)/shard_map/all_to_all | solution.py:526
  113.7 4.3 %collective-permute-start.6 = (bf16[2,128,1024]{2,1,0:T(8,128)(2,1)}, bf16[2,128,1024]{2,1,0:T(8,128)(2,1)}, u32[]{:S(2)}, u32[]{:S(2)}) collective-permute-start(bf16[2,128,1024]{2,1,0:T(8,128)(2,1)} %get-tuple-element.54), channel_id=1, source_target_pairs={{0,2},{1,3},{2,4},{3,5},{4,6},{5,7},{6,8},{7,9},{8,10},{9,11},{10,... | collective-permute-start | bytes 1572872 | tf_op jit(solution)/shard_map/ppermute | solution.py:522
  118.0 4.0 %collective-permute-start.7 = (bf16[2,128,1024]{2,1,0:T(8,128)(2,1)}, bf16[2,128,1024]{2,1,0:T(8,128)(2,1)}, u32[]{:S(2)}, u32[]{:S(2)}) collective-permute-start(bf16[2,128,1024]{2,1,0:T(8,128)(2,1)} %get-tuple-element.54), channel_id=1, source_target_pairs={{0,1},{1,2},{2,3},{3,4},{4,5},{5,6},{6,7},{7,8},{8,9},{9,10},{10,1... | collective-permute-start | bytes 1572872 | tf_op jit(solution)/shard_map/ppermute | solution.py:522
  124.1 35.8 %collective-permute-done.6.both2_ref = bf16[2,128,1024]{2,1,0:T(8,128)(2,1)} collective-permute-done((bf16[2,128,1024]{2,1,0:T(8,128)(2,1)}, bf16[2,128,1024]{2,1,0:T(8,128)(2,1)}, u32[]{:S(2)}, u32[]{:S(2)}) %collective-permute-start.6) | collective-permute-done | bytes 524320 | tf_op jit(solution)/shard_map/ppermute | solution.py:522
  159.9 10.6 %collective-permute-done.7.both1_ref = bf16[2,128,1024]{2,1,0:T(8,128)(2,1)} collective-permute-done((bf16[2,128,1024]{2,1,0:T(8,128)(2,1)}, bf16[2,128,1024]{2,1,0:T(8,128)(2,1)}, u32[]{:S(2)}, u32[]{:S(2)}) %collective-permute-start.7) | collective-permute-done | bytes 524320 | tf_op jit(solution)/shard_map/ppermute | solution.py:522
  170.5 5.9 %attention_probs.1 = (f32[16,384,128]{2,1,0:T(8,128)}, f32[16,8,128]{2,1,0:T(8,128)}, f32[128,1024]{1,0:T(8,128)}) custom-call(s32[1]{0:T(128)} %bitcast.13.first_ref, bf16[128,1024]{1,0:T(8,128)(2,1)} %q_ref.3, bf16[2,128,1024]{2,1,0:T(8,128)(2,1)} %collective-permute-done.6.both2_ref, bf16[2,128,1024]{2,1,0:T(8,128)(2,1)} %collective-permute-done.7.both1_ref, ...), custom_call_target="tpu_custom_call" | custom-call | tf_op jit(solution)/shard_map/attention_probs/pallas_call | solution.py:315
  176.5 8.5 %fusion.1 = f32[1024,1024]{1,0:T(8,128)} fusion(bf16[1536,1024]{1,0:T(8,128)(2,1)} %get-tuple-element.56, bf16[1536,1024]{1,0:T(8,128)(2,1)} %get-tuple-element.58), kind=kOutput, calls=%fused_computation.1 | convolution fusion | flops 3221225472 | bytes 10485760 | tf_op jit(solution)/shard_map/dot_general | solution.py:559
  185.0 5.0 %fusion = f32[1024,1024]{1,0:T(8,128)} fusion(bf16[1536,1024]{1,0:T(8,128)(2,1)S(1)} %copy-done, bf16[1536,1024]{1,0:T(8,128)(2,1)S(1)} %copy-done.7), kind=kOutput, calls=%fused_computation | convolution fusion | flops 3221225472 | bytes 10485760 | tf_op jit(solution)/shard_map/dot_general | solution.py:558
  190.0 5.0 %fusion.2 = f32[1024,1024]{1,0:T(8,128)} fusion(bf16[1536,1024]{1,0:T(8,128)(2,1)S(1)} %copy-done.1, bf16[1536,1024]{1,0:T(8,128)(2,1)S(1)} %copy-done.6), kind=kOutput, calls=%fused_computation.2 | convolution fusion | flops 3221225472 | bytes 10485760 | tf_op jit(solution)/shard_map/dot_general | solution.py:560
  195.0 4.8 %stream_gradient.1 = (bf16[128,1024]{1,0:T(8,128)(2,1)}, bf16[144,1024]{1,0:T(8,128)(2,1)}) custom-call(bf16[1024,1536]{1,0:T(8,128)(2,1)S(1)} %bitcast.23, bf16[144,1024]{1,0:T(8,128)(2,1)} %get-tuple-element.41.refs_2_.block_ref, bf16[128,1024]{1,0:T(8,128)(2,1)} %stream_ref.3, f32[1,1024]{1,0:T(1,128)} %bitcast.40, f32[128,1024]{1,0:T(8,128)} %get-tuple-element.63.attn_ref), custom_call_target="tpu_custom_call" | custom-call | tf_op jit(solution)/shard_map/stream_gradient/pallas_call | solution.py:408
  199.8 2.2 collective-permute-start.12
  202.0 5.2 %collective-permute-start.13 = (bf16[144,1024]{1,0:T(8,128)(2,1)}, bf16[144,1024]{1,0:T(8,128)(2,1)S(1)}, u32[]{:S(2)}, u32[]{:S(2)}) collective-permute-start(bf16[144,1024]{1,0:T(8,128)(2,1)} %get-tuple-element.64.o_ref.extra_ref), channel_id=1, source_target_pairs={{2,0},{3,1},{4,2},{5,3},{6,4},{7,5},{8,6},{9,7},{10,8},{11,9},{12,... | collective-permute-start | bytes 884744 | tf_op jit(solution)/shard_map/ppermute | solution.py:522
  207.2 2.7 %collective-permute-start.9 = (bf16[128,1024]{1,0:T(8,128)(2,1)}, bf16[128,1024]{1,0:T(8,128)(2,1)S(1)}, u32[]{:S(2)}, u32[]{:S(2)}) collective-permute-start(bf16[128,1024]{1,0:T(8,128)(2,1)} %q_ref.3), channel_id=1, source_target_pairs={{2,0},{3,1},{4,2},{5,3},{6,4},{7,5},{8,6},{9,7},{10,8},{11,9},{12,... | collective-permute-start | bytes 786440 | tf_op jit(solution)/shard_map/ppermute | solution.py:522
  209.9 2.2 collective-permute-start.10
  212.1 4.9 %collective-permute-start.11 = (f32[16,8,128]{2,1,0:T(8,128)S(1)}, f32[16,8,128]{2,1,0:T(8,128)S(1)}, u32[]{:S(2)}, u32[]{:S(2)}) collective-permute-start(f32[16,8,128]{2,1,0:T(8,128)S(1)} %copy-done.8), channel_id=1, source_target_pairs={{2,0},{3,1},{4,2},{5,3},{6,4},{7,5},{8,6},{9,7},{10,8},{11,9},{12,... | collective-permute-start | bytes 196616 | tf_op jit(solution)/shard_map/ppermute | solution.py:522
  217.0 10.4 %collective-permute-done.9.q2_ref = bf16[128,1024]{1,0:T(8,128)(2,1)S(1)} collective-permute-done((bf16[128,1024]{1,0:T(8,128)(2,1)}, bf16[128,1024]{1,0:T(8,128)(2,1)S(1)}, u32[]{:S(2)}, u32[]{:S(2)}) %collective-permute-start.9) | collective-permute-done | bytes 262176 | tf_op jit(solution)/shard_map/ppermute | solution.py:522
  229.4 4.2 %later_probs.1.p_ref = f32[16,2,128,128]{3,2,1,0:T(8,128)} custom-call(bf16[128,1024]{1,0:T(8,128)(2,1)} %copy-done.2, bf16[128,1024]{1,0:T(8,128)(2,1)} %copy-done.3, f32[16,8,128]{2,1,0:T(8,128)} %copy-done.4, f32[16,8,128]{2,1,0:T(8,128)} %copy-done.5, bf16[128,1024]{1,0:T(8,128)(2,1)} %k_ref.7), custom_call_target="tpu_custom_call" | custom-call | tf_op jit(solution)/shard_map/later_probs/pallas_call | solution.py:349
  233.6 5.9 %own_grads.1 = (bf16[128,1024]{1,0:T(8,128)(2,1)}, f32[128,1024]{1,0:T(8,128)}, f32[128,1024]{1,0:T(8,128)}) custom-call(f32[16,384,128]{2,1,0:T(8,128)} %get-tuple-element.61.p_ref, bf16[144,1024]{1,0:T(8,128)(2,1)} %get-tuple-element.64.o_ref.extra_ref, bf16[144,1024]{1,0:T(8,128)(2,1)} %get-tuple-element.64.o_ref.extra_ref, bf16[128,1024]{1,0:T(8,128)(2,1)} %q_ref.3, ...), custom_call_target="tpu_custom_call" | custom-call | tf_op jit(solution)/shard_map/own_grads/pallas_call | solution.py:463
  239.5 4.9 %later_grads.1 = (bf16[128,1024]{1,0:T(8,128)(2,1)}, bf16[128,1024]{1,0:T(8,128)(2,1)}) custom-call(f32[16,2,128,128]{3,2,1,0:T(8,128)} %later_probs.1.p_ref, bf16[144,1024]{1,0:T(8,128)(2,1)S(1)} %collective-permute-done.12.o1_ref, bf16[144,1024]{1,0:T(8,128)(2,1)S(1)} %collective-permute-done.13.o2_ref, bf16[128,1024]{1,0:T(8,128)(2,1)} %copy-done.2, ...), custom_call_target="tpu_custom_call" | custom-call | tf_op jit(solution)/shard_map/later_grads/pallas_call | solution.py:500
  (34 shorter events, 9.8 us)
Async XLA Ops:
  3.5 29.3 %all-to-all-start.1 = ((bf16[32,8,1536]{2,1,0:T(8,128)(2,1)}), bf16[32,8,1536]{2,1,0:T(8,128)(2,1)S(1)}, u32[]{:S(2)}, u32[]{:S(2)}) async-start(bf16[32,8,1536]{2,1,0:T(8,128)(2,1)} %bitcast.38), calls=%async_computation.1 | async-start | bytes 1572864 | tf_op jit(solution)/shard_map/all_to_all | solution.py:526
  12.1 8.5 %collective-permute-start = (bf16[144,1024]{1,0:T(8,128)(2,1)}, bf16[144,1024]{1,0:T(8,128)(2,1)S(1)}, u32[]{:S(2)}, u32[]{:S(2)}) collective-permute-start(bf16[144,1024]{1,0:T(8,128)(2,1)} %get-tuple-element.41.refs_2_.block_ref), channel_id=1, source_target_pairs={{0,1},{1,2},{2,3},{3,0},{4,5},{5,6},{6,7},{7,4},{8,9},{9,10},{10,1... | collective-permute-start | bytes 884744 | tf_op jit(solution)/shard_map/ppermute | solution.py:516
  12.4 9.6 %collective-permute-start.1 = (bf16[144,1024]{1,0:T(8,128)(2,1)}, bf16[144,1024]{1,0:T(8,128)(2,1)S(1)}, u32[]{:S(2)}, u32[]{:S(2)}) collective-permute-start(bf16[144,1024]{1,0:T(8,128)(2,1)} %get-tuple-element.41.refs_2_.block_ref), channel_id=1, source_target_pairs={{0,3},{1,0},{2,1},{3,2},{4,7},{5,4},{6,5},{7,6},{8,11},{9,8},{10,9... | collective-permute-start | bytes 884744 | tf_op jit(solution)/shard_map/ppermute | solution.py:516
  13.7 14.1 %collective-permute-start.2 = (bf16[144,1024]{1,0:T(8,128)(2,1)}, bf16[144,1024]{1,0:T(8,128)(2,1)S(1)}, u32[]{:S(2)}, u32[]{:S(2)}) collective-permute-start(bf16[144,1024]{1,0:T(8,128)(2,1)} %get-tuple-element.41.refs_2_.block_ref), channel_id=1, source_target_pairs={{0,2},{1,3},{2,0},{3,1},{4,6},{5,7},{6,4},{7,5},{8,10},{9,11},{10,... | collective-permute-start | bytes 884744 | tf_op jit(solution)/shard_map/ppermute | solution.py:516
  32.8 51.2 %all-to-all-start = ((bf16[32,32,1536]{2,1,0:T(8,128)(2,1)}), bf16[32,32,1536]{2,1,0:T(8,128)(2,1)}, u32[]{:S(2)}, u32[]{:S(2)}) async-start(bf16[32,32,1536]{2,1,0:T(8,128)(2,1)} %bitcast.35), calls=%async_computation | async-start | bytes 6291456 | tf_op jit(solution)/shard_map/all_to_all | solution.py:526
  41.6 18.9 %collective-permute-start.3 = (bf16[256,1536]{1,0:T(8,128)(2,1)S(1)}, bf16[256,1536]{1,0:T(8,128)(2,1)S(1)}, u32[]{:S(2)}, u32[]{:S(2)}) collective-permute-start(bf16[256,1536]{1,0:T(8,128)(2,1)S(1)} %bitcast.24), channel_id=1, source_target_pairs={{0,1},{1,2},{2,3},{3,0},{4,5},{5,6},{6,7},{7,4},{8,9},{9,10},{10,1... | collective-permute-start | bytes 2359304 | tf_op jit(solution)/shard_map/ppermute | solution.py:516
  42.7 25.5 %collective-permute-start.5 = (bf16[256,1536]{1,0:T(8,128)(2,1)S(1)}, bf16[256,1536]{1,0:T(8,128)(2,1)S(1)}, u32[]{:S(2)}, u32[]{:S(2)}) collective-permute-start(bf16[256,1536]{1,0:T(8,128)(2,1)S(1)} %bitcast.25), channel_id=1, source_target_pairs={{0,3},{1,0},{2,1},{3,2},{4,7},{5,4},{6,5},{7,6},{8,11},{9,8},{10,9... | collective-permute-start | bytes 2359304 | tf_op jit(solution)/shard_map/ppermute | solution.py:516
  60.5 18.1 %collective-permute-start.4 = (bf16[256,1536]{1,0:T(8,128)(2,1)S(1)}, bf16[256,1536]{1,0:T(8,128)(2,1)S(1)}, u32[]{:S(2)}, u32[]{:S(2)}) collective-permute-start(bf16[256,1536]{1,0:T(8,128)(2,1)S(1)} %collective-permute-done.3.refs_0_), channel_id=1, source_target_pairs={{0,1},{1,2},{2,3},{3,0},{4,5},{5,6},{6,7},{7,4},{8,9},{9,10},{10,1... | collective-permute-start | bytes 2359304 | tf_op jit(solution)/shard_map/ppermute | solution.py:516
  102.2 92.8 %all-to-all-start.2 = ((bf16[128,8,1536]{2,1,0:T(8,128)(2,1)}), bf16[128,8,1536]{2,1,0:T(8,128)(2,1)S(1)}, u32[]{:S(2)}, u32[]{:S(2)}) async-start(bf16[128,8,1536]{2,1,0:T(8,128)(2,1)} %bitcast.36), calls=%async_computation.2 | async-start | bytes 6291456 | tf_op jit(solution)/shard_map/all_to_all | solution.py:526
  113.7 46.2 %collective-permute-start.6 = (bf16[2,128,1024]{2,1,0:T(8,128)(2,1)}, bf16[2,128,1024]{2,1,0:T(8,128)(2,1)}, u32[]{:S(2)}, u32[]{:S(2)}) collective-permute-start(bf16[2,128,1024]{2,1,0:T(8,128)(2,1)} %get-tuple-element.54), channel_id=1, source_target_pairs={{0,2},{1,3},{2,4},{3,5},{4,6},{5,7},{6,8},{7,9},{8,10},{9,11},{10,... | collective-permute-start | bytes 1572872 | tf_op jit(solution)/shard_map/ppermute | solution.py:522
  118.0 52.5 %collective-permute-start.7 = (bf16[2,128,1024]{2,1,0:T(8,128)(2,1)}, bf16[2,128,1024]{2,1,0:T(8,128)(2,1)}, u32[]{:S(2)}, u32[]{:S(2)}) collective-permute-start(bf16[2,128,1024]{2,1,0:T(8,128)(2,1)} %get-tuple-element.54), channel_id=1, source_target_pairs={{0,1},{1,2},{2,3},{3,4},{4,5},{5,6},{6,7},{7,8},{8,9},{9,10},{10,1... | collective-permute-start | bytes 1572872 | tf_op jit(solution)/shard_map/ppermute | solution.py:522
  122.0 90.1 %collective-permute-start.8 = (bf16[128,1024]{1,0:T(8,128)(2,1)}, bf16[128,1024]{1,0:T(8,128)(2,1)S(1)}, u32[]{:S(2)}, u32[]{:S(2)}) collective-permute-start(bf16[128,1024]{1,0:T(8,128)(2,1)} %q_ref.3), channel_id=1, source_target_pairs={{1,0},{2,1},{3,2},{4,3},{5,4},{6,5},{7,6},{8,7},{9,8},{10,9},{11,1... | collective-permute-start | bytes 786440 | tf_op jit(solution)/shard_map/ppermute | solution.py:522
  176.5 8.5 %copy-start = (bf16[1536,1024]{1,0:T(8,128)(2,1)S(1)}, bf16[1536,1024]{1,0:T(8,128)(2,1)}, u32[]{:S(2)}) copy-start(bf16[1536,1024]{1,0:T(8,128)(2,1)} %get-tuple-element.56) | copy-start | bytes 9437188
  176.5 8.5 %copy-start.7 = (bf16[1536,1024]{1,0:T(8,128)(2,1)S(1)}, bf16[1536,1024]{1,0:T(8,128)(2,1)}, u32[]{:S(2)}) copy-start(bf16[1536,1024]{1,0:T(8,128)(2,1)} %get-tuple-element.57) | copy-start | bytes 9437188
  185.0 5.0 %copy-start.1 = (bf16[1536,1024]{1,0:T(8,128)(2,1)S(1)}, bf16[1536,1024]{1,0:T(8,128)(2,1)}, u32[]{:S(2)}) copy-start(bf16[1536,1024]{1,0:T(8,128)(2,1)} %get-tuple-element.59) | copy-start | bytes 9437188
  185.0 5.0 %copy-start.6 = (bf16[1536,1024]{1,0:T(8,128)(2,1)S(1)}, bf16[1536,1024]{1,0:T(8,128)(2,1)}, u32[]{:S(2)}) copy-start(bf16[1536,1024]{1,0:T(8,128)(2,1)} %get-tuple-element.60) | copy-start | bytes 9437188
  195.0 14.9 %copy-start.8 = (f32[16,8,128]{2,1,0:T(8,128)S(1)}, f32[16,8,128]{2,1,0:T(8,128)}, u32[]{:S(2)}) copy-start(f32[16,8,128]{2,1,0:T(8,128)} %get-tuple-element.66) | copy-start | bytes 196612
  199.8 39.7 %collective-permute-start.12 = (bf16[144,1024]{1,0:T(8,128)(2,1)}, bf16[144,1024]{1,0:T(8,128)(2,1)S(1)}, u32[]{:S(2)}, u32[]{:S(2)}) collective-permute-start(bf16[144,1024]{1,0:T(8,128)(2,1)} %get-tuple-element.64.o_ref.extra_ref), channel_id=1, source_target_pairs={{1,0},{2,1},{3,2},{4,3},{5,4},{6,5},{7,6},{8,7},{9,8},{10,9},{11,1... | collective-permute-start | bytes 884744 | tf_op jit(solution)/shard_map/ppermute | solution.py:522
  202.0 37.5 %collective-permute-start.13 = (bf16[144,1024]{1,0:T(8,128)(2,1)}, bf16[144,1024]{1,0:T(8,128)(2,1)S(1)}, u32[]{:S(2)}, u32[]{:S(2)}) collective-permute-start(bf16[144,1024]{1,0:T(8,128)(2,1)} %get-tuple-element.64.o_ref.extra_ref), channel_id=1, source_target_pairs={{2,0},{3,1},{4,2},{5,3},{6,4},{7,5},{8,6},{9,7},{10,8},{11,9},{12,... | collective-permute-start | bytes 884744 | tf_op jit(solution)/shard_map/ppermute | solution.py:522
  207.2 20.2 %collective-permute-start.9 = (bf16[128,1024]{1,0:T(8,128)(2,1)}, bf16[128,1024]{1,0:T(8,128)(2,1)S(1)}, u32[]{:S(2)}, u32[]{:S(2)}) collective-permute-start(bf16[128,1024]{1,0:T(8,128)(2,1)} %q_ref.3), channel_id=1, source_target_pairs={{2,0},{3,1},{4,2},{5,3},{6,4},{7,5},{8,6},{9,7},{10,8},{11,9},{12,... | collective-permute-start | bytes 786440 | tf_op jit(solution)/shard_map/ppermute | solution.py:522
  209.9 18.1 %collective-permute-start.10 = (f32[16,8,128]{2,1,0:T(8,128)S(1)}, f32[16,8,128]{2,1,0:T(8,128)S(1)}, u32[]{:S(2)}, u32[]{:S(2)}) collective-permute-start(f32[16,8,128]{2,1,0:T(8,128)S(1)} %copy-done.8), channel_id=1, source_target_pairs={{1,0},{2,1},{3,2},{4,3},{5,4},{6,5},{7,6},{8,7},{9,8},{10,9},{11,1... | collective-permute-start | bytes 196616 | tf_op jit(solution)/shard_map/ppermute | solution.py:522
  212.1 16.7 %copy-start.2 = (bf16[128,1024]{1,0:T(8,128)(2,1)}, bf16[128,1024]{1,0:T(8,128)(2,1)S(1)}, u32[]{:S(2)}) copy-start(bf16[128,1024]{1,0:T(8,128)(2,1)S(1)} %collective-permute-done.8.q1_ref) | copy-start | bytes 786436
  212.1 16.7 %collective-permute-start.11 = (f32[16,8,128]{2,1,0:T(8,128)S(1)}, f32[16,8,128]{2,1,0:T(8,128)S(1)}, u32[]{:S(2)}, u32[]{:S(2)}) collective-permute-start(f32[16,8,128]{2,1,0:T(8,128)S(1)} %copy-done.8), channel_id=1, source_target_pairs={{2,0},{3,1},{4,2},{5,3},{6,4},{7,5},{8,6},{9,7},{10,8},{11,9},{12,... | collective-permute-start | bytes 196616 | tf_op jit(solution)/shard_map/ppermute | solution.py:522
  227.4 1.4 copy-start.3
  228.0 0.8 copy-start.4
  228.8 0.6 copy-start.5

commit v4 on v3

--- a/solution.py
+++ b/solution.py
@@ -330,6 +330,7 @@
 
 
 def later_probs_kernel(q1_ref, q2_ref, stats1_ref, stats2_ref, k_ref, p_ref):
+    start = STEP_HEADS * pl.program_id(0)
     shape = (FRAMES, FRAMES)
     allowed = iota(shape, 0) >= jnp.where(iota(shape, 1) >= SPAN, SPAN, 0)
     for n in range(STEP_PAIRS):
@@ -341,15 +342,15 @@
                 scores = matmul(k, one_head(q, h), NT) * SCALE
                 if m == 1:
                     scores = jnp.where(allowed, scores, -jnp.inf)
-                p_ref[at, m] = jnp.exp(scores - stats_ref[at, 0:1, :]) * stats_ref[at, 1:2, :]
+                p_ref[at, m] = jnp.exp(scores - stats_ref[start + at, 0:1, :]) * stats_ref[start + at, 1:2, :]
 
 
 def later_probs(q1, q2, stats1, stats2, k):
-    one, stats = columns_spec(FRAMES), heads_spec(8, FRAMES)
+    one = columns_spec(FRAMES)
     return pl.pallas_call(
         later_probs_kernel,
         grid=(STEPS,),
-        in_specs=[one, one, stats, stats, one],
+        in_specs=[one, one, VMEM_SPEC, VMEM_SPEC, one],
         out_specs=heads_spec(2, FRAMES, FRAMES),
         out_shape=jax.ShapeDtypeStruct((HEADS, 2, FRAMES, FRAMES), F32),
         name="later_probs",
@@ -563,7 +564,7 @@
     probs, stats, attn = attention_probs(first, queries, both2, both1, keys, values)
     stats1 = shifted(stats, -1)
     stats2 = shifted(stats, -2)
-    later = later_probs(q1, q2, stats1, stats2, keys)
+    later = later_probs(q1, q2, near(stats1), near(stats2), keys)
     returned, probs, gate_grad, up_grad, down_grad = lax.optimization_barrier(
         (returned, probs, gate_grad, up_grad, down_grad)
     )

time: 245 us -> 245 us (level)
  no operation moved by 1% of the time
where the time goes in v4:
time: 245 us; the launch traced here: 244 us
  waiting for transfers between devices  91.3 us (37%)
  Pallas kernels  70.2 us (29%)
  starting transfers between devices  62.9 us (26%)
  matrix products  18.5 us (8%)
    ppermute x8, waiting for transfers between devices, shifted(): return lax.ppermute(x, ('tm', 'ep'), route)  58.2 us
    ppermute x6, waiting for transfers between devices, turned(): return lax.ppermute(x, 'ep', [(i, (i + distance) % EP) for i in range(EP)])  33.1 us
    all_to_all x3, starting transfers between devices, exchanged(): return lax.all_to_all(x, axes, split_axis=0, concat_axis=0, tiled=True)  29 us
    ppermute x8, starting transfers between devices, shifted(): return lax.ppermute(x, ('tm', 'ep'), route)  27.5 us
    pallas_call x3, Pallas kernels, expert_forward(): pl.pallas_call(lambda *refs: forward_kernel(n, *refs), grid=(D // N_BLOCK...  18.6 us
    pallas_call x1, Pallas kernels, expert_backward(): pl.pallas_call(backward_kernel, grid_spec=pltpu.PrefetchScalarGridSpec(nu...  18 us
    dot_general x1, matrix products, step(): up_grad = jnp.dot(x_rows.T, dup, preferred_element_type=F32)  8.47 us
    ppermute x6, starting transfers between devices, turned(): return lax.ppermute(x, 'ep', [(i, (i + distance) % EP) for i in range(EP)])  6.39 us
  transfers between devices with their start and end apart: 17, of which 10 were waited for; matrix products, arithmetic and copies ran while one was open for 8% of the time, Pallas kernels for 18%

profile of v4, /device:TPU:31, one launch (start us, length us, event | category | flops | bytes accessed | tf_op | source)
XLA Modules:
  0.0 243.7 jit_solution(9302213764159714567)
XLA Ops:
  0.6 2.9 %dispatch_x.1 = (bf16[256,1536]{1,0:T(8,128)(2,1)}, bf16[144,1024]{1,0:T(8,128)(2,1)}, bf16[2,128,1024]{2,1,0:T(8,128)(2,1)}) custom-call(bf16[128,1024]{1,0:T(8,128)(2,1)} %stream_ref.3, bf16[128,1024]{1,0:T(8,128)(2,1)} %grad_ref.1, f32[1,1024]{1,0:T(1,128)} %bitcast.39, s32[2,128]{1,0:T(2,128)} %bitcast.41, f32[2,128]{1,0:T(2,128)} %bitcast.42, ...), custom_call_target="tpu_custom_call" | custom-call | tf_op jit(solution)/shard_map/dispatch_x/pallas_call | solution.py:93
  3.5 8.6 %all-to-all-start.1 = ((bf16[32,8,1536]{2,1,0:T(8,128)(2,1)}), bf16[32,8,1536]{2,1,0:T(8,128)(2,1)S(1)}, u32[]{:S(2)}, u32[]{:S(2)}) async-start(bf16[32,8,1536]{2,1,0:T(8,128)(2,1)} %bitcast.38), calls=%async_computation.1 | async-start | bytes 1572864 | tf_op jit(solution)/shard_map/all_to_all | solution.py:527
  14.8 5.8 %collective-permute-done.refs_0_ = bf16[144,1024]{1,0:T(8,128)(2,1)S(1)} collective-permute-done((bf16[144,1024]{1,0:T(8,128)(2,1)}, bf16[144,1024]{1,0:T(8,128)(2,1)S(1)}, u32[]{:S(2)}, u32[]{:S(2)}) %collective-permute-start) | collective-permute-done | bytes 294944 | tf_op jit(solution)/shard_map/ppermute | solution.py:517
  22.0 5.8 %collective-permute-done.2.refs_3_ = bf16[144,1024]{1,0:T(8,128)(2,1)S(1)} collective-permute-done((bf16[144,1024]{1,0:T(8,128)(2,1)}, bf16[144,1024]{1,0:T(8,128)(2,1)S(1)}, u32[]{:S(2)}, u32[]{:S(2)}) %collective-permute-start.2) | collective-permute-done | bytes 294944 | tf_op jit(solution)/shard_map/ppermute | solution.py:517
  27.8 5.0 %dispatch_g.1 = bf16[32,4,8,1536]{3,2,1,0:T(8,128)(2,1)} custom-call(bf16[144,1024]{1,0:T(8,128)(2,1)S(1)} %collective-permute-done.refs_0_, bf16[144,1024]{1,0:T(8,128)(2,1)S(1)} %collective-permute-done.1.refs_1_, bf16[144,1024]{1,0:T(8,128)(2,1)} %get-tuple-element.41.refs_2_.block_ref, bf16[144,1024]{1,0:T(8,128)(2,1)S(1)} %collective-permute-done.2.refs_3_), custom_call_target="tpu_custom_call" | custom-call | tf_op jit(solution)/shard_map/dispatch_g/pallas_call | solution.py:138
  32.8 8.8 %all-to-all-start = ((bf16[32,32,1536]{2,1,0:T(8,128)(2,1)}), bf16[32,32,1536]{2,1,0:T(8,128)(2,1)}, u32[]{:S(2)}, u32[]{:S(2)}) async-start(bf16[32,32,1536]{2,1,0:T(8,128)(2,1)} %bitcast.35), calls=%async_computation | async-start | bytes 6291456 | tf_op jit(solution)/shard_map/all_to_all | solution.py:527
  43.2 17.3 %collective-permute-done.3.refs_0_ = bf16[256,1536]{1,0:T(8,128)(2,1)S(1)} collective-permute-done((bf16[256,1536]{1,0:T(8,128)(2,1)S(1)}, bf16[256,1536]{1,0:T(8,128)(2,1)S(1)}, u32[]{:S(2)}, u32[]{:S(2)}) %collective-permute-start.3) | collective-permute-done | bytes 786464 | tf_op jit(solution)/shard_map/ppermute | solution.py:517
  60.5 2.2 collective-permute-start.4
  62.7 5.5 %expert_forward.3 = (bf16[1536,1024]{1,0:T(8,128)(2,1)}, f32[1536,1024]{1,0:T(8,128)}, f32[1536,1024]{1,0:T(8,128)}, bf16[1536,1024]{1,0:T(8,128)(2,1)}) custom-call(bf16[256,1536]{1,0:T(8,128)(2,1)S(1)} %bitcast.26, bf16[1024,1024]{1,0:T(8,128)(2,1)} %bitcast.27, bf16[1024,1024]{1,0:T(8,128)(2,1)} %bitcast.31), custom_call_target="tpu_custom_call" | custom-call | tf_op jit(solution)/shard_map/expert_forward/pallas_call | solution.py:195
  68.2 7.7 %expert_forward.4 = (bf16[1536,1024]{1,0:T(8,128)(2,1)}, f32[1536,1024]{1,0:T(8,128)}, f32[1536,1024]{1,0:T(8,128)}, bf16[1536,1024]{1,0:T(8,128)(2,1)}) custom-call(bf16[256,1536]{1,0:T(8,128)(2,1)S(1)} %collective-permute-done.3.refs_0_, ...), custom_call_target="tpu_custom_call", output_to_operand_aliasing={{0}: (4, {}), {1}: (5, {}), {2}: (6, {}), {3}: (7, {})} | custom-call | tf_op jit(solution)/shard_map/expert_forward/pallas_call | solution.py:195
  75.8 2.7 %collective-permute-done.4.refs_0_ = bf16[256,1536]{1,0:T(8,128)(2,1)S(1)} collective-permute-done((bf16[256,1536]{1,0:T(8,128)(2,1)S(1)}, bf16[256,1536]{1,0:T(8,128)(2,1)S(1)}, u32[]{:S(2)}, u32[]{:S(2)}) %collective-permute-start.4) | collective-permute-done | bytes 786464 | tf_op jit(solution)/shard_map/ppermute | solution.py:517
  78.6 5.5 %expert_forward.5 = (bf16[1536,1024]{1,0:T(8,128)(2,1)}, f32[1536,1024]{1,0:T(8,128)}, f32[1536,1024]{1,0:T(8,128)}, bf16[1536,1024]{1,0:T(8,128)(2,1)}) custom-call(bf16[256,1536]{1,0:T(8,128)(2,1)S(1)} %collective-permute-done.4.refs_0_, bf16[1024,1024]{1,0:T(8,128)(2,1)} %bitcast.29, ...), custom_call_target="tpu_custom_call", output_to_operand_aliasing={{0}: (3, {}), {1}: (4, {}), {2}: (5, {}), {3}: (6, {})} | custom-call | tf_op jit(solution)/shard_map/expert_forward/pallas_call | solution.py:195
  84.0 18.0 %expert_backward.1 = (bf16[1536,1024]{1,0:T(8,128)(2,1)}, bf16[1536,1024]{1,0:T(8,128)(2,1)}, bf16[1536,1024]{1,0:T(8,128)(2,1)}, bf16[32,4,8,1536]{3,2,1,0:T(8,128)(2,1)}) custom-call(s32[1]{0:T(128)} %bitcast.column_ref, bf16[32,4,8,1536]{3,2,1,0:T(8,128)(2,1)} %bitcast.5.packed_ref, f32[1536,1024]{1,0:T(8,128)} %get-tuple-element.51.a_ref, ...), custom_call_target="tpu_custom_call" | custom-call | tf_op jit(solution)/shard_map/expert_backward/pallas_call | solution.py:235
  102.1 11.6 %all-to-all-start.2 = ((bf16[128,8,1536]{2,1,0:T(8,128)(2,1)}), bf16[128,8,1536]{2,1,0:T(8,128)(2,1)S(1)}, u32[]{:S(2)}, u32[]{:S(2)}) async-start(bf16[128,8,1536]{2,1,0:T(8,128)(2,1)} %bitcast.36), calls=%async_computation.2 | async-start | bytes 6291456 | tf_op jit(solution)/shard_map/all_to_all | solution.py:527
  113.7 4.3 %collective-permute-start.6 = (bf16[2,128,1024]{2,1,0:T(8,128)(2,1)}, bf16[2,128,1024]{2,1,0:T(8,128)(2,1)}, u32[]{:S(2)}, u32[]{:S(2)}) collective-permute-start(bf16[2,128,1024]{2,1,0:T(8,128)(2,1)} %get-tuple-element.54), channel_id=1, source_target_pairs={{0,2},{1,3},{2,4},{3,5},{4,6},{5,7},{6,8},{7,9},{8,10},{9,11},{10,... | collective-permute-start | bytes 1572872 | tf_op jit(solution)/shard_map/ppermute | solution.py:523
  118.0 4.0 %collective-permute-start.7 = (bf16[2,128,1024]{2,1,0:T(8,128)(2,1)}, bf16[2,128,1024]{2,1,0:T(8,128)(2,1)}, u32[]{:S(2)}, u32[]{:S(2)}) collective-permute-start(bf16[2,128,1024]{2,1,0:T(8,128)(2,1)} %get-tuple-element.54), channel_id=1, source_target_pairs={{0,1},{1,2},{2,3},{3,4},{4,5},{5,6},{6,7},{7,8},{8,9},{9,10},{10,1... | collective-permute-start | bytes 1572872 | tf_op jit(solution)/shard_map/ppermute | solution.py:523
  124.1 35.8 %collective-permute-done.6.both2_ref = bf16[2,128,1024]{2,1,0:T(8,128)(2,1)} collective-permute-done((bf16[2,128,1024]{2,1,0:T(8,128)(2,1)}, bf16[2,128,1024]{2,1,0:T(8,128)(2,1)}, u32[]{:S(2)}, u32[]{:S(2)}) %collective-permute-start.6) | collective-permute-done | bytes 524320 | tf_op jit(solution)/shard_map/ppermute | solution.py:523
  159.9 10.6 %collective-permute-done.7.both1_ref = bf16[2,128,1024]{2,1,0:T(8,128)(2,1)} collective-permute-done((bf16[2,128,1024]{2,1,0:T(8,128)(2,1)}, bf16[2,128,1024]{2,1,0:T(8,128)(2,1)}, u32[]{:S(2)}, u32[]{:S(2)}) %collective-permute-start.7) | collective-permute-done | bytes 524320 | tf_op jit(solution)/shard_map/ppermute | solution.py:523
  170.6 5.9 %attention_probs.1 = (f32[16,384,128]{2,1,0:T(8,128)}, f32[16,8,128]{2,1,0:T(8,128)}, f32[128,1024]{1,0:T(8,128)}) custom-call(s32[1]{0:T(128)} %bitcast.13.first_ref, bf16[128,1024]{1,0:T(8,128)(2,1)} %q_ref.3, bf16[2,128,1024]{2,1,0:T(8,128)(2,1)} %collective-permute-done.6.both2_ref, bf16[2,128,1024]{2,1,0:T(8,128)(2,1)} %collective-permute-done.7.both1_ref, ...), custom_call_target="tpu_custom_call" | custom-call | tf_op jit(solution)/shard_map/attention_probs/pallas_call | solution.py:315
  176.5 8.5 %fusion.1 = f32[1024,1024]{1,0:T(8,128)} fusion(bf16[1536,1024]{1,0:T(8,128)(2,1)} %get-tuple-element.56, bf16[1536,1024]{1,0:T(8,128)(2,1)} %get-tuple-element.58), kind=kOutput, calls=%fused_computation.1 | convolution fusion | flops 3221225472 | bytes 10485760 | tf_op jit(solution)/shard_map/dot_general | solution.py:560
  185.0 5.0 %fusion = f32[1024,1024]{1,0:T(8,128)} fusion(bf16[1536,1024]{1,0:T(8,128)(2,1)S(1)} %copy-done, bf16[1536,1024]{1,0:T(8,128)(2,1)S(1)} %copy-done.5), kind=kOutput, calls=%fused_computation | convolution fusion | flops 3221225472 | bytes 10485760 | tf_op jit(solution)/shard_map/dot_general | solution.py:559
  190.0 5.0 %fusion.2 = f32[1024,1024]{1,0:T(8,128)} fusion(bf16[1536,1024]{1,0:T(8,128)(2,1)S(1)} %copy-done.1, bf16[1536,1024]{1,0:T(8,128)(2,1)S(1)} %copy-done.4), kind=kOutput, calls=%fused_computation.2 | convolution fusion | flops 3221225472 | bytes 10485760 | tf_op jit(solution)/shard_map/dot_general | solution.py:561
  195.0 4.8 %stream_gradient.1 = (bf16[128,1024]{1,0:T(8,128)(2,1)}, bf16[144,1024]{1,0:T(8,128)(2,1)}) custom-call(bf16[1024,1536]{1,0:T(8,128)(2,1)S(1)} %bitcast.23, bf16[144,1024]{1,0:T(8,128)(2,1)} %get-tuple-element.41.refs_2_.block_ref, bf16[128,1024]{1,0:T(8,128)(2,1)} %stream_ref.3, f32[1,1024]{1,0:T(1,128)} %bitcast.40, f32[128,1024]{1,0:T(8,128)} %get-tuple-element.63.attn_ref), custom_call_target="tpu_custom_call" | custom-call | tf_op jit(solution)/shard_map/stream_gradient/pallas_call | solution.py:409
  199.8 2.2 collective-permute-start.12
  202.0 5.2 %collective-permute-start.13 = (bf16[144,1024]{1,0:T(8,128)(2,1)}, bf16[144,1024]{1,0:T(8,128)(2,1)S(1)}, u32[]{:S(2)}, u32[]{:S(2)}) collective-permute-start(bf16[144,1024]{1,0:T(8,128)(2,1)} %get-tuple-element.64.o_ref.extra_ref), channel_id=1, source_target_pairs={{2,0},{3,1},{4,2},{5,3},{6,4},{7,5},{8,6},{9,7},{10,8},{11,9},{12,... | collective-permute-start | bytes 884744 | tf_op jit(solution)/shard_map/ppermute | solution.py:523
  207.2 2.7 %collective-permute-start.9 = (bf16[128,1024]{1,0:T(8,128)(2,1)}, bf16[128,1024]{1,0:T(8,128)(2,1)S(1)}, u32[]{:S(2)}, u32[]{:S(2)}) collective-permute-start(bf16[128,1024]{1,0:T(8,128)(2,1)} %q_ref.3), channel_id=1, source_target_pairs={{2,0},{3,1},{4,2},{5,3},{6,4},{7,5},{8,6},{9,7},{10,8},{11,9},{12,... | collective-permute-start | bytes 786440 | tf_op jit(solution)/shard_map/ppermute | solution.py:523
  209.9 2.2 collective-permute-start.10
  212.1 4.9 %collective-permute-start.11 = (f32[16,8,128]{2,1,0:T(8,128)S(1)}, f32[16,8,128]{2,1,0:T(8,128)S(1)}, u32[]{:S(2)}, u32[]{:S(2)}) collective-permute-start(f32[16,8,128]{2,1,0:T(8,128)S(1)} %copy-done.6), channel_id=1, source_target_pairs={{2,0},{3,1},{4,2},{5,3},{6,4},{7,5},{8,6},{9,7},{10,8},{11,9},{12,... | collective-permute-start | bytes 196616 | tf_op jit(solution)/shard_map/ppermute | solution.py:523
  217.0 10.4 %collective-permute-done.9.q2_ref = bf16[128,1024]{1,0:T(8,128)(2,1)S(1)} collective-permute-done((bf16[128,1024]{1,0:T(8,128)(2,1)}, bf16[128,1024]{1,0:T(8,128)(2,1)S(1)}, u32[]{:S(2)}, u32[]{:S(2)}) %collective-permute-start.9) | collective-permute-done | bytes 262176 | tf_op jit(solution)/shard_map/ppermute | solution.py:523
  228.8 4.1 %later_probs.1.p_ref = f32[16,2,128,128]{3,2,1,0:T(8,128)} custom-call(bf16[128,1024]{1,0:T(8,128)(2,1)} %copy-done.2, bf16[128,1024]{1,0:T(8,128)(2,1)} %copy-done.3, f32[16,8,128]{2,1,0:T(8,128)S(1)} %collective-permute-done.10.stats1_ref, f32[16,8,128]{2,1,0:T(8,128)S(1)} %collective-permute-done.11.stats2_ref, bf16[128,1024]{1,0:T(8,128)(2,1)} %k_ref.7), custom_call_target="tpu_custom_call" | custom-call | tf_op jit(solution)/shard_map/later_probs/pallas_call | solution.py:350
  232.9 5.9 %own_grads.1 = (bf16[128,1024]{1,0:T(8,128)(2,1)}, f32[128,1024]{1,0:T(8,128)}, f32[128,1024]{1,0:T(8,128)}) custom-call(f32[16,384,128]{2,1,0:T(8,128)} %get-tuple-element.61.p_ref, bf16[144,1024]{1,0:T(8,128)(2,1)} %get-tuple-element.64.o_ref.extra_ref, bf16[144,1024]{1,0:T(8,128)(2,1)} %get-tuple-element.64.o_ref.extra_ref, bf16[128,1024]{1,0:T(8,128)(2,1)} %q_ref.3, ...), custom_call_target="tpu_custom_call" | custom-call | tf_op jit(solution)/shard_map/own_grads/pallas_call | solution.py:464
  238.8 4.9 %later_grads.1 = (bf16[128,1024]{1,0:T(8,128)(2,1)}, bf16[128,1024]{1,0:T(8,128)(2,1)}) custom-call(f32[16,2,128,128]{3,2,1,0:T(8,128)} %later_probs.1.p_ref, bf16[144,1024]{1,0:T(8,128)(2,1)S(1)} %collective-permute-done.12.o1_ref, bf16[144,1024]{1,0:T(8,128)(2,1)S(1)} %collective-permute-done.13.o2_ref, bf16[128,1024]{1,0:T(8,128)(2,1)} %copy-done.2, ...), custom_call_target="tpu_custom_call" | custom-call | tf_op jit(solution)/shard_map/later_grads/pallas_call | solution.py:501
  (30 shorter events, 9.1 us)
Async XLA Ops:
  3.5 29.3 %all-to-all-start.1 = ((bf16[32,8,1536]{2,1,0:T(8,128)(2,1)}), bf16[32,8,1536]{2,1,0:T(8,128)(2,1)S(1)}, u32[]{:S(2)}, u32[]{:S(2)}) async-start(bf16[32,8,1536]{2,1,0:T(8,128)(2,1)} %bitcast.38), calls=%async_computation.1 | async-start | bytes 1572864 | tf_op jit(solution)/shard_map/all_to_all | solution.py:527
  12.1 8.5 %collective-permute-start = (bf16[144,1024]{1,0:T(8,128)(2,1)}, bf16[144,1024]{1,0:T(8,128)(2,1)S(1)}, u32[]{:S(2)}, u32[]{:S(2)}) collective-permute-start(bf16[144,1024]{1,0:T(8,128)(2,1)} %get-tuple-element.41.refs_2_.block_ref), channel_id=1, source_target_pairs={{0,1},{1,2},{2,3},{3,0},{4,5},{5,6},{6,7},{7,4},{8,9},{9,10},{10,1... | collective-permute-start | bytes 884744 | tf_op jit(solution)/shard_map/ppermute | solution.py:517
  12.4 9.6 %collective-permute-start.1 = (bf16[144,1024]{1,0:T(8,128)(2,1)}, bf16[144,1024]{1,0:T(8,128)(2,1)S(1)}, u32[]{:S(2)}, u32[]{:S(2)}) collective-permute-start(bf16[144,1024]{1,0:T(8,128)(2,1)} %get-tuple-element.41.refs_2_.block_ref), channel_id=1, source_target_pairs={{0,3},{1,0},{2,1},{3,2},{4,7},{5,4},{6,5},{7,6},{8,11},{9,8},{10,9... | collective-permute-start | bytes 884744 | tf_op jit(solution)/shard_map/ppermute | solution.py:517
  13.7 14.1 %collective-permute-start.2 = (bf16[144,1024]{1,0:T(8,128)(2,1)}, bf16[144,1024]{1,0:T(8,128)(2,1)S(1)}, u32[]{:S(2)}, u32[]{:S(2)}) collective-permute-start(bf16[144,1024]{1,0:T(8,128)(2,1)} %get-tuple-element.41.refs_2_.block_ref), channel_id=1, source_target_pairs={{0,2},{1,3},{2,0},{3,1},{4,6},{5,7},{6,4},{7,5},{8,10},{9,11},{10,... | collective-permute-start | bytes 884744 | tf_op jit(solution)/shard_map/ppermute | solution.py:517
  32.8 51.2 %all-to-all-start = ((bf16[32,32,1536]{2,1,0:T(8,128)(2,1)}), bf16[32,32,1536]{2,1,0:T(8,128)(2,1)}, u32[]{:S(2)}, u32[]{:S(2)}) async-start(bf16[32,32,1536]{2,1,0:T(8,128)(2,1)} %bitcast.35), calls=%async_computation | async-start | bytes 6291456 | tf_op jit(solution)/shard_map/all_to_all | solution.py:527
  41.6 18.9 %collective-permute-start.3 = (bf16[256,1536]{1,0:T(8,128)(2,1)S(1)}, bf16[256,1536]{1,0:T(8,128)(2,1)S(1)}, u32[]{:S(2)}, u32[]{:S(2)}) collective-permute-start(bf16[256,1536]{1,0:T(8,128)(2,1)S(1)} %bitcast.24), channel_id=1, source_target_pairs={{0,1},{1,2},{2,3},{3,0},{4,5},{5,6},{6,7},{7,4},{8,9},{9,10},{10,1... | collective-permute-start | bytes 2359304 | tf_op jit(solution)/shard_map/ppermute | solution.py:517
  42.7 25.5 %collective-permute-start.5 = (bf16[256,1536]{1,0:T(8,128)(2,1)S(1)}, bf16[256,1536]{1,0:T(8,128)(2,1)S(1)}, u32[]{:S(2)}, u32[]{:S(2)}) collective-permute-start(bf16[256,1536]{1,0:T(8,128)(2,1)S(1)} %bitcast.25), channel_id=1, source_target_pairs={{0,3},{1,0},{2,1},{3,2},{4,7},{5,4},{6,5},{7,6},{8,11},{9,8},{10,9... | collective-permute-start | bytes 2359304 | tf_op jit(solution)/shard_map/ppermute | solution.py:517
  60.5 18.1 %collective-permute-start.4 = (bf16[256,1536]{1,0:T(8,128)(2,1)S(1)}, bf16[256,1536]{1,0:T(8,128)(2,1)S(1)}, u32[]{:S(2)}, u32[]{:S(2)}) collective-permute-start(bf16[256,1536]{1,0:T(8,128)(2,1)S(1)} %collective-permute-done.3.refs_0_), channel_id=1, source_target_pairs={{0,1},{1,2},{2,3},{3,0},{4,5},{5,6},{6,7},{7,4},{8,9},{9,10},{10,1... | collective-permute-start | bytes 2359304 | tf_op jit(solution)/shard_map/ppermute | solution.py:517
  102.1 92.9 %all-to-all-start.2 = ((bf16[128,8,1536]{2,1,0:T(8,128)(2,1)}), bf16[128,8,1536]{2,1,0:T(8,128)(2,1)S(1)}, u32[]{:S(2)}, u32[]{:S(2)}) async-start(bf16[128,8,1536]{2,1,0:T(8,128)(2,1)} %bitcast.36), calls=%async_computation.2 | async-start | bytes 6291456 | tf_op jit(solution)/shard_map/all_to_all | solution.py:527
  113.7 46.2 %collective-permute-start.6 = (bf16[2,128,1024]{2,1,0:T(8,128)(2,1)}, bf16[2,128,1024]{2,1,0:T(8,128)(2,1)}, u32[]{:S(2)}, u32[]{:S(2)}) collective-permute-start(bf16[2,128,1024]{2,1,0:T(8,128)(2,1)} %get-tuple-element.54), channel_id=1, source_target_pairs={{0,2},{1,3},{2,4},{3,5},{4,6},{5,7},{6,8},{7,9},{8,10},{9,11},{10,... | collective-permute-start | bytes 1572872 | tf_op jit(solution)/shard_map/ppermute | solution.py:523
  118.0 52.5 %collective-permute-start.7 = (bf16[2,128,1024]{2,1,0:T(8,128)(2,1)}, bf16[2,128,1024]{2,1,0:T(8,128)(2,1)}, u32[]{:S(2)}, u32[]{:S(2)}) collective-permute-start(bf16[2,128,1024]{2,1,0:T(8,128)(2,1)} %get-tuple-element.54), channel_id=1, source_target_pairs={{0,1},{1,2},{2,3},{3,4},{4,5},{5,6},{6,7},{7,8},{8,9},{9,10},{10,1... | collective-permute-start | bytes 1572872 | tf_op jit(solution)/shard_map/ppermute | solution.py:523
  122.0 90.1 %collective-permute-start.8 = (bf16[128,1024]{1,0:T(8,128)(2,1)}, bf16[128,1024]{1,0:T(8,128)(2,1)S(1)}, u32[]{:S(2)}, u32[]{:S(2)}) collective-permute-start(bf16[128,1024]{1,0:T(8,128)(2,1)} %q_ref.3), channel_id=1, source_target_pairs={{1,0},{2,1},{3,2},{4,3},{5,4},{6,5},{7,6},{8,7},{9,8},{10,9},{11,1... | collective-permute-start | bytes 786440 | tf_op jit(solution)/shard_map/ppermute | solution.py:523
  176.5 8.5 %copy-start = (bf16[1536,1024]{1,0:T(8,128)(2,1)S(1)}, bf16[1536,1024]{1,0:T(8,128)(2,1)}, u32[]{:S(2)}) copy-start(bf16[1536,1024]{1,0:T(8,128)(2,1)} %get-tuple-element.56) | copy-start | bytes 9437188
  176.5 8.5 %copy-start.5 = (bf16[1536,1024]{1,0:T(8,128)(2,1)S(1)}, bf16[1536,1024]{1,0:T(8,128)(2,1)}, u32[]{:S(2)}) copy-start(bf16[1536,1024]{1,0:T(8,128)(2,1)} %get-tuple-element.57) | copy-start | bytes 9437188
  185.0 5.0 %copy-start.1 = (bf16[1536,1024]{1,0:T(8,128)(2,1)S(1)}, bf16[1536,1024]{1,0:T(8,128)(2,1)}, u32[]{:S(2)}) copy-start(bf16[1536,1024]{1,0:T(8,128)(2,1)} %get-tuple-element.59) | copy-start | bytes 9437188
  185.0 5.0 %copy-start.4 = (bf16[1536,1024]{1,0:T(8,128)(2,1)S(1)}, bf16[1536,1024]{1,0:T(8,128)(2,1)}, u32[]{:S(2)}) copy-start(bf16[1536,1024]{1,0:T(8,128)(2,1)} %get-tuple-element.60) | copy-start | bytes 9437188
  195.0 14.9 %copy-start.6 = (f32[16,8,128]{2,1,0:T(8,128)S(1)}, f32[16,8,128]{2,1,0:T(8,128)}, u32[]{:S(2)}) copy-start(f32[16,8,128]{2,1,0:T(8,128)} %get-tuple-element.66) | copy-start | bytes 196612
  199.8 39.0 %collective-permute-start.12 = (bf16[144,1024]{1,0:T(8,128)(2,1)}, bf16[144,1024]{1,0:T(8,128)(2,1)S(1)}, u32[]{:S(2)}, u32[]{:S(2)}) collective-permute-start(bf16[144,1024]{1,0:T(8,128)(2,1)} %get-tuple-element.64.o_ref.extra_ref), channel_id=1, source_target_pairs={{1,0},{2,1},{3,2},{4,3},{5,4},{6,5},{7,6},{8,7},{9,8},{10,9},{11,1... | collective-permute-start | bytes 884744 | tf_op jit(solution)/shard_map/ppermute | solution.py:523
  202.0 36.8 %collective-permute-start.13 = (bf16[144,1024]{1,0:T(8,128)(2,1)}, bf16[144,1024]{1,0:T(8,128)(2,1)S(1)}, u32[]{:S(2)}, u32[]{:S(2)}) collective-permute-start(bf16[144,1024]{1,0:T(8,128)(2,1)} %get-tuple-element.64.o_ref.extra_ref), channel_id=1, source_target_pairs={{2,0},{3,1},{4,2},{5,3},{6,4},{7,5},{8,6},{9,7},{10,8},{11,9},{12,... | collective-permute-start | bytes 884744 | tf_op jit(solution)/shard_map/ppermute | solution.py:523
  207.2 20.2 %collective-permute-start.9 = (bf16[128,1024]{1,0:T(8,128)(2,1)}, bf16[128,1024]{1,0:T(8,128)(2,1)S(1)}, u32[]{:S(2)}, u32[]{:S(2)}) collective-permute-start(bf16[128,1024]{1,0:T(8,128)(2,1)} %q_ref.3), channel_id=1, source_target_pairs={{2,0},{3,1},{4,2},{5,3},{6,4},{7,5},{8,6},{9,7},{10,8},{11,9},{12,... | collective-permute-start | bytes 786440 | tf_op jit(solution)/shard_map/ppermute | solution.py:523
  209.9 18.1 %collective-permute-start.10 = (f32[16,8,128]{2,1,0:T(8,128)S(1)}, f32[16,8,128]{2,1,0:T(8,128)S(1)}, u32[]{:S(2)}, u32[]{:S(2)}) collective-permute-start(f32[16,8,128]{2,1,0:T(8,128)S(1)} %copy-done.6), channel_id=1, source_target_pairs={{1,0},{2,1},{3,2},{4,3},{5,4},{6,5},{7,6},{8,7},{9,8},{10,9},{11,1... | collective-permute-start | bytes 196616 | tf_op jit(solution)/shard_map/ppermute | solution.py:523
  212.1 16.7 %copy-start.2 = (bf16[128,1024]{1,0:T(8,128)(2,1)}, bf16[128,1024]{1,0:T(8,128)(2,1)S(1)}, u32[]{:S(2)}) copy-start(bf16[128,1024]{1,0:T(8,128)(2,1)S(1)} %collective-permute-done.8.q1_ref) | copy-start | bytes 786436
  212.1 16.7 %collective-permute-start.11 = (f32[16,8,128]{2,1,0:T(8,128)S(1)}, f32[16,8,128]{2,1,0:T(8,128)S(1)}, u32[]{:S(2)}, u32[]{:S(2)}) collective-permute-start(f32[16,8,128]{2,1,0:T(8,128)S(1)} %copy-done.6), channel_id=1, source_target_pairs={{2,0},{3,1},{4,2},{5,3},{6,4},{7,5},{8,6},{9,7},{10,8},{11,9},{12,... | collective-permute-start | bytes 196616 | tf_op jit(solution)/shard_map/ppermute | solution.py:523
  227.4 1.4 copy-start.3
